TPU v7x, 32 devices: a whole 2x2x4 slice. The times are simulated.
32 devices in a mesh: fsdp: 4 (over y, core), tensor: 8 (over z, x).
Axes of the slice: x: 2, y: 2, z: 4, core: 2. Of those that a mesh axis runs over, the one named last changes fastest.
Arguments:
- layer_input: bfloat16 [8, 1024, 1024], P('fsdp', 'tensor'), may hold values from -7 to 7
- cotangent: bfloat16 [8, 1024, 1024], P('fsdp', 'tensor'), may hold values from -6 to 6
- attn_weight: float32 [1024, 3072], P('fsdp', 'tensor'), may hold values from -0.1875 to 0.1875
- attn_bias: float32 [16, 192], P('tensor', 'fsdp'), may hold values from -3 to 3
- out_weight: float32 [1024, 1024], P('tensor', 'fsdp'), may hold values from -3 to 3
- up_weight: float32 [1024, 4096], P('fsdp', 'tensor'), may hold values from -0.1875 to 0.1875
- up_bias: float32 [4096], P(('tensor', 'fsdp')), may hold values from -3 to 3
- down_weight: float32 [4096, 1024], P('tensor', 'fsdp'), may hold values from -0.09375 to 0.09375
- norm_gains: float32 [2, 1024], P(None, 'fsdp'), may hold values from 0.25 to 1.75
- norm_shifts: float32 [4, 1024], P(None, 'fsdp'), may hold values from -2 to 2
- attn_weight_moments: float32 [2, 1024, 3072], P(None, 'fsdp', 'tensor'), may hold values from -18.101934 to 18.101934, as said below
- attn_bias_moments: float32 [2, 16, 192], P(None, 'tensor', 'fsdp'), may hold values from -18.101934 to 18.101934, as said below
- out_weight_moments: float32 [2, 1024, 1024], P(None, 'tensor', 'fsdp'), may hold values from -18.101934 to 18.101934, as said below
- up_weight_moments: float32 [2, 1024, 4096], P(None, 'fsdp', 'tensor'), may hold values from -18.101934 to 18.101934, as said below
- up_bias_moments: float32 [2, 4096], P(None, ('tensor', 'fsdp')), may hold values from -18.101934 to 18.101934, as said below
- down_weight_moments: float32 [2, 4096, 1024], P(None, 'tensor', 'fsdp'), may hold values from -18.101934 to 18.101934, as said below
- norm_gains_moments: float32 [2, 2, 1024], P(None, None, 'fsdp'), may hold values from -18.101934 to 18.101934, as said below
- norm_shifts_moments: float32 [2, 4, 1024], P(None, None, 'fsdp'), may hold values from -18.101934 to 18.101934, as said below
Outputs:
- layer_output: bfloat16 [8, 1024, 1024], P('fsdp', 'tensor')
- input_grad: float32 [8, 1024, 1024], P('fsdp', 'tensor')
- grad_attn_weight: float32 [1024, 3072], P('fsdp', 'tensor')
- grad_attn_bias: float32 [16, 192], P('tensor', 'fsdp')
- grad_out_weight: float32 [1024, 1024], P('tensor', 'fsdp')
- grad_up_weight: float32 [1024, 4096], P('fsdp', 'tensor')
- grad_up_bias: float32 [4096], P(('tensor', 'fsdp'))
- grad_down_weight: float32 [4096, 1024], P('tensor', 'fsdp')
- grad_norm_gains: float32 [2, 1024], P(None, 'fsdp')
- grad_norm_shifts: float32 [4, 1024], P(None, 'fsdp')
- new_attn_weight: float32 [1024, 3072], P('fsdp', 'tensor')
- new_attn_bias: float32 [16, 192], P('tensor', 'fsdp')
- new_out_weight: float32 [1024, 1024], P('tensor', 'fsdp')
- new_up_weight: float32 [1024, 4096], P('fsdp', 'tensor')
- new_up_bias: float32 [4096], P(('tensor', 'fsdp'))
- new_down_weight: float32 [4096, 1024], P('tensor', 'fsdp')
- new_norm_gains: float32 [2, 1024], P(None, 'fsdp')
- new_norm_shifts: float32 [4, 1024], P(None, 'fsdp')
- new_attn_weight_moments: float32 [2, 1024, 3072], P(None, 'fsdp', 'tensor')
- new_attn_bias_moments: float32 [2, 16, 192], P(None, 'tensor', 'fsdp')
- new_out_weight_moments: float32 [2, 1024, 1024], P(None, 'tensor', 'fsdp')
- new_up_weight_moments: float32 [2, 1024, 4096], P(None, 'fsdp', 'tensor')
- new_up_bias_moments: float32 [2, 4096], P(None, ('tensor', 'fsdp'))
- new_down_weight_moments: float32 [2, 4096, 1024], P(None, 'tensor', 'fsdp')
- new_norm_gains_moments: float32 [2, 2, 1024], P(None, None, 'fsdp')
- new_norm_shifts_moments: float32 [2, 4, 1024], P(None, None, 'fsdp')
Inputs may be any that keep to these rules, and one draw needn't show every extreme that they name: `attn_weight_moments`: index 0 of the first dimension holds first moments, index 1 positive second moments. `attn_bias_moments`: index 0 of the first dimension holds first moments, index 1 positive second moments. `out_weight_moments`: index 0 of the first dimension holds first moments, index 1 positive second moments. `up_weight_moments`: index 0 of the first dimension holds first moments, index 1 positive second moments. `up_bias_moments`: index 0 of the first dimension holds first moments, index 1 positive second moments. `down_weight_moments`: index 0 of the first dimension holds first moments, index 1 positive second moments. `norm_gains_moments`: index 0 of the first dimension holds first moments, index 1 positive second moments. `norm_shifts_moments`: index 0 of the first dimension holds first moments, index 1 positive second moments.
All inputs are finite; a program needn't handle non-finite values.
Results may differ from a plain program's by a relative error of at most 0.012.
The roundings to bfloat16 on the way count: a program that leaves them out, or rounds other values in their place, can miss the bound.
Values may be sent and summed in bfloat16 or wider, within the bound.
No kernel may reach another device: no remote copies, remote signals or barrier semaphores. Data moves between devices by JAX's collectives and lax.ppermute only.
A program may use at most 128 MiB of HBM per device.

v0:
```python
import jax
import jax.numpy as jnp
from jax import lax
from jax.sharding import PartitionSpec as P

norm_eps = 1e-05
beta_one = 0.9
beta_two = 0.999
adam_eps = 1e-08
adam_step = 4.0
matrix_rate = 0.01
output_rate = 0.1
vector_rate = 0.1
decay_rate = 0.1
inv_root_two = 0.7071067811865476
inv_root_tau = 0.3989422804014327


def layer_norm(resid, gain_row, shift_row):
    center = resid - jnp.mean(resid, axis=-1, keepdims=True)
    spread = lax.rsqrt(jnp.mean(center * center, axis=-1, keepdims=True) + norm_eps)
    normed = center * spread
    return (normed * gain_row + shift_row, normed, spread)


def norm_back(grad_out, gain_row, normed, spread):
    scaled = grad_out * gain_row
    return spread * (
        scaled
        - jnp.mean(scaled, axis=-1, keepdims=True)
        - normed * jnp.mean(scaled * normed, axis=-1, keepdims=True)
    )


def gelu_value(inner):
    return inner * 0.5 * (1.0 + jax.scipy.special.erf(inner * inv_root_two))


def gelu_slope(inner):
    return (
        0.5 * (1.0 + jax.scipy.special.erf(inner * inv_root_two))
        + inner * jnp.exp(-0.5 * inner * inner) * inv_root_tau
    )


def split_heads(qkv, heads, head_width):
    seq_length = qkv.shape[0]
    triple = jnp.transpose(qkv.reshape(seq_length, heads, 3, head_width), (2, 1, 0, 3))
    return (triple[0], triple[1], triple[2])


def merge_heads(mixed):
    heads, seq_length, head_width = mixed.shape
    return jnp.transpose(mixed, (1, 0, 2)).reshape(seq_length, heads * head_width)


def attention_forward(queries, key_rows, values):
    heads, seq_length, head_width = queries.shape
    block_rows = min(512, seq_length)
    block_count = seq_length // block_rows
    score_scale = head_width ** (-0.5)

    def one_block(block_index):
        row_block = lax.dynamic_slice_in_dim(queries, block_index * block_rows, block_rows, 1)
        scores = (
            jnp.einsum("hqd,hkd->hqk", row_block, key_rows, preferred_element_type=jnp.float32)
            * score_scale
        )
        row_max = jnp.max(scores, axis=-1, keepdims=True)
        logsum = row_max + jnp.log(jnp.sum(jnp.exp(scores - row_max), axis=-1, keepdims=True))
        softmax_weights = jnp.exp(scores - logsum).astype(jnp.bfloat16)
        mixed = jnp.einsum(
            "hqk,hkd->hqd", softmax_weights, values, preferred_element_type=jnp.float32
        )
        return (mixed.astype(jnp.bfloat16), logsum[..., 0])

    mixed, logsum = lax.map(one_block, jnp.arange(block_count, dtype=jnp.int32))
    mixed = jnp.transpose(mixed, (1, 0, 2, 3)).reshape(heads, seq_length, head_width)
    logsum = jnp.transpose(logsum, (1, 0, 2)).reshape(heads, seq_length)
    return (mixed, logsum)


def attention_back(queries, key_rows, values, logsum, grad_mixed):
    heads, seq_length, head_width = queries.shape
    block_rows = min(512, seq_length)
    block_count = seq_length // block_rows
    score_scale = head_width ** (-0.5)

    def block_step(carry, block_index):
        grad_keys, grad_values = carry
        first_row = block_index * block_rows
        row_block = lax.dynamic_slice_in_dim(queries, first_row, block_rows, 1)
        log_block = lax.dynamic_slice_in_dim(logsum, first_row, block_rows, 1)
        grad_block = lax.dynamic_slice_in_dim(grad_mixed, first_row, block_rows, 1)
        scores = (
            jnp.einsum("hqd,hkd->hqk", row_block, key_rows, preferred_element_type=jnp.float32)
            * score_scale
        )
        chances = jnp.exp(scores - log_block[..., None])
        chances_b = chances.astype(jnp.bfloat16)
        grad_values = grad_values + jnp.einsum(
            "hqk,hqd->hkd", chances_b, grad_block, preferred_element_type=jnp.float32
        )
        grad_scores = jnp.einsum(
            "hqd,hkd->hqk", grad_block, values, preferred_element_type=jnp.float32
        )
        grad_logits = chances * (
            grad_scores - jnp.sum(chances * grad_scores, axis=-1, keepdims=True)
        )
        logits_b = grad_logits.astype(jnp.bfloat16)
        grad_query = (
            jnp.einsum("hqk,hkd->hqd", logits_b, key_rows, preferred_element_type=jnp.float32)
            * score_scale
        )
        grad_keys = (
            grad_keys
            + jnp.einsum("hqk,hqd->hkd", logits_b, row_block, preferred_element_type=jnp.float32)
            * score_scale
        )
        return ((grad_keys, grad_values), grad_query)

    zeros = jnp.zeros((heads, seq_length, head_width), jnp.float32)
    (grad_keys, grad_values), grad_queries = lax.scan(
        block_step, (zeros, zeros), jnp.arange(block_count, dtype=jnp.int32)
    )
    grad_queries = jnp.transpose(grad_queries, (1, 0, 2, 3)).reshape(heads, seq_length, head_width)
    return (grad_queries, grad_keys, grad_values)


def adamw_update(weight, moments, grad, rate, decay):
    first_moment = beta_one * moments[0] + (1.0 - beta_one) * grad
    second_moment = beta_two * moments[1] + (1.0 - beta_two) * grad * grad
    direction = (
        first_moment
        / (1.0 - beta_one**adam_step)
        / (jnp.sqrt(second_moment / (1.0 - beta_two**adam_step)) + adam_eps)
    )
    return (weight - rate * (direction + decay * weight), jnp.stack([first_moment, second_moment]))


def fetch_params(pieces):
    return (
        lax.all_gather(pieces[0], "fsdp", axis=0, tiled=True),
        lax.all_gather(pieces[1], "fsdp", axis=1, tiled=True),
        lax.all_gather(pieces[2], "fsdp", axis=1, tiled=True),
        lax.all_gather(pieces[3], "fsdp", axis=0, tiled=True),
        lax.all_gather(pieces[4], "fsdp", axis=0, tiled=True),
        lax.all_gather(pieces[5], "fsdp", axis=1, tiled=True),
        lax.all_gather(pieces[6], "fsdp", axis=1, tiled=True),
        lax.all_gather(pieces[7], "fsdp", axis=1, tiled=True),
    )


def refetch_params(pieces):
    return (
        lax.all_gather(pieces[0], "fsdp", axis=0, tiled=True),
        lax.all_gather(pieces[1], "fsdp", axis=1, tiled=True),
        lax.all_gather(pieces[2], "fsdp", axis=1, tiled=True),
        lax.all_gather(pieces[3], "fsdp", axis=0, tiled=True),
        lax.all_gather(pieces[4], "fsdp", axis=0, tiled=True),
        lax.all_gather(pieces[5], "fsdp", axis=1, tiled=True),
        lax.all_gather(pieces[6], "fsdp", axis=1, tiled=True),
        lax.all_gather(pieces[7], "fsdp", axis=1, tiled=True),
    )


def per_device(
    layer_input,
    cotangent,
    attn_weight,
    attn_bias,
    out_weight,
    up_weight,
    up_bias,
    down_weight,
    norm_gains,
    norm_shifts,
    attn_weight_moments,
    attn_bias_moments,
    out_weight_moments,
    up_weight_moments,
    up_bias_moments,
    down_weight_moments,
    norm_gains_moments,
    norm_shifts_moments,
):
    fsdp_count = lax.axis_size("fsdp")
    local_heads = attn_bias.shape[0]
    head_width = attn_bias.shape[1] * fsdp_count // 3
    model_width = norm_gains.shape[1] * fsdp_count
    weights = (
        attn_weight,
        attn_bias,
        out_weight,
        up_weight,
        up_bias,
        down_weight,
        norm_gains,
        norm_shifts,
    )
    pieces = tuple((weight.astype(jnp.bfloat16) for weight in weights))
    zero_grads = (
        jnp.zeros((model_width, attn_weight.shape[1]), jnp.float32),
        jnp.zeros((local_heads, 3 * head_width), jnp.float32),
        jnp.zeros((out_weight.shape[0], model_width), jnp.float32),
        jnp.zeros((model_width, up_weight.shape[1]), jnp.float32),
        jnp.zeros((up_bias.shape[0] * fsdp_count,), jnp.float32),
        jnp.zeros((down_weight.shape[0], model_width), jnp.float32),
        jnp.zeros((2, model_width), jnp.float32),
        jnp.zeros((4, model_width), jnp.float32),
    )

    def micro_step(totals, inputs):
        tokens, upstream = inputs
        w_attn, b_attn, w_output, w_upward, b_upward, w_downward, gains_b, shifts_b = fetch_params(
            pieces
        )
        gain_rows = gains_b.astype(jnp.float32)
        shift_rows = shifts_b.astype(jnp.float32)
        gathered = lax.all_gather(tokens, "tensor", axis=0, tiled=True)
        qkv = (
            jnp.dot(gathered, w_attn, preferred_element_type=jnp.float32)
            + b_attn.reshape(-1).astype(jnp.float32)
        ).astype(jnp.bfloat16)
        queries, key_rows, values = split_heads(qkv, local_heads, head_width)
        mixed, logsum = attention_forward(queries, key_rows, values)
        attn = merge_heads(mixed)
        attn_out = lax.psum_scatter(
            jnp.dot(attn, w_output, preferred_element_type=jnp.float32),
            "tensor",
            scatter_dimension=0,
            tiled=True,
        )
        resid_one = attn_out + shift_rows[0] + tokens.astype(jnp.float32)
        hidden_one, normed_one, spread_one = layer_norm(resid_one, gain_rows[0], shift_rows[1])
        hidden_one_b = hidden_one.astype(jnp.bfloat16)
        expanded = lax.all_gather(hidden_one_b, "tensor", axis=0, tiled=True)
        inner = jnp.dot(expanded, w_upward, preferred_element_type=jnp.float32) + b_upward.astype(
            jnp.float32
        )
        active = gelu_value(inner).astype(jnp.bfloat16)
        ffn_out = lax.psum_scatter(
            jnp.dot(active, w_downward, preferred_element_type=jnp.float32),
            "tensor",
            scatter_dimension=0,
            tiled=True,
        )
        resid_two = ffn_out + shift_rows[2] + hidden_one
        result, normed_two, spread_two = layer_norm(resid_two, gain_rows[1], shift_rows[3])
        output = result.astype(jnp.bfloat16)
        w_attn, b_attn, w_output, w_upward, b_upward, w_downward, gains_b, shifts_b = (
            refetch_params(pieces)
        )
        gain_rows = gains_b.astype(jnp.float32)
        upward = upstream.astype(jnp.float32)
        grad_two = norm_back(upward, gain_rows[1], normed_two, spread_two)
        grad_two_b = grad_two.astype(jnp.bfloat16)
        grad_full = lax.all_gather(grad_two_b, "tensor", axis=0, tiled=True)
        grad_down = jnp.dot(active.T, grad_full, preferred_element_type=jnp.float32)
        grad_inner = jnp.dot(
            grad_full, w_downward.T, preferred_element_type=jnp.float32
        ) * gelu_slope(inner)
        grad_inner_b = grad_inner.astype(jnp.bfloat16)
        grad_upward = jnp.dot(expanded.T, grad_inner_b, preferred_element_type=jnp.float32)
        grad_hidden = grad_two + lax.psum_scatter(
            jnp.dot(grad_inner_b, w_upward.T, preferred_element_type=jnp.float32),
            "tensor",
            scatter_dimension=0,
            tiled=True,
        )
        grad_one = norm_back(grad_hidden, gain_rows[0], normed_one, spread_one)
        grad_one_b = grad_one.astype(jnp.bfloat16)
        one_full = lax.all_gather(grad_one_b, "tensor", axis=0, tiled=True)
        grad_output = jnp.dot(attn.T, one_full, preferred_element_type=jnp.float32)
        grad_attn = jnp.dot(one_full, w_output.T, preferred_element_type=jnp.float32).astype(
            jnp.bfloat16
        )
        seq_length = one_full.shape[0]
        grad_mixed = jnp.transpose(
            grad_attn.reshape(seq_length, local_heads, head_width), (1, 0, 2)
        )
        grad_queries, grad_keys, grad_values = attention_back(
            queries, key_rows, values, logsum, grad_mixed
        )
        grad_qkv = jnp.transpose(
            jnp.stack([grad_queries, grad_keys, grad_values]), (2, 1, 0, 3)
        ).reshape(seq_length, -1)
        grad_qkv_b = grad_qkv.astype(jnp.bfloat16)
        grad_attn_w = jnp.dot(gathered.T, grad_qkv_b, preferred_element_type=jnp.float32)
        input_grad = grad_one + lax.psum_scatter(
            jnp.dot(grad_qkv_b, w_attn.T, preferred_element_type=jnp.float32),
            "tensor",
            scatter_dimension=0,
            tiled=True,
        )
        grad_gain = jnp.stack(
            [jnp.sum(grad_hidden * normed_one, axis=0), jnp.sum(upward * normed_two, axis=0)]
        )
        grad_shift = jnp.stack(
            [
                jnp.sum(grad_one, axis=0),
                jnp.sum(grad_hidden, axis=0),
                jnp.sum(grad_two, axis=0),
                jnp.sum(upward, axis=0),
            ]
        )
        terms = (
            grad_attn_w,
            jnp.sum(grad_qkv, axis=0).reshape(local_heads, 3 * head_width),
            grad_output,
            grad_upward,
            jnp.sum(grad_inner, axis=0),
            grad_down,
            grad_gain,
            grad_shift,
        )
        return (tuple((total + term for total, term in zip(totals, terms))), (output, input_grad))

    totals, (outputs, input_grads) = lax.scan(micro_step, zero_grads, (layer_input, cotangent))
    shards = (
        lax.psum_scatter(totals[0], "fsdp", scatter_dimension=0, tiled=True),
        lax.psum_scatter(totals[1], "fsdp", scatter_dimension=1, tiled=True),
        lax.psum_scatter(totals[2], "fsdp", scatter_dimension=1, tiled=True),
        lax.psum_scatter(totals[3], "fsdp", scatter_dimension=0, tiled=True),
        lax.psum_scatter(totals[4], "fsdp", scatter_dimension=0, tiled=True),
        lax.psum_scatter(totals[5], "fsdp", scatter_dimension=1, tiled=True),
        lax.psum_scatter(totals[6], "fsdp", scatter_dimension=1, tiled=True),
        lax.psum_scatter(totals[7], "fsdp", scatter_dimension=1, tiled=True),
    )
    gain_grad, shift_grad = lax.psum((shards[6], shards[7]), "tensor")
    grads = (
        shards[0],
        shards[1],
        shards[2],
        shards[3],
        shards[4],
        shards[5],
        gain_grad,
        shift_grad,
    )
    moments = (
        attn_weight_moments,
        attn_bias_moments,
        out_weight_moments,
        up_weight_moments,
        up_bias_moments,
        down_weight_moments,
        norm_gains_moments,
        norm_shifts_moments,
    )
    rates = (
        matrix_rate,
        vector_rate,
        output_rate,
        matrix_rate,
        vector_rate,
        matrix_rate,
        vector_rate,
        vector_rate,
    )
    decays = (decay_rate, 0.0, decay_rate, decay_rate, 0.0, decay_rate, 0.0, 0.0)
    updated = [
        adamw_update(weights[place], moments[place], grads[place], rates[place], decays[place])
        for place in range(8)
    ]
    new_weights = tuple((pair[0] for pair in updated))
    new_moments = tuple((pair[1] for pair in updated))
    return (outputs, input_grads) + grads + new_weights + new_moments


def solution(mesh):
    return jax.shard_map(
        per_device,
        mesh=mesh,
        in_specs=(
            P("fsdp", "tensor", None),
            P("fsdp", "tensor", None),
            P("fsdp", "tensor"),
            P("tensor", "fsdp"),
            P("tensor", "fsdp"),
            P("fsdp", "tensor"),
            P(("tensor", "fsdp")),
            P("tensor", "fsdp"),
            P(None, "fsdp"),
            P(None, "fsdp"),
            P(None, "fsdp", "tensor"),
            P(None, "tensor", "fsdp"),
            P(None, "tensor", "fsdp"),
            P(None, "fsdp", "tensor"),
            P(None, ("tensor", "fsdp")),
            P(None, "tensor", "fsdp"),
            P(None, None, "fsdp"),
            P(None, None, "fsdp"),
        ),
        out_specs=(
            P("fsdp", "tensor", None),
            P("fsdp", "tensor", None),
            P("fsdp", "tensor"),
            P("tensor", "fsdp"),
            P("tensor", "fsdp"),
            P("fsdp", "tensor"),
            P(("tensor", "fsdp")),
            P("tensor", "fsdp"),
            P(None, "fsdp"),
            P(None, "fsdp"),
            P("fsdp", "tensor"),
            P("tensor", "fsdp"),
            P("tensor", "fsdp"),
            P("fsdp", "tensor"),
            P(("tensor", "fsdp")),
            P("tensor", "fsdp"),
            P(None, "fsdp"),
            P(None, "fsdp"),
            P(None, "fsdp", "tensor"),
            P(None, "tensor", "fsdp"),
            P(None, "tensor", "fsdp"),
            P(None, "fsdp", "tensor"),
            P(None, ("tensor", "fsdp")),
            P(None, "tensor", "fsdp"),
            P(None, None, "fsdp"),
            P(None, None, "fsdp"),
        ),
        check_vma=False,
    )
```

profile of v0, /device:TPU:13, one launch (start us, length us, event | category | flops | bytes accessed | tf_op | source)
XLA Modules:
  0.0 1479.4 jit_solution(5837257049917221244)
XLA Ops:
  15.7 1255.9 %while.60 = (s32[]{:T(128)}, f32[1024,384]{1,0:T(8,128)}, f32[2,192]{1,0:T(2,128)S(1)}, f32[128,1024]{1,0:T(8,128)}, f32[1024,512]{1,0:T(8,128)}, /*index=5*/f32...) while((s32[]{:T(128)}, f32[1024,384]{1,0:T(8,128)}, ...), condition=%wide.region_28.29_spmd.clone, body=%wide.region_0.28_spmd.clone.sunk | while | flops 10649358336 | bytes 308377216 | solution.py:319
  17.7 5.5 all-gather.10
  23.3 5.9 all_gather.60
  29.2 8.7 all_gather.59
  37.9 30.9 %all-gather.19.cloned.1.call-done = bf16[1,1024,1024]{2,1,0:T(8,128)(2,1)} async-done(((bf16[1,128,1024]{2,1,0:T(8,128)(2,1)}), bf16[1,1024,1024]{2,1,0:T(8,128)(2,1)}) %all-gather.19.cloned.1.call-update) | async-done | bytes 2097168 | tf_op jit(solution)/shard_map/while/body/eval_jaxpr/all_gather | solution.py:220
  68.8 2.6 add_convert_fusion.3
  71.6 8.0 while.61
  79.6 2.7 fusion.204
  83.0 6.4 all_gather.62
  89.4 5.1 all_gather.61
  94.6 75.4 %reduce-scatter.32.cloned.1.call-done = f32[128,1024]{1,0:T(8,128)} async-done(((f32[1024,1024]{1,0:T(8,128)}), f32[128,1024]{1,0:T(8,128)}) %reduce-scatter.32.cloned.1.call-update) | async-done | bytes 524304 | tf_op jit(solution)/shard_map/while/body/eval_jaxpr/reduce_scatter | solution.py:228
  173.0 5.7 all-gather.11
  178.7 41.9 %all-gather.21.cloned.1.call-done = bf16[1024,1024]{1,0:T(8,128)(2,1)} async-done(((bf16[128,1024]{1,0:T(8,128)(2,1)}), bf16[1024,1024]{1,0:T(8,128)(2,1)}) %all-gather.21.cloned.1.call-update) | async-done | bytes 2097168 | tf_op jit(solution)/shard_map/while/body/eval_jaxpr/all_gather | solution.py:237
  220.6 4.6 multiply_convert_fusion.4
  225.2 13.1 all-gather.25.cloned.1.call-done
  238.3 4.4 fusion.209
  242.8 88.3 %reduce-scatter.34.cloned.1.call-done = f32[128,1024]{1,0:T(8,128)} async-done(((f32[1024,1024]{1,0:T(8,128)}), f32[128,1024]{1,0:T(8,128)}) %reduce-scatter.34.cloned.1.call-update) | async-done | bytes 524304 | tf_op jit(solution)/shard_map/while/body/eval_jaxpr/reduce_scatter | solution.py:242
  333.9 48.4 %all-gather.27.cloned.1.call-done = bf16[1024,1024]{1,0:T(8,128)(2,1)} async-done(((bf16[128,1024]{1,0:T(8,128)(2,1)}), bf16[1024,1024]{1,0:T(8,128)(2,1)}) %all-gather.27.cloned.1.call-update) | async-done | bytes 2097168 | tf_op jit(solution)/shard_map/while/body/eval_jaxpr/all_gather | solution.py:258
  382.3 5.2 fusion.213
  388.4 3.2 fusion.214
  391.8 87.1 %reduce-scatter.36.cloned.1.call-done = f32[128,1024]{1,0:T(8,128)} async-done(((f32[1024,1024]{1,0:T(8,128)}), f32[128,1024]{1,0:T(8,128)}) %reduce-scatter.36.cloned.1.call-update) | async-done | bytes 524304 | tf_op jit(solution)/shard_map/while/body/eval_jaxpr/reduce_scatter | solution.py:265
  481.2 48.4 %all-gather.29.cloned.1.call-done = bf16[1024,1024]{1,0:T(8,128)(2,1)} async-done(((bf16[128,1024]{1,0:T(8,128)(2,1)}), bf16[1024,1024]{1,0:T(8,128)(2,1)}) %all-gather.29.cloned.1.call-update) | async-done | bytes 2097168 | tf_op jit(solution)/shard_map/while/body/eval_jaxpr/all_gather | solution.py:273
  532.0 16.4 %while.62 = (s32[]{:T(128)}, f32[2,1024,64]{1,2,0:T(8,128)S(1)}, f32[2,1024,64]{1,2,0:T(8,128)S(1)}, f32[2,2,512,64]{2,3,1,0:T(8,128)}, s32[2]{0:T(128)S(1)}, /*...) while((s32[]{:T(128)}, f32[2,1024,64]{1,2,0:T(8,128)S(1)}, ...), condition=%wide.region_18.18_spmd.clone, body=%wide.region_16.17_spmd.clone.sunk | while | flops 684391424 | bytes 39350560 | solution.py:123
  551.6 3.3 fusion.219
  556.9 4.6 select_add_fusion.14
  564.4 3.0 convolution_add_fusion.2
  567.5 2.5 select_add_fusion.10
  570.0 72.6 %reduce-scatter.38.cloned.1.call-done = f32[128,1024]{1,0:T(8,128)} async-done(((f32[1024,1024]{1,0:T(8,128)}), f32[128,1024]{1,0:T(8,128)}) %reduce-scatter.38.cloned.1.call-update) | async-done | bytes 524304 | tf_op jit(solution)/shard_map/while/body/eval_jaxpr/reduce_scatter | solution.py:290
  646.5 5.7 all-gather.10
  652.4 5.9 all_gather.60
  658.2 8.7 all_gather.59
  666.9 29.1 %all-gather.19.cloned.1.call-done = bf16[1,1024,1024]{2,1,0:T(8,128)(2,1)} async-done(((bf16[1,128,1024]{2,1,0:T(8,128)(2,1)}), bf16[1,1024,1024]{2,1,0:T(8,128)(2,1)}) %all-gather.19.cloned.1.call-update) | async-done | bytes 2097168 | tf_op jit(solution)/shard_map/while/body/eval_jaxpr/all_gather | solution.py:220
  696.0 2.6 add_convert_fusion.3
  698.8 8.0 while.61
  706.8 2.7 fusion.204
  710.3 6.4 all_gather.62
  716.7 5.1 all_gather.61
  721.9 75.1 %reduce-scatter.32.cloned.1.call-done = f32[128,1024]{1,0:T(8,128)} async-done(((f32[1024,1024]{1,0:T(8,128)}), f32[128,1024]{1,0:T(8,128)}) %reduce-scatter.32.cloned.1.call-update) | async-done | bytes 524304 | tf_op jit(solution)/shard_map/while/body/eval_jaxpr/reduce_scatter | solution.py:228
  800.0 5.7 all-gather.11
  805.7 41.9 %all-gather.21.cloned.1.call-done = bf16[1024,1024]{1,0:T(8,128)(2,1)} async-done(((bf16[128,1024]{1,0:T(8,128)(2,1)}), bf16[1024,1024]{1,0:T(8,128)(2,1)}) %all-gather.21.cloned.1.call-update) | async-done | bytes 2097168 | tf_op jit(solution)/shard_map/while/body/eval_jaxpr/all_gather | solution.py:237
  847.6 4.6 multiply_convert_fusion.4
  852.2 13.1 all-gather.25.cloned.1.call-done
  865.3 4.4 fusion.209
  869.8 88.3 %reduce-scatter.34.cloned.1.call-done = f32[128,1024]{1,0:T(8,128)} async-done(((f32[1024,1024]{1,0:T(8,128)}), f32[128,1024]{1,0:T(8,128)}) %reduce-scatter.34.cloned.1.call-update) | async-done | bytes 524304 | tf_op jit(solution)/shard_map/while/body/eval_jaxpr/reduce_scatter | solution.py:242
  960.9 48.4 %all-gather.27.cloned.1.call-done = bf16[1024,1024]{1,0:T(8,128)(2,1)} async-done(((bf16[128,1024]{1,0:T(8,128)(2,1)}), bf16[1024,1024]{1,0:T(8,128)(2,1)}) %all-gather.27.cloned.1.call-update) | async-done | bytes 2097168 | tf_op jit(solution)/shard_map/while/body/eval_jaxpr/all_gather | solution.py:258
  1009.3 5.2 fusion.213
  1015.4 3.2 fusion.214
  1018.7 87.1 %reduce-scatter.36.cloned.1.call-done = f32[128,1024]{1,0:T(8,128)} async-done(((f32[1024,1024]{1,0:T(8,128)}), f32[128,1024]{1,0:T(8,128)}) %reduce-scatter.36.cloned.1.call-update) | async-done | bytes 524304 | tf_op jit(solution)/shard_map/while/body/eval_jaxpr/reduce_scatter | solution.py:265
  1108.2 48.3 %all-gather.29.cloned.1.call-done = bf16[1024,1024]{1,0:T(8,128)(2,1)} async-done(((bf16[128,1024]{1,0:T(8,128)(2,1)}), bf16[1024,1024]{1,0:T(8,128)(2,1)}) %all-gather.29.cloned.1.call-update) | async-done | bytes 2097168 | tf_op jit(solution)/shard_map/while/body/eval_jaxpr/all_gather | solution.py:273
  1159.0 16.4 %while.62 = (s32[]{:T(128)}, f32[2,1024,64]{1,2,0:T(8,128)S(1)}, f32[2,1024,64]{1,2,0:T(8,128)S(1)}, f32[2,2,512,64]{2,3,1,0:T(8,128)}, s32[2]{0:T(128)S(1)}, /*...) while((s32[]{:T(128)}, f32[2,1024,64]{1,2,0:T(8,128)S(1)}, ...), condition=%wide.region_18.18_spmd.clone, body=%wide.region_16.17_spmd.clone.sunk | while | flops 684391424 | bytes 39350560 | solution.py:123
  1178.6 3.3 fusion.219
  1183.8 5.3 select_add_fusion.14
  1192.0 3.1 convolution_add_fusion.2
  1195.2 4.0 select_add_fusion.10
  1199.2 70.4 %reduce-scatter.38.cloned.1.call-done = f32[128,1024]{1,0:T(8,128)} async-done(((f32[1024,1024]{1,0:T(8,128)}), f32[128,1024]{1,0:T(8,128)}) %reduce-scatter.38.cloned.1.call-update) | async-done | bytes 524304 | tf_op jit(solution)/shard_map/while/body/eval_jaxpr/reduce_scatter | solution.py:290
  1279.0 5.9 all-reduce
  1286.0 6.9 reduce-scatter.26.cloned.1.call-done
  1294.9 23.1 %reduce-scatter.28.cloned.1.call-done = f32[256,2]{1,0:T(8,128)} async-done(((f32[1024,2]{1,0:T(8,128)}), f32[256,2]{1,0:T(8,128)}) %reduce-scatter.28.cloned.1.call-update) | async-done | bytes 2064
  1319.0 23.7 %reduce-scatter.30.cloned.1.call-done = f32[256,4]{1,0:T(8,128)} async-done(((f32[1024,4]{1,0:T(8,128)}), f32[256,4]{1,0:T(8,128)}) %reduce-scatter.30.cloned.1.call-update) | async-done | bytes 4112
  1343.7 15.1 %all-reduce.1 = (f32[2,256]{1,0:T(2,128)S(1)}, f32[4,256]{1,0:T(4,128)S(1)}) all-reduce(f32[2,256]{1,0:T(2,128)S(1)} %copy.65, f32[4,256]{1,0:T(4,128)S(1)} %copy.67), channel_id=1, replica_groups=mesh['fsdp'=4,'tensor'=8] {'tensor'}, use_global_device_ids=true, to_apply=%region_36.37 | all-reduce | flops 1536 | bytes 12288 | tf_op jit(solution)/shard_map/psum | solution.py:330
  1361.3 6.7 reduce-scatter.20.cloned.1.call-done
  1370.3 29.0 %reduce-scatter.18.cloned.1.call-done = f32[256,384]{1,0:T(8,128)} async-done(((f32[1024,384]{1,0:T(8,128)}), f32[256,384]{1,0:T(8,128)}) %reduce-scatter.18.cloned.1.call-update) | async-done | bytes 393232 | tf_op jit(solution)/shard_map/reduce_scatter | solution.py:321
  1402.4 31.5 %reduce-scatter.24.cloned.1.call-done = f32[512,256]{1,0:T(8,128)} async-done(((f32[512,1024]{1,0:T(8,128)}), f32[512,256]{1,0:T(8,128)}) %reduce-scatter.24.cloned.1.call-update) | async-done | bytes 524304 | tf_op jit(solution)/shard_map/reduce_scatter | solution.py:326
  1437.1 31.4 %reduce-scatter.22.cloned.1.call-done = f32[256,512]{1,0:T(8,128)} async-done(((f32[1024,512]{1,0:T(8,128)}), f32[256,512]{1,0:T(8,128)}) %reduce-scatter.22.cloned.1.call-update) | async-done | bytes 524304 | tf_op jit(solution)/shard_map/reduce_scatter | solution.py:324
  (416 shorter events, 125.7 us)
Async XLA Ops:
  15.7 55.8 %copy-start.10 = (bf16[256,512]{1,0:T(8,128)(2,1)}, bf16[256,512]{1,0:T(8,128)(2,1)S(1)}, u32[]{:S(2)}) copy-start(bf16[256,512]{1,0:T(8,128)(2,1)S(1)} %get-tuple-element.1005) | copy-start | bytes 786436 | tf_op jit(solution)/shard_map/while
  15.7 55.8 %copy-start.12 = (bf16[256,384]{1,0:T(8,128)(2,1)}, bf16[256,384]{1,0:T(8,128)(2,1)S(1)}, u32[]{:S(2)}) copy-start(bf16[256,384]{1,0:T(8,128)(2,1)S(1)} %get-tuple-element.1000) | copy-start | bytes 589828 | tf_op jit(solution)/shard_map/while
  15.7 67.3 %copy-start.25 = (bf16[2,256]{1,0:T(2,128)(2,1)}, bf16[2,256]{1,0:T(2,128)(2,1)S(1)}, u32[]{:S(2)}) copy-start(bf16[2,256]{1,0:T(2,128)(2,1)S(1)} %get-tuple-element.1004) | copy-start | bytes 3076 | tf_op jit(solution)/shard_map/while
  15.7 157.3 %copy-start.30 = (bf16[128]{0:T(256)(128)(2,1)}, bf16[128]{0:T(256)(128)(2,1)S(1)}, u32[]{:S(2)}) copy-start(bf16[128]{0:T(256)(128)(2,1)S(1)} %get-tuple-element.1006) | copy-start | bytes 772 | tf_op jit(solution)/shard_map/while
  15.7 53.1 %all-gather.19.cloned.1.call-start = ((), (), s32[]{:S(2)}) async-start(), calls=%async_computation.18 | async-start | bytes 2359296 | tf_op jit(solution)/shard_map/while/body/eval_jaxpr/all_gather | solution.py:220
  17.6 152.4 %reduce-scatter.32.cloned.1.call-start = ((), (), s32[]{:S(2)}) async-start(), calls=%async_computation.19 | async-start | bytes 4718592 | tf_op jit(solution)/shard_map/while/body/eval_jaxpr/reduce_scatter | solution.py:228
  37.9 33.6 %copy-start.2 = (bf16[1024,384]{1,0:T(8,128)(2,1)}, bf16[1024,384]{1,0:T(8,128)(2,1)S(1)}, u32[]{:S(2)}) copy-start(bf16[1024,384]{1,0:T(8,128)(2,1)S(1)} %all_gather.59) | copy-start | bytes 2359300 | tf_op jit(solution)/shard_map/while
  82.4 96.3 %all-gather.23.cloned.1.call-start = ((), (), s32[]{:S(2)}) async-start(), calls=%async_computation.21 | async-start | bytes 1310720 | tf_op jit(solution)/shard_map/while/body/eval_jaxpr/all_gather | solution.py:146
  83.0 137.7 %all-gather.21.cloned.1.call-start = ((), (), s32[]{:S(2)}) async-start(), calls=%async_computation.20 | async-start | bytes 2359296 | tf_op jit(solution)/shard_map/while/body/eval_jaxpr/all_gather | solution.py:237
  172.4 65.9 %all-gather.25.cloned.1.call-start = ((), (), s32[]{:S(2)}) async-start(), calls=%async_computation.22 | async-start | bytes 1310720 | tf_op jit(solution)/shard_map/while/body/eval_jaxpr/all_gather | solution.py:148
  173.0 158.1 %reduce-scatter.34.cloned.1.call-start = ((), (), s32[]{:S(2)}) async-start(), calls=%async_computation.23 | async-start | bytes 4718592 | tf_op jit(solution)/shard_map/while/body/eval_jaxpr/reduce_scatter | solution.py:242
  242.8 139.5 %all-gather.27.cloned.1.call-start = ((), (), s32[]{:S(2)}) async-start(), calls=%async_computation.24 | async-start | bytes 2359296 | tf_op jit(solution)/shard_map/while/body/eval_jaxpr/all_gather | solution.py:258
  333.9 144.9 %reduce-scatter.36.cloned.1.call-start = ((), (), s32[]{:S(2)}) async-start(), calls=%async_computation.25 | async-start | bytes 4718592 | tf_op jit(solution)/shard_map/while/body/eval_jaxpr/reduce_scatter | solution.py:265
  391.7 137.9 %all-gather.29.cloned.1.call-start = ((), (), s32[]{:S(2)}) async-start(), calls=%async_computation.26 | async-start | bytes 2359296 | tf_op jit(solution)/shard_map/while/body/eval_jaxpr/all_gather | solution.py:273
  481.2 161.4 %reduce-scatter.38.cloned.1.call-start = ((), (), s32[]{:S(2)}) async-start(), calls=%async_computation.27 | async-start | bytes 4718592 | tf_op jit(solution)/shard_map/while/body/eval_jaxpr/reduce_scatter | solution.py:290
  567.4 77.1 %copy-start.7 = (bf16[2,128,1024]{2,1,0:T(8,128)(2,1)S(1)}, bf16[2,128,1024]{2,1,0:T(8,128)(2,1)}, u32[]{:S(2)}) copy-start(bf16[2,128,1024]{2,1,0:T(8,128)(2,1)} %get-tuple-element.1079) | copy-start | bytes 1572868 | tf_op jit(solution)/shard_map/while
  567.4 77.1 %copy-start.11 = (bf16[256,512]{1,0:T(8,128)(2,1)S(1)}, bf16[256,512]{1,0:T(8,128)(2,1)}, u32[]{:S(2)}) copy-start(bf16[256,512]{1,0:T(8,128)(2,1)} %copy-done.10) | copy-start | bytes 786436 | tf_op jit(solution)/shard_map/while
  567.4 77.1 %copy-start.13 = (bf16[256,384]{1,0:T(8,128)(2,1)S(1)}, bf16[256,384]{1,0:T(8,128)(2,1)}, u32[]{:S(2)}) copy-start(bf16[256,384]{1,0:T(8,128)(2,1)} %copy-done.12) | copy-start | bytes 589828 | tf_op jit(solution)/shard_map/while
  567.4 77.1 %copy-start.26 = (bf16[2,256]{1,0:T(2,128)(2,1)S(1)}, bf16[2,256]{1,0:T(2,128)(2,1)}, u32[]{:S(2)}) copy-start(bf16[2,256]{1,0:T(2,128)(2,1)} %copy-done.25) | copy-start | bytes 3076 | tf_op jit(solution)/shard_map/while
  567.4 77.1 %copy-start.29 = (bf16[2,48]{1,0:T(2,128)(2,1)S(1)}, bf16[2,48]{1,0:T(2,128)(2,1)}, u32[]{:S(2)}) copy-start(bf16[2,48]{1,0:T(2,128)(2,1)} %copy-done.28) | copy-start | bytes 580 | tf_op jit(solution)/shard_map/while
  567.4 77.1 %copy-start.31 = (bf16[128]{0:T(256)(128)(2,1)S(1)}, bf16[128]{0:T(256)(128)(2,1)}, u32[]{:S(2)}) copy-start(bf16[128]{0:T(256)(128)(2,1)} %copy-done.30) | copy-start | bytes 772 | tf_op jit(solution)/shard_map/while
  644.5 54.1 %copy-start.10 = (bf16[256,512]{1,0:T(8,128)(2,1)}, bf16[256,512]{1,0:T(8,128)(2,1)S(1)}, u32[]{:S(2)}) copy-start(bf16[256,512]{1,0:T(8,128)(2,1)S(1)} %get-tuple-element.1005) | copy-start | bytes 786436 | tf_op jit(solution)/shard_map/while
  644.5 54.1 %copy-start.12 = (bf16[256,384]{1,0:T(8,128)(2,1)}, bf16[256,384]{1,0:T(8,128)(2,1)S(1)}, u32[]{:S(2)}) copy-start(bf16[256,384]{1,0:T(8,128)(2,1)S(1)} %get-tuple-element.1000) | copy-start | bytes 589828 | tf_op jit(solution)/shard_map/while
  644.6 65.7 %copy-start.25 = (bf16[2,256]{1,0:T(2,128)(2,1)}, bf16[2,256]{1,0:T(2,128)(2,1)S(1)}, u32[]{:S(2)}) copy-start(bf16[2,256]{1,0:T(2,128)(2,1)S(1)} %get-tuple-element.1004) | copy-start | bytes 3076 | tf_op jit(solution)/shard_map/while
  644.6 155.4 %copy-start.30 = (bf16[128]{0:T(256)(128)(2,1)}, bf16[128]{0:T(256)(128)(2,1)S(1)}, u32[]{:S(2)}) copy-start(bf16[128]{0:T(256)(128)(2,1)S(1)} %get-tuple-element.1006) | copy-start | bytes 772 | tf_op jit(solution)/shard_map/while
  644.6 51.4 %all-gather.19.cloned.1.call-start = ((), (), s32[]{:S(2)}) async-start(), calls=%async_computation.18 | async-start | bytes 2359296 | tf_op jit(solution)/shard_map/while/body/eval_jaxpr/all_gather | solution.py:220
  646.4 150.6 %reduce-scatter.32.cloned.1.call-start = ((), (), s32[]{:S(2)}) async-start(), calls=%async_computation.19 | async-start | bytes 4718592 | tf_op jit(solution)/shard_map/while/body/eval_jaxpr/reduce_scatter | solution.py:228
  709.5 96.2 %all-gather.23.cloned.1.call-start = ((), (), s32[]{:S(2)}) async-start(), calls=%async_computation.21 | async-start | bytes 1310720 | tf_op jit(solution)/shard_map/while/body/eval_jaxpr/all_gather | solution.py:146
  710.3 137.3 %all-gather.21.cloned.1.call-start = ((), (), s32[]{:S(2)}) async-start(), calls=%async_computation.20 | async-start | bytes 2359296 | tf_op jit(solution)/shard_map/while/body/eval_jaxpr/all_gather | solution.py:237
  799.3 65.9 %all-gather.25.cloned.1.call-start = ((), (), s32[]{:S(2)}) async-start(), calls=%async_computation.22 | async-start | bytes 1310720 | tf_op jit(solution)/shard_map/while/body/eval_jaxpr/all_gather | solution.py:148
  799.9 158.1 %reduce-scatter.34.cloned.1.call-start = ((), (), s32[]{:S(2)}) async-start(), calls=%async_computation.23 | async-start | bytes 4718592 | tf_op jit(solution)/shard_map/while/body/eval_jaxpr/reduce_scatter | solution.py:242
  869.7 139.5 %all-gather.27.cloned.1.call-start = ((), (), s32[]{:S(2)}) async-start(), calls=%async_computation.24 | async-start | bytes 2359296 | tf_op jit(solution)/shard_map/while/body/eval_jaxpr/all_gather | solution.py:258
  960.9 144.9 %reduce-scatter.36.cloned.1.call-start = ((), (), s32[]{:S(2)}) async-start(), calls=%async_computation.25 | async-start | bytes 4718592 | tf_op jit(solution)/shard_map/while/body/eval_jaxpr/reduce_scatter | solution.py:265
  1018.7 137.9 %all-gather.29.cloned.1.call-start = ((), (), s32[]{:S(2)}) async-start(), calls=%async_computation.26 | async-start | bytes 2359296 | tf_op jit(solution)/shard_map/while/body/eval_jaxpr/all_gather | solution.py:273
  1108.1 161.4 %reduce-scatter.38.cloned.1.call-start = ((), (), s32[]{:S(2)}) async-start(), calls=%async_computation.27 | async-start | bytes 4718592 | tf_op jit(solution)/shard_map/while/body/eval_jaxpr/reduce_scatter | solution.py:290
  1195.1 76.3 %copy-start.7 = (bf16[2,128,1024]{2,1,0:T(8,128)(2,1)S(1)}, bf16[2,128,1024]{2,1,0:T(8,128)(2,1)}, u32[]{:S(2)}) copy-start(bf16[2,128,1024]{2,1,0:T(8,128)(2,1)} %get-tuple-element.1079) | copy-start | bytes 1572868 | tf_op jit(solution)/shard_map/while
  1195.1 76.3 %copy-start.11 = (bf16[256,512]{1,0:T(8,128)(2,1)S(1)}, bf16[256,512]{1,0:T(8,128)(2,1)}, u32[]{:S(2)}) copy-start(bf16[256,512]{1,0:T(8,128)(2,1)} %copy-done.10) | copy-start | bytes 786436 | tf_op jit(solution)/shard_map/while
  1195.1 76.3 %copy-start.13 = (bf16[256,384]{1,0:T(8,128)(2,1)S(1)}, bf16[256,384]{1,0:T(8,128)(2,1)}, u32[]{:S(2)}) copy-start(bf16[256,384]{1,0:T(8,128)(2,1)} %copy-done.12) | copy-start | bytes 589828 | tf_op jit(solution)/shard_map/while
  1195.1 76.3 %copy-start.26 = (bf16[2,256]{1,0:T(2,128)(2,1)S(1)}, bf16[2,256]{1,0:T(2,128)(2,1)}, u32[]{:S(2)}) copy-start(bf16[2,256]{1,0:T(2,128)(2,1)} %copy-done.25) | copy-start | bytes 3076 | tf_op jit(solution)/shard_map/while
  1195.1 76.3 %copy-start.29 = (bf16[2,48]{1,0:T(2,128)(2,1)S(1)}, bf16[2,48]{1,0:T(2,128)(2,1)}, u32[]{:S(2)}) copy-start(bf16[2,48]{1,0:T(2,128)(2,1)} %copy-done.28) | copy-start | bytes 580 | tf_op jit(solution)/shard_map/while
  1195.1 76.3 %copy-start.31 = (bf16[128]{0:T(256)(128)(2,1)S(1)}, bf16[128]{0:T(256)(128)(2,1)}, u32[]{:S(2)}) copy-start(bf16[128]{0:T(256)(128)(2,1)} %copy-done.30) | copy-start | bytes 772 | tf_op jit(solution)/shard_map/while
  1271.6 21.3 %reduce-scatter.26.cloned.1.call-start = ((), (), s32[]{:S(2)}) async-start(), calls=%async_computation.15 | async-start | bytes 122880
  1272.5 45.5 %reduce-scatter.28.cloned.1.call-start = ((), (), s32[]{:S(2)}) async-start(), calls=%async_computation.16 | async-start | bytes 655360
  1273.6 69.1 %reduce-scatter.30.cloned.1.call-start = ((), (), s32[]{:S(2)}) async-start(), calls=%async_computation.17 | async-start | bytes 655360
  1274.7 93.2 %reduce-scatter.20.cloned.1.call-start = ((), (), s32[]{:S(2)}) async-start(), calls=%async_computation.12 | async-start | bytes 655360 | tf_op jit(solution)/shard_map/reduce_scatter | solution.py:323
  1275.4 123.9 %reduce-scatter.18.cloned.1.call-start = ((), (), s32[]{:S(2)}) async-start(), calls=%async_computation.11 | async-start | bytes 1966080 | tf_op jit(solution)/shard_map/reduce_scatter | solution.py:321
  1276.2 157.6 %reduce-scatter.24.cloned.1.call-start = ((), (), s32[]{:S(2)}) async-start(), calls=%async_computation.14 | async-start | bytes 2621440 | tf_op jit(solution)/shard_map/reduce_scatter | solution.py:326
  1276.3 82.5 %copy-start.33 = (f32[2,256]{1,0:T(2,128)S(1)}, f32[2,256]{1,0:T(2,128)}, u32[]{:S(2)}) copy-start(f32[2,256]{1,0:T(2,128)} %param.32) | copy-start | bytes 6148
  1276.3 82.5 %copy-start.34 = (f32[2,2,256]{2,1,0:T(2,128)S(1)}, f32[2,2,256]{2,1,0:T(2,128)}, u32[]{:S(2)}) copy-start(f32[2,2,256]{2,1,0:T(2,128)} %param.40) | copy-start | bytes 12292
  1276.3 83.7 %copy-start.27 = (f32[4,256]{1,0:T(4,128)S(1)}, f32[4,256]{1,0:T(4,128)}, u32[]{:S(2)}) copy-start(f32[4,256]{1,0:T(4,128)} %param.33) | copy-start | bytes 12292
  1276.3 83.7 %copy-start.32 = (f32[2,4,256]{2,1,0:T(4,128)S(1)}, f32[2,4,256]{2,1,0:T(4,128)}, u32[]{:S(2)}) copy-start(f32[2,4,256]{2,1,0:T(4,128)} %param.41) | copy-start | bytes 24580
  1276.4 91.6 %copy-start.22 = (f32[128,256]{1,0:T(8,128)S(1)}, f32[128,256]{1,0:T(8,128)}, u32[]{:S(2)}) copy-start(f32[128,256]{1,0:T(8,128)} %param.28) | copy-start | bytes 393220
  1276.4 91.5 %copy-start.23 = (f32[2,128,256]{2,1,0:T(8,128)S(1)}, f32[2,128,256]{2,1,0:T(8,128)}, u32[]{:S(2)}) copy-start(f32[2,128,256]{2,1,0:T(8,128)} %param.36) | copy-start | bytes 786436
  1276.9 122.4 %copy-start.18 = (f32[256,384]{1,0:T(8,128)S(1)}, f32[256,384]{1,0:T(8,128)}, u32[]{:S(2)}) copy-start(f32[256,384]{1,0:T(8,128)} %param.26) | copy-start | bytes 1179652
  1276.9 122.4 %copy-start.21 = (f32[2,256,384]{2,1,0:T(8,128)S(1)}, f32[2,256,384]{2,1,0:T(8,128)}, u32[]{:S(2)}) copy-start(f32[2,256,384]{2,1,0:T(8,128)} %param.34) | copy-start | bytes 2359300
  1277.0 191.5 %reduce-scatter.22.cloned.1.call-start = ((), (), s32[]{:S(2)}) async-start(), calls=%async_computation.13 | async-start | bytes 2621440 | tf_op jit(solution)/shard_map/reduce_scatter | solution.py:324
  1284.9 116.5 %copy-start.40 = (f32[128]{0:T(128)}, f32[128]{0:T(128)S(1)}, u32[]{:S(2)}) copy-start(f32[128]{0:T(128)S(1)} %get-tuple-element.456) | copy-start | bytes 1540
  1293.7 107.7 %copy-start.36 = (f32[2,48]{1,0:T(2,128)}, f32[2,48]{1,0:T(2,128)S(1)}, u32[]{:S(2)}) copy-start(f32[2,48]{1,0:T(2,128)S(1)} %copy.63) | copy-start | bytes 1156
  1358.8 42.6 %copy-start.35 = (f32[4,256]{1,0:T(4,128)}, f32[4,256]{1,0:T(4,128)S(1)}, u32[]{:S(2)}) copy-start(f32[4,256]{1,0:T(4,128)S(1)} %get-tuple-element.443) | copy-start | bytes 12292
  1358.8 42.6 %copy-start.39 = (f32[2,256]{1,0:T(2,128)}, f32[2,256]{1,0:T(2,128)S(1)}, u32[]{:S(2)}) copy-start(f32[2,256]{1,0:T(2,128)S(1)} %get-tuple-element.442) | copy-start | bytes 6148
  1370.3 63.5 %copy-start.14 = (f32[512,256]{1,0:T(8,128)S(1)}, f32[512,256]{1,0:T(8,128)}, u32[]{:S(2)}) copy-start(f32[512,256]{1,0:T(8,128)} %param.31) | copy-start | bytes 1572868
  1370.3 63.5 %copy-start.19 = (f32[2,512,256]{2,1,0:T(8,128)S(1)}, f32[2,512,256]{2,1,0:T(8,128)}, u32[]{:S(2)}) copy-start(f32[2,512,256]{2,1,0:T(8,128)} %param.39) | copy-start | bytes 3145732
  1402.3 66.1 %copy-start.15 = (f32[256,512]{1,0:T(8,128)S(1)}, f32[256,512]{1,0:T(8,128)}, u32[]{:S(2)}) copy-start(f32[256,512]{1,0:T(8,128)} %param.29) | copy-start | bytes 1572868
  1402.4 66.1 %copy-start.20 = (f32[2,256,512]{2,1,0:T(8,128)S(1)}, f32[2,256,512]{2,1,0:T(8,128)}, u32[]{:S(2)}) copy-start(f32[2,256,512]{2,1,0:T(8,128)} %param.37) | copy-start | bytes 3145732
  (45 other events, 214.6 us)
Sparse Core Ops, SparseCore 0:
  19.3 49.5 all-gather.18
  82.5 87.4 reduce-scatter.31
  334.0 48.2 all-gather.26
  481.3 48.2 all-gather.28
  555.1 87.4 reduce-scatter.37
  647.8 48.1 all-gather.18
  709.6 87.2 reduce-scatter.31
  961.0 48.2 all-gather.26
  1108.3 48.2 all-gather.28
  1182.0 87.4 reduce-scatter.37
Sparse Core Ops, SparseCore 1:
  85.1 15.4 all-gather.22
  172.5 48.1 all-gather.20
  222.7 15.6 all-gather.24
  242.8 88.2 reduce-scatter.33
  391.8 87.0 reduce-scatter.35
  712.5 15.4 all-gather.22
  799.4 48.1 all-gather.20
  849.7 15.6 all-gather.24
  869.8 88.2 reduce-scatter.33
  1018.8 87.0 reduce-scatter.35
  1275.1 17.7 reduce-scatter.25
  1296.0 21.9 reduce-scatter.27
  1321.1 21.6 reduce-scatter.29
  1346.4 21.5 reduce-scatter.19
  1371.2 28.1 reduce-scatter.17
  1402.5 31.3 reduce-scatter.23
  1437.1 31.3 reduce-scatter.21
where the time goes:
time: 1480 us
  waiting for transfers between devices  1170 us (79%)
  matrix products  107 us (7%)
  blocking collectives  95.7 us (6%)
  other arithmetic  55.6 us (4%)
  local copies, waits for them, and re-layouts  30.9 us (2%)
  between operations  16.7 us (1%)
    reduce_scatter x2, waiting for transfers between devices, micro_step(): lax.psum_scatter(jnp.dot(active, w_downward, preferred_element_type=jnp.f...  177 us
    reduce_scatter x2, waiting for transfers between devices, micro_step(): lax.psum_scatter(jnp.dot(grad_inner_b, w_upward.T, preferred_element_type...  174 us
    reduce_scatter x2, waiting for transfers between devices, micro_step(): lax.psum_scatter(jnp.dot(attn, w_output, preferred_element_type=jnp.float...  150 us
    reduce_scatter x2, waiting for transfers between devices, micro_step(): lax.psum_scatter(jnp.dot(grad_qkv_b, w_attn.T, preferred_element_type=jnp...  143 us
    all_gather x2, waiting for transfers between devices, micro_step(): grad_full = lax.all_gather(grad_two_b, 'tensor', axis=0, tiled=True)  96.7 us
    all_gather x2, waiting for transfers between devices, micro_step(): one_full = lax.all_gather(grad_one_b, 'tensor', axis=0, tiled=True)  96.7 us
    all_gather x2, waiting for transfers between devices, micro_step(): expanded = lax.all_gather(hidden_one_b, 'tensor', axis=0, tiled=True)  83.8 us
    all_gather x2, waiting for transfers between devices, micro_step(): gathered = lax.all_gather(tokens, 'tensor', axis=0, tiled=True)  60 us
  transfers between devices with their start and end apart: 27, of which 25 were waited for; matrix products, arithmetic and copies ran while one was open for 4% of the time, Pallas kernels for 0%

commit v1 on v0

v1 whole, which is shorter than its diff:
```python
import jax
import jax.numpy as jnp
from jax import lax
from jax.sharding import PartitionSpec as P

norm_eps = 1e-05
beta_one = 0.9
beta_two = 0.999
adam_eps = 1e-08
adam_step = 4.0
matrix_rate = 0.01
output_rate = 0.1
vector_rate = 0.1
decay_rate = 0.1
inv_root_two = 0.7071067811865476
inv_root_tau = 0.3989422804014327


def layer_norm(resid, gain_row, shift_row):
    center = resid - jnp.mean(resid, axis=-1, keepdims=True)
    spread = lax.rsqrt(jnp.mean(center * center, axis=-1, keepdims=True) + norm_eps)
    normed = center * spread
    return (normed * gain_row + shift_row, normed, spread)


def norm_back(grad_out, gain_row, normed, spread):
    scaled = grad_out * gain_row
    return spread * (
        scaled
        - jnp.mean(scaled, axis=-1, keepdims=True)
        - normed * jnp.mean(scaled * normed, axis=-1, keepdims=True)
    )


def gelu_value(inner):
    return inner * 0.5 * (1.0 + jax.scipy.special.erf(inner * inv_root_two))


def gelu_slope(inner):
    return (
        0.5 * (1.0 + jax.scipy.special.erf(inner * inv_root_two))
        + inner * jnp.exp(-0.5 * inner * inner) * inv_root_tau
    )


def split_heads(qkv, heads, head_width):
    seq_length = qkv.shape[0]
    triple = jnp.transpose(qkv.reshape(seq_length, heads, 3, head_width), (2, 1, 0, 3))
    return (triple[0], triple[1], triple[2])


def merge_heads(mixed):
    heads, seq_length, head_width = mixed.shape
    return jnp.transpose(mixed, (1, 0, 2)).reshape(seq_length, heads * head_width)


def attention_forward(queries, key_rows, values):
    heads, seq_length, head_width = queries.shape
    block_rows = min(512, seq_length)
    block_count = seq_length // block_rows
    score_scale = head_width ** (-0.5)

    def one_block(block_index):
        row_block = lax.dynamic_slice_in_dim(queries, block_index * block_rows, block_rows, 1)
        scores = (
            jnp.einsum("hqd,hkd->hqk", row_block, key_rows, preferred_element_type=jnp.float32)
            * score_scale
        )
        row_max = jnp.max(scores, axis=-1, keepdims=True)
        logsum = row_max + jnp.log(jnp.sum(jnp.exp(scores - row_max), axis=-1, keepdims=True))
        softmax_weights = jnp.exp(scores - logsum).astype(jnp.bfloat16)
        mixed = jnp.einsum(
            "hqk,hkd->hqd", softmax_weights, values, preferred_element_type=jnp.float32
        )
        return (mixed.astype(jnp.bfloat16), logsum[..., 0])

    mixed, logsum = lax.map(one_block, jnp.arange(block_count, dtype=jnp.int32))
    mixed = jnp.transpose(mixed, (1, 0, 2, 3)).reshape(heads, seq_length, head_width)
    logsum = jnp.transpose(logsum, (1, 0, 2)).reshape(heads, seq_length)
    return (mixed, logsum)


def attention_back(queries, key_rows, values, logsum, grad_mixed):
    heads, seq_length, head_width = queries.shape
    block_rows = min(512, seq_length)
    block_count = seq_length // block_rows
    score_scale = head_width ** (-0.5)

    def block_step(carry, block_index):
        grad_keys, grad_values = carry
        first_row = block_index * block_rows
        row_block = lax.dynamic_slice_in_dim(queries, first_row, block_rows, 1)
        log_block = lax.dynamic_slice_in_dim(logsum, first_row, block_rows, 1)
        grad_block = lax.dynamic_slice_in_dim(grad_mixed, first_row, block_rows, 1)
        scores = (
            jnp.einsum("hqd,hkd->hqk", row_block, key_rows, preferred_element_type=jnp.float32)
            * score_scale
        )
        chances = jnp.exp(scores - log_block[..., None])
        chances_b = chances.astype(jnp.bfloat16)
        grad_values = grad_values + jnp.einsum(
            "hqk,hqd->hkd", chances_b, grad_block, preferred_element_type=jnp.float32
        )
        grad_scores = jnp.einsum(
            "hqd,hkd->hqk", grad_block, values, preferred_element_type=jnp.float32
        )
        grad_logits = chances * (
            grad_scores - jnp.sum(chances * grad_scores, axis=-1, keepdims=True)
        )
        logits_b = grad_logits.astype(jnp.bfloat16)
        grad_query = (
            jnp.einsum("hqk,hkd->hqd", logits_b, key_rows, preferred_element_type=jnp.float32)
            * score_scale
        )
        grad_keys = (
            grad_keys
            + jnp.einsum("hqk,hqd->hkd", logits_b, row_block, preferred_element_type=jnp.float32)
            * score_scale
        )
        return ((grad_keys, grad_values), grad_query)

    zeros = jnp.zeros((heads, seq_length, head_width), jnp.float32)
    (grad_keys, grad_values), grad_queries = lax.scan(
        block_step, (zeros, zeros), jnp.arange(block_count, dtype=jnp.int32)
    )
    grad_queries = jnp.transpose(grad_queries, (1, 0, 2, 3)).reshape(heads, seq_length, head_width)
    return (grad_queries, grad_keys, grad_values)


def adamw_update(weight, moments, grad, rate, decay):
    first_moment = beta_one * moments[0] + (1.0 - beta_one) * grad
    second_moment = beta_two * moments[1] + (1.0 - beta_two) * grad * grad
    direction = (
        first_moment
        / (1.0 - beta_one**adam_step)
        / (jnp.sqrt(second_moment / (1.0 - beta_two**adam_step)) + adam_eps)
    )
    return (weight - rate * (direction + decay * weight), jnp.stack([first_moment, second_moment]))

AXES = ("fsdp", "tensor")


class Layout:
    def __init__(self, local_heads, local_seqs):
        self.fsdp = lax.axis_size("fsdp")
        self.tensor = lax.axis_size("tensor")
        self.seqs = local_seqs
        self.core = 2 if local_heads % 2 == 0 and self.fsdp % 2 == 0 else 1
        self.outer = self.fsdp // self.core
        self.high = self.core * local_seqs
        self.low = self.tensor // self.high
        self.fsdp_index = lax.axis_index("fsdp")
        self.outer_index = self.fsdp_index // self.core
        self.core_index = self.fsdp_index % self.core
        self.high_index = lax.axis_index("tensor") // self.low

    def send(self, value, target):
        pairs = []
        for outer in range(self.outer):
            for core in range(self.core):
                for high in range(self.high):
                    for low in range(self.low):
                        o, c, h, l = target(outer, core, high, low)
                        source_id = (outer * self.core + core) * self.tensor + high * self.low + low
                        target_id = (o * self.core + c) * self.tensor + h * self.low + l
                        pairs.append((source_id, target_id))
        return lax.ppermute(value, AXES, pairs)

    def swap_core(self, value):
        return self.send(value, lambda o, c, h, l: (o, 1 - c, h, l))

    def to_low(self, value, step):
        return self.send(value, lambda o, c, h, l: (o, c, h, (l + step) % self.low))

    def to_high(self, value, step):
        return self.send(value, lambda o, c, h, l: (o, c, (h + step) % self.high, l))

    def to_outer(self, value, step):
        return self.send(value, lambda o, c, h, l: ((o + step) % self.outer, c, h, l))

    def to_sequence(self, blocks):
        within = self.high_index % self.seqs
        return [
            self.send(
                lax.dynamic_index_in_dim(blocks, (within + k) % self.seqs, 0, keepdims=False),
                lambda o, c, h, l, k=k: (
                    o,
                    h // self.seqs,
                    c * self.seqs + (h % self.seqs + k) % self.seqs,
                    l,
                ),
            )
            for k in range(self.seqs)
        ]

    def from_sequence(self, pieces):
        within = self.high_index % self.seqs
        back = []
        for k in range(self.seqs):
            back.append(
                self.send(
                    pieces[k],
                    lambda o, c, h, l, k=k: (
                        o,
                        h // self.seqs,
                        c * self.seqs + (h % self.seqs - k) % self.seqs,
                        l,
                    ),
                )
            )
        if self.seqs == 2:
            return jnp.where(within == 0, jnp.stack(back), jnp.stack(back[::-1]))
        stacked = jnp.stack(back)
        order = (jnp.arange(self.seqs) - within) % self.seqs
        return jnp.take(stacked, order, axis=0)

    def share(self, own):
        pieces = []
        for step in range(self.low):
            piece = own if step == 0 else self.to_low(own, -step)
            pieces.append(piece)
            if self.core == 2:
                pieces.append(self.swap_core(piece))
        return jnp.concatenate(pieces, axis=0)

    def reduce(self, partial):
        count = partial.shape[0] // (self.core * self.low)
        sums = []
        for step in range(self.low):
            base = step * self.core * count
            total = partial[base : base + count]
            if self.core == 2:
                other = partial[base + count : base + 2 * count].astype(jnp.bfloat16)
                total = total + self.swap_core(other).astype(jnp.float32)
            sums.append(total)
        result = sums[0]
        for step in range(1, self.low):
            result = result + self.to_low(sums[step].astype(jnp.bfloat16), step).astype(jnp.float32)
        return result

    def ordered(self, index, parts, axis):
        count = len(parts)
        if count == 1:
            return parts[0]
        if count == 2:
            return jnp.where(
                index == 0,
                jnp.concatenate(parts, axis=axis),
                jnp.concatenate(parts[::-1], axis=axis),
            )
        width = parts[0].shape[axis]
        shape = list(parts[0].shape)
        shape[axis] = width * count
        result = jnp.zeros(shape, parts[0].dtype)
        for step, part in enumerate(parts):
            result = lax.dynamic_update_slice_in_dim(
                result, part, ((index + step) % count) * width, axis
            )
        return result

    def core_rows(self, rows, core):
        count = rows.shape[0] // self.core
        return lax.dynamic_slice_in_dim(rows, core * count, count, 0)

    def gather_weight(self, rows, extra=None):
        mine = self.core_rows(rows, self.core_index)
        if extra is not None:
            mine = jnp.concatenate([mine, extra], axis=0)
        if self.core == 2:
            other = self.core_rows(rows, 1 - self.core_index)
            if extra is not None:
                other = jnp.concatenate([other, extra], axis=0)
            mine = self.ordered(self.core_index, [mine, self.swap_core(other)], 1)
        column = [mine] + [self.to_high(mine, -step) for step in range(1, self.high)]
        column = jnp.concatenate(column, axis=0)
        return self.ordered(
            self.outer_index,
            [column] + [self.to_outer(column, -step) for step in range(1, self.outer)],
            1,
        )

    def scatter_weight(self, grad, extra=None):
        if extra is not None:
            grad = jnp.concatenate([grad, extra], axis=1)
        width = grad.shape[2] // self.outer

        def columns(place):
            return lax.dynamic_slice_in_dim(grad, (place % self.outer) * width, width, 2)

        total = columns(self.outer_index)
        for step in range(1, self.outer):
            part = columns(self.outer_index + step).astype(jnp.bfloat16)
            total = total + self.to_outer(part, step).astype(jnp.float32)
        column = total[0]
        for step in range(1, self.high):
            part = total[step].astype(jnp.bfloat16)
            column = column + self.to_high(part, step).astype(jnp.float32)
        if self.core == 1:
            if extra is None:
                return column
            return column[: -extra.shape[1]], column[-extra.shape[1] :]
        width = width // self.core
        mine = lax.dynamic_slice_in_dim(column, self.core_index * width, width, 1)
        other = self.swap_core(
            lax.dynamic_slice_in_dim(column, (1 - self.core_index) * width, width, 1)
        )
        if extra is None:
            return self.ordered(self.core_index, [mine, other], 0)
        count = extra.shape[1]
        return (
            self.ordered(self.core_index, [mine[:-count], other[:-count]], 0),
            mine[-count:] + other[-count:],
        )

    def total(self, value):
        if self.core == 2:
            value = value + self.swap_core(value)
        bit = 1
        while bit < self.low:
            value = value + self.send(value, lambda o, c, h, l: (o, c, h, l ^ bit))
            bit *= 2
        bit = 1
        while bit < self.outer:
            value = value + self.send(value, lambda o, c, h, l: (o ^ bit, c, h, l))
            bit *= 2
        bit = 1
        while bit < self.high:
            value = value + self.send(value, lambda o, c, h, l: (o, c, h ^ bit, l))
            bit *= 2
        return value


SMALL_ROWS = 16


def pad_columns(rows, width):
    return jnp.pad(rows, [(0, 0)] * (rows.ndim - 1) + [(0, width - rows.shape[-1])])


def per_device(
    layer_input,
    cotangent,
    attn_weight,
    attn_bias,
    out_weight,
    up_weight,
    up_bias,
    down_weight,
    norm_gains,
    norm_shifts,
    attn_weight_moments,
    attn_bias_moments,
    out_weight_moments,
    up_weight_moments,
    up_bias_moments,
    down_weight_moments,
    norm_gains_moments,
    norm_shifts_moments,
):
    local_heads = attn_bias.shape[0]
    local_seqs, block_tokens, model_width = layer_input.shape
    lay = Layout(local_heads, local_seqs)
    fsdp, core, high = lay.fsdp, lay.core, lay.high
    bias_width = attn_bias.shape[1]
    head_width = bias_width * fsdp // 3
    part_heads = local_heads // core
    heads = part_heads * high
    shard_width = model_width // fsdp
    hidden_part = up_bias.shape[0]
    weights = (
        attn_weight,
        attn_bias,
        out_weight,
        up_weight,
        up_bias,
        down_weight,
        norm_gains,
        norm_shifts,
    )
    half = jnp.bfloat16
    wide = jnp.float32

    pairs = lay.to_sequence(jnp.stack([layer_input, cotangent], axis=1))
    tokens = jnp.concatenate([pair[0] for pair in pairs], axis=0)
    upward = jnp.concatenate([pair[1] for pair in pairs], axis=0).astype(wide)
    small = jnp.concatenate(
        [
            norm_gains.astype(half),
            norm_shifts.astype(half),
            pad_columns(attn_bias.astype(half).reshape(1, -1), shard_width),
            pad_columns(up_bias.astype(half).reshape(1, -1), shard_width),
            jnp.zeros((SMALL_ROWS - 8, shard_width), half),
        ],
        axis=0,
    )
    attn_rows = part_heads * 3 * head_width
    packed = lay.gather_weight(attn_weight.astype(half).T, small)
    packed = packed.reshape(high, attn_rows + SMALL_ROWS, model_width)
    w_attn = packed[:, :attn_rows].reshape(high * attn_rows, model_width)
    small = packed[:, attn_rows:]
    gain_rows = small[0, 0:2].astype(wide)
    shift_rows = small[0, 2:6].astype(wide)
    b_attn = small[:, 6].reshape(high, fsdp, shard_width)[:, :, : local_heads * bias_width]
    b_attn = b_attn.reshape(high, fsdp, core, part_heads, bias_width)
    b_attn = lax.dynamic_index_in_dim(b_attn, lay.core_index, 2, keepdims=False)
    b_attn = jnp.transpose(b_attn, (0, 2, 1, 3)).reshape(-1).astype(wide)
    b_upward = small[:, 7].reshape(high, fsdp, shard_width)[:, :, :hidden_part]
    b_upward = b_upward.reshape(high, core, (fsdp // core) * hidden_part)
    b_upward = lax.dynamic_index_in_dim(b_upward, lay.core_index, 1, keepdims=False)
    b_upward = b_upward.reshape(-1).astype(wide)
    w_output = lay.gather_weight(out_weight.astype(half))
    w_upward = lay.gather_weight(up_weight.astype(half).T)
    w_downward = lay.gather_weight(down_weight.astype(half))

    def times(left, right):
        return jnp.dot(left, right, preferred_element_type=wide)

    def times_t(left, right):
        return lax.dot_general(left, right, (((1,), (1,)), ((), ())), preferred_element_type=wide)

    def t_times(left, right):
        return lax.dot_general(left, right, (((0,), (0,)), ((), ())), preferred_element_type=wide)

    gathered = lay.share(tokens)
    seq_length = gathered.shape[0]
    qkv = (times_t(gathered, w_attn) + b_attn).astype(half)
    queries, key_rows, values = split_heads(qkv, heads, head_width)
    mixed, logsum = attention_forward(queries, key_rows, values)
    attn = merge_heads(mixed)
    attn_out = lay.reduce(times(attn, w_output))
    resid_one = attn_out + shift_rows[0] + tokens.astype(wide)
    hidden_one, normed_one, spread_one = layer_norm(resid_one, gain_rows[0], shift_rows[1])
    expanded = lay.share(hidden_one.astype(half))
    inner = times_t(expanded, w_upward) + b_upward
    active = gelu_value(inner).astype(half)
    ffn_out = lay.reduce(times(active, w_downward))
    resid_two = ffn_out + shift_rows[2] + hidden_one
    result, normed_two, spread_two = layer_norm(resid_two, gain_rows[1], shift_rows[3])
    output = result.astype(half).reshape(local_seqs, block_tokens, model_width)
    outputs = lay.from_sequence(output)

    grad_two = norm_back(upward, gain_rows[1], normed_two, spread_two)
    grad_full = lay.share(grad_two.astype(half))
    grad_inner = times_t(grad_full, w_downward) * gelu_slope(inner)
    grad_inner_b = grad_inner.astype(half)
    grad_hidden = grad_two + lay.reduce(times(grad_inner_b, w_upward))
    grad_down = t_times(active, grad_full)
    grad_upward = t_times(grad_inner_b, expanded)
    grad_one = norm_back(grad_hidden, gain_rows[0], normed_one, spread_one)
    one_full = lay.share(grad_one.astype(half))
    grad_attn = times_t(one_full, w_output).astype(half)
    grad_mixed = jnp.transpose(grad_attn.reshape(seq_length, heads, head_width), (1, 0, 2))
    grad_output = t_times(attn, one_full)
    grad_queries, grad_keys, grad_values = attention_back(
        queries, key_rows, values, logsum, grad_mixed
    )
    grad_qkv = jnp.transpose(
        jnp.stack([grad_queries, grad_keys, grad_values]), (2, 1, 0, 3)
    ).reshape(seq_length, -1)
    grad_qkv_b = grad_qkv.astype(half)
    input_grad = grad_one + lay.reduce(times(grad_qkv_b, w_attn))
    input_grads = lay.from_sequence(input_grad.reshape(local_seqs, block_tokens, model_width))
    grad_attn_w = t_times(grad_qkv_b, gathered)

    norm_sums = lay.total(
        jnp.stack(
            [
                jnp.sum(grad_hidden * normed_one, axis=0),
                jnp.sum(upward * normed_two, axis=0),
                jnp.sum(grad_one, axis=0),
                jnp.sum(grad_hidden, axis=0),
                jnp.sum(grad_two, axis=0),
                jnp.sum(upward, axis=0),
            ]
        )
    )
    norm_sums = lax.dynamic_slice_in_dim(norm_sums, lay.fsdp_index * shard_width, shard_width, 1)
    core_here = jnp.arange(core) == lay.core_index
    bias_sums = jnp.sum(grad_qkv, axis=0).reshape(high, part_heads, fsdp, bias_width)
    bias_sums = jnp.transpose(bias_sums, (0, 2, 1, 3))[:, :, None]
    bias_sums = jnp.where(core_here[:, None, None], bias_sums, 0.0)
    bias_sums = pad_columns(bias_sums.reshape(high, fsdp, -1), shard_width)
    up_sums = jnp.sum(grad_inner, axis=0).reshape(high, 1, (fsdp // core) * hidden_part)
    up_sums = jnp.where(core_here[:, None], up_sums, 0.0)
    up_sums = pad_columns(up_sums.reshape(high, fsdp, hidden_part), shard_width)
    small_sums = jnp.pad(
        jnp.stack([bias_sums.reshape(high, -1), up_sums.reshape(high, -1)], axis=1),
        ((0, 0), (0, SMALL_ROWS - 2), (0, 0)),
    )
    down_shard = lay.scatter_weight(grad_down.reshape(high, -1, model_width))
    up_shard = lay.scatter_weight(grad_upward.reshape(high, -1, model_width)).T
    out_shard = lay.scatter_weight(grad_output.reshape(high, -1, model_width))
    attn_shard, small_shard = lay.scatter_weight(
        grad_attn_w.reshape(high, -1, model_width), small_sums
    )
    grads = (
        attn_shard.T,
        small_shard[0, : local_heads * bias_width].reshape(local_heads, bias_width),
        out_shard,
        up_shard,
        small_shard[1, :hidden_part],
        down_shard,
        norm_sums[0:2],
        norm_sums[2:6],
    )
    moments = (
        attn_weight_moments,
        attn_bias_moments,
        out_weight_moments,
        up_weight_moments,
        up_bias_moments,
        down_weight_moments,
        norm_gains_moments,
        norm_shifts_moments,
    )
    rates = (
        matrix_rate,
        vector_rate,
        output_rate,
        matrix_rate,
        vector_rate,
        matrix_rate,
        vector_rate,
        vector_rate,
    )
    decays = (decay_rate, 0.0, decay_rate, decay_rate, 0.0, decay_rate, 0.0, 0.0)
    updated = [
        adamw_update(weights[place], moments[place], grads[place], rates[place], decays[place])
        for place in range(8)
    ]
    new_weights = tuple((pair[0] for pair in updated))
    new_moments = tuple((pair[1] for pair in updated))
    return (outputs, input_grads) + grads + new_weights + new_moments


def solution(mesh):
    return jax.shard_map(
        per_device,
        mesh=mesh,
        in_specs=(
            P("fsdp", "tensor", None),
            P("fsdp", "tensor", None),
            P("fsdp", "tensor"),
            P("tensor", "fsdp"),
            P("tensor", "fsdp"),
            P("fsdp", "tensor"),
            P(("tensor", "fsdp")),
            P("tensor", "fsdp"),
            P(None, "fsdp"),
            P(None, "fsdp"),
            P(None, "fsdp", "tensor"),
            P(None, "tensor", "fsdp"),
            P(None, "tensor", "fsdp"),
            P(None, "fsdp", "tensor"),
            P(None, ("tensor", "fsdp")),
            P(None, "tensor", "fsdp"),
            P(None, None, "fsdp"),
            P(None, None, "fsdp"),
        ),
        out_specs=(
            P("fsdp", "tensor", None),
            P("fsdp", "tensor", None),
            P("fsdp", "tensor"),
            P("tensor", "fsdp"),
            P("tensor", "fsdp"),
            P("fsdp", "tensor"),
            P(("tensor", "fsdp")),
            P("tensor", "fsdp"),
            P(None, "fsdp"),
            P(None, "fsdp"),
            P("fsdp", "tensor"),
            P("tensor", "fsdp"),
            P("tensor", "fsdp"),
            P("fsdp", "tensor"),
            P(("tensor", "fsdp")),
            P("tensor", "fsdp"),
            P(None, "fsdp"),
            P(None, "fsdp"),
            P(None, "fsdp", "tensor"),
            P(None, "tensor", "fsdp"),
            P(None, "tensor", "fsdp"),
            P(None, "fsdp", "tensor"),
            P(None, ("tensor", "fsdp")),
            P(None, "tensor", "fsdp"),
            P(None, None, "fsdp"),
            P(None, None, "fsdp"),
        ),
        check_vma=False,
    )
```

time: 1480 us -> 538 us (0.36)
  waiting for transfers between devices: 1170 us -> 207 us
  starting transfers between devices: 1.18 us -> 106 us
  blocking collectives: 95.7 us -> 0 us
  local copies, waits for them, and re-layouts: 30.9 us -> 51.8 us
    reduce_scatter x12 -> x0, waiting for transfers between devices: 743 us -> none  [the longest x2 177 us: micro_step(): lax.psum_scatter(jnp.dot(active, w_downward, preferred_element_type=jnp.f...]
    all_gather x12 -> x0, waiting for transfers between devices: 363 us -> none  [the longest x2 96.7 us: micro_step(): grad_full = lax.all_gather(grad_two_b, 'tensor', axis=0, tiled=True)]
    ppermute x0 -> x75, waiting for transfers between devices: none -> 207 us  [send(): return lax.ppermute(value, AXES, pairs)]
    ppermute x0 -> x75, starting transfers between devices: none -> 106 us  [send(): return lax.ppermute(value, AXES, pairs)]
    all_gather x12 -> x0, blocking collectives: 74.8 us -> none  [the longest x2 17.4 us: fetch_params(): lax.all_gather(pieces[0], 'fsdp', axis=0, tiled=True)]
    unnamed x10 -> x0, waiting for transfers between devices: 56.4 us -> none
    psum x1 -> x0, blocking collectives: 15.1 us -> none  [per_device(): gain_grad, shift_grad = lax.psum((shards[6], shards[7]), 'tensor')]
    dot_general x24 -> x12, matrix products: 82.2 us -> 70.5 us  [the longest x4 31.5 us: times(): return jnp.dot(left, right, preferred_element_type=wide)]
  transfers between devices with their start and end apart: 27 -> 75, of which waited for: 25 -> 36; matrix products, arithmetic and copies ran while one was open for 4% -> 23% of each run, Pallas kernels for 0% -> 0%
where the time goes in v1:
time: 538 us; the launch traced here: 528 us
  waiting for transfers between devices  207 us (38%)
  starting transfers between devices  106 us (20%)
  matrix products  95.9 us (18%)
  other arithmetic  61.5 us (11%)
  local copies, waits for them, and re-layouts  51.8 us (10%)
    ppermute x75, waiting for transfers between devices, send(): return lax.ppermute(value, AXES, pairs)  207 us
    ppermute x75, starting transfers between devices, send(): return lax.ppermute(value, AXES, pairs)  106 us
    dot_general x4, matrix products, times(): return jnp.dot(left, right, preferred_element_type=wide)  31.5 us
    dot_general x4, matrix products, times_t(): lax.dot_general(left, right, (((1,), (1,)), ((), ())), preferred_element_...  24.6 us
    unnamed x169, local copies, waits for them, and re-layouts  19.3 us
    dot_general x4, matrix products, t_times(): lax.dot_general(left, right, (((0,), (0,)), ((), ())), preferred_element_...  14.4 us
    another operation x16, other arithmetic, adamw_update(): jnp.stack([first_moment, second_moment])  11.9 us
  transfers between devices with their start and end apart: 75, of which 36 were waited for; matrix products, arithmetic and copies ran while one was open for 23% of the time, Pallas kernels for 0%

profile of v1, /device:TPU:13, one launch (start us, length us, event | category | flops | bytes accessed | tf_op | source)
XLA Modules:
  0.0 528.0 jit_solution(10289809691025043637)
XLA Ops:
  8.7 4.5 collective-permute-start
  13.8 3.2 collective-permute-start.12
  17.1 28.7 %collective-permute-done.13 = bf16[64,512]{1,0:T(8,128)(2,1)S(1)} collective-permute-done((bf16[64,512]{1,0:T(8,128)(2,1)S(1)}, bf16[64,512]{1,0:T(8,128)(2,1)S(1)}, u32[]{:S(2)}, u32[]{:S(2)}) %collective-permute-start.13) | collective-permute-done | bytes 65568 | tf_op jit(solution)/shard_map/ppermute | solution.py:167
  50.8 8.8 %collective-permute-done.8 = bf16[208,512]{1,0:T(8,128)(2,1)S(1)} collective-permute-done((bf16[208,512]{1,0:T(8,128)(2,1)S(1)}, bf16[208,512]{1,0:T(8,128)(2,1)S(1)}, u32[]{:S(2)}, u32[]{:S(2)}) %collective-permute-start.8) | collective-permute-done | bytes 213024 | tf_op jit(solution)/shard_map/ppermute | solution.py:167
  59.7 2.3 collective-permute-done.7
  68.3 2.2 collective-permute-start.23
  70.5 9.8 %collective-permute-done.3 = bf16[256,1024]{1,0:T(8,128)(2,1)S(1)} collective-permute-done((bf16[256,1024]{1,0:T(8,128)(2,1)S(1)}, bf16[256,1024]{1,0:T(8,128)(2,1)S(1)}, u32[]{:S(2)}, u32[]{:S(2)}) %collective-permute-start.3) | collective-permute-done | bytes 524320 | tf_op jit(solution)/shard_map/ppermute | solution.py:167
  80.5 6.6 %collective-permute-done.9 = bf16[832,512]{1,0:T(8,128)(2,1)S(1)} collective-permute-done((bf16[832,512]{1,0:T(8,128)(2,1)S(1)}, bf16[832,512]{1,0:T(8,128)(2,1)S(1)}, u32[]{:S(2)}, u32[]{:S(2)}) %collective-permute-start.9) | collective-permute-done | bytes 852000 | tf_op jit(solution)/shard_map/ppermute | solution.py:167
  90.8 3.9 add_convert_fusion
  95.4 15.7 %while.27 = (s32[]{:T(128)}, bf16[2,4,512,64]{2,3,1,0:T(8,128)(2,1)}, f32[2,4,512]{2,1,0:T(4,128)S(1)}, s32[2]{0:T(128)}, bf16[4,1024,64]{1,2,0:T(8,128)(2,1)S(1...) while((s32[]{:T(128)}, ...), condition=%wide.region_3.4_spmd, body=%wide.region_0.3_spmd.sunk | while | flops 553777152 | bytes 30998772 | solution.py:77
  112.4 2.1 fusion.164
  115.3 2.2 pad_maximum_fusion.3
  119.7 12.0 %collective-permute-done.17 = bf16[256,1024]{1,0:T(8,128)(2,1)S(1)} collective-permute-done((bf16[256,1024]{1,0:T(8,128)(2,1)S(1)}, bf16[256,1024]{1,0:T(8,128)(2,1)S(1)}, u32[]{:S(2)}, u32[]{:S(2)}) %collective-permute-start.17) | collective-permute-done | bytes 524320 | tf_op jit(solution)/shard_map/ppermute | solution.py:167
  140.3 4.5 collective-permute-done.29
  144.8 12.5 %collective-permute-start.18 = (bf16[256,1024]{1,0:T(8,128)(2,1)}, bf16[256,1024]{1,0:T(8,128)(2,1)}, u32[]{:S(2)}, u32[]{:S(2)}) collective-permute-start(bf16[256,1024]{1,0:T(8,128)(2,1)} %fusion.70), channel_id=1, source_target_pairs={{0,8},{1,9},{2,10},{3,11},{4,12},{5,13},{6,14},{7,15},{8,0},{9,1},... | collective-permute-start | bytes 1572872 | tf_op jit(solution)/shard_map/ppermute | solution.py:167
  157.4 3.6 collective-permute-done.28
  163.3 7.5 %multiply_convert_fusion.1 = (bf16[1024,1024]{1,0:T(8,128)(2,1)S(1)}, f32[1024,1024]{1,0:T(8,128)}) fusion(f32[1024]{0:T(1024)S(1)} %bitcast.393, bf16[1024,512]{1,0:T(8,128)(2,1)} %collective-permute-done.25, bf16[256,512]{1,0:T(8,128)(2,1)} %collective-permute-done.24, bf16[256,512]{1,0:T(8,128)(2,1)} %collective-permute-done.23, ...), kind=kOutput, calls=%fused_computation.46 | convolution fusion | flops 2184183808 | bytes 10489857 | tf_op jit(solution)/shard_map/dot_general | solution.py:419
  170.8 15.4 %collective-permute-done.30 = bf16[1024,512]{1,0:T(8,128)(2,1)} collective-permute-done((bf16[1024,512]{1,0:T(8,128)(2,1)S(1)}, bf16[1024,512]{1,0:T(8,128)(2,1)}, u32[]{:S(2)}, u32[]{:S(2)}) %collective-permute-start.30) | collective-permute-done | bytes 1048608 | tf_op jit(solution)/shard_map/ppermute | solution.py:167
  186.2 11.4 %fusion.165 = (bf16[1024,1024]{1,0:T(8,128)(2,1)S(1)}, f32[1024,1024]{1,0:T(8,128)S(1)}) fusion(bf16[1024,1024]{1,0:T(8,128)(2,1)S(1)} %get-tuple-element.393, bf16[1024,512]{1,0:T(8,128)(2,1)} %collective-permute-done.30, bf16[256,512]{1,0:T(8,128)(2,1)S(1)} %copy-done.51, bf16[256,512]{1,0:T(8,128)(2,1)S(1)} %copy-done.53, ...), kind=kOutput, calls=%fused_computation.353 | convolution fusion | flops 2170552320 | bytes 10485761 | tf_op jit(solution)/shard_map/dot_general | solution.py:416
  201.4 12.6 %collective-permute-done.33 = bf16[256,1024]{1,0:T(8,128)(2,1)S(1)} collective-permute-done((bf16[256,1024]{1,0:T(8,128)(2,1)S(1)}, bf16[256,1024]{1,0:T(8,128)(2,1)S(1)}, u32[]{:S(2)}, u32[]{:S(2)}) %collective-permute-start.33) | collective-permute-done | bytes 524320 | tf_op jit(solution)/shard_map/ppermute | solution.py:167
  227.5 4.7 collective-permute-done.37
  236.1 4.1 collective-permute-start.34
  240.3 2.2 fusion.158
  246.7 4.1 collective-permute-done.35
  252.9 10.0 %fusion.168 = (f32[1024]{0:T(1024)S(1)}, bf16[1024,1024]{1,0:T(8,128)(2,1)}) fusion(f32[1024,1024]{1,0:T(8,128)} %get-tuple-element.394, f32[1024]{0:T(1024)S(1)} %bitcast.394, bf16[1024,512]{1,0:T(8,128)(2,1)} %collective-permute-done.30, bf16[256,512]{1,0:T(8,128)(2,1)} %copy-done.50, bf16[256,512]{1,0:T(8,128)(2,1)} %copy-done.52, ...), kind=kOutput, calls=%fused_computation.356 | convolution fusion | flops 2190474240 | bytes 10493953 | tf_op jit(solution)/shard_map/dot_general | solution.py:419
  263.0 16.1 %fusion.166 = (bf16[1024,1024]{1,0:T(8,128)(2,1)S(1)}, f32[1024,1024]{1,0:T(8,128)S(1)}) fusion(bf16[1024,512]{1,0:T(8,128)(2,1)} %collective-permute-done.25, bf16[256,512]{1,0:T(8,128)(2,1)} %collective-permute-done.24, bf16[256,512]{1,0:T(8,128)(2,1)} %collective-permute-done.23, bf16[256,512]{1,0:T(8,128)(2,1)} %collective-permute-done.22, ...), kind=kOutput, calls=%fused_computation.354 | convolution fusion | flops 2170552320 | bytes 10485761 | tf_op jit(solution)/shard_map/dot_general | solution.py:416
  279.2 4.0 fusion.97
  286.9 4.1 fusion.66
  293.1 7.2 %collective-permute-done.41 = bf16[256,1024]{1,0:T(8,128)(2,1)S(1)} collective-permute-done((bf16[256,1024]{1,0:T(8,128)(2,1)S(1)}, bf16[256,1024]{1,0:T(8,128)(2,1)S(1)}, u32[]{:S(2)}, u32[]{:S(2)}) %collective-permute-start.41) | collective-permute-done | bytes 524320 | tf_op jit(solution)/shard_map/ppermute | solution.py:167
  308.9 2.3 fusion.144
  311.2 8.7 %collective-permute-done.71 = f32[6,1024]{1,0:T(8,128)S(1)} collective-permute-done((f32[6,1024]{1,0:T(8,128)S(1)}, f32[6,1024]{1,0:T(8,128)S(1)}, u32[]{:S(2)}, u32[]{:S(2)}) %collective-permute-start.71) | collective-permute-done | bytes 24608 | tf_op jit(solution)/shard_map/ppermute | solution.py:167
  320.6 10.8 %collective-permute-done.60 = bf16[4,256,512]{2,1,0:T(8,128)(2,1)} collective-permute-done((bf16[4,256,512]{2,1,0:T(8,128)(2,1)}, bf16[4,256,512]{2,1,0:T(8,128)(2,1)}, u32[]{:S(2)}, u32[]{:S(2)}) %collective-permute-start.60) | collective-permute-done | bytes 1048608 | tf_op jit(solution)/shard_map/ppermute | solution.py:167
  335.9 2.2 collective-permute-start.74
  343.8 2.3 collective-permute-start.66
  346.1 4.5 collective-permute-done.63
  350.8 7.8 %collective-permute-done.62 = bf16[256,512]{1,0:T(8,128)(2,1)S(1)} collective-permute-done((bf16[256,512]{1,0:T(8,128)(2,1)S(1)}, bf16[256,512]{1,0:T(8,128)(2,1)S(1)}, u32[]{:S(2)}, u32[]{:S(2)}) %collective-permute-start.62) | collective-permute-done | bytes 262176 | tf_op jit(solution)/shard_map/ppermute | solution.py:167
  358.6 3.3 collective-permute-start.67
  362.1 11.7 %collective-permute-done.66 = bf16[256,512]{1,0:T(8,128)(2,1)S(1)} collective-permute-done((bf16[256,512]{1,0:T(8,128)(2,1)S(1)}, bf16[256,512]{1,0:T(8,128)(2,1)S(1)}, u32[]{:S(2)}, u32[]{:S(2)}) %collective-permute-start.66) | collective-permute-done | bytes 262176 | tf_op jit(solution)/shard_map/ppermute | solution.py:167
  373.8 8.9 %collective-permute-start.64 = (f32[256,256]{1,0:T(8,128)S(1)}, f32[256,256]{1,0:T(8,128)S(1)}, u32[]{:S(2)}, u32[]{:S(2)}) collective-permute-start(f32[256,256]{1,0:T(8,128)S(1)} %get-tuple-element.352), channel_id=1, source_target_pairs={{0,8},{1,9},{2,10},{3,11},{4,12},{5,13},{6,14},{7,15},{8,0},{9,1},... | collective-permute-start | bytes 786440 | tf_op jit(solution)/shard_map/ppermute | solution.py:167
  383.5 2.8 collective-permute-start.69
  390.1 2.6 multiply_add_fusion.1
  392.6 2.7 fusion.100
  396.4 2.5 copy.112
  401.0 2.3 pad_maximum_fusion.6
  403.3 2.9 multiply_subtract_fusion
  406.2 3.2 convolution_convert_fusion
  409.4 28.2 %while.28 = (s32[]{:T(128)}, f32[4,1024,64]{1,2,0:T(8,128)S(1)}, f32[4,1024,64]{1,2,0:T(8,128)S(1)}, f32[2,4,512,64]{2,3,1,0:T(8,128)}, s32[2]{0:T(128)S(1)}, /*...) while((s32[]{:T(128)}, f32[4,1024,64]{1,2,0:T(8,128)S(1)}, ...), condition=%wide.region_14.15_spmd.clone, body=%wide.region_12.14_spmd.clone.sunk | while | flops 1368782848 | bytes 82895200 | solution.py:123
  410.9 2.3 fusion.214
  415.1 2.9 multiply_reduce_fusion.10
  424.9 2.3 fusion.214
  429.1 2.9 multiply_reduce_fusion.10
  437.7 3.0 copy.96
  443.7 2.8 fusion.37
  447.9 3.5 fusion.39
  455.3 2.2 collective-permute-start.58
  462.7 2.6 collective-permute-start.59
  468.7 4.4 collective-permute-done.50
  478.7 3.1 collective-permute-done.47
  484.0 8.3 %collective-permute-done.52 = bf16[208,512]{1,0:T(8,128)(2,1)S(1)} collective-permute-done((bf16[208,512]{1,0:T(8,128)(2,1)S(1)}, bf16[208,512]{1,0:T(8,128)(2,1)S(1)}, u32[]{:S(2)}, u32[]{:S(2)}) %collective-permute-start.52) | collective-permute-done | bytes 213024 | tf_op jit(solution)/shard_map/ppermute | solution.py:167
  495.4 4.6 collective-permute-start.48
  500.0 2.7 collective-permute-start.49
  508.7 4.0 collective-permute-done.48
  512.7 12.6 %collective-permute-done.49 = f32[128,1024]{1,0:T(8,128)} collective-permute-done((f32[128,1024]{1,0:T(8,128)}, f32[128,1024]{1,0:T(8,128)}, u32[]{:S(2)}, u32[]{:S(2)}) %collective-permute-start.49) | collective-permute-done | bytes 524320 | tf_op jit(solution)/shard_map/ppermute | solution.py:167
  525.3 2.3 maximum_select_fusion.3
  (491 shorter events, 163.9 us)
Async XLA Ops:
  1.7 12.0 %collective-permute-start.10 = (bf16[64,256]{1,0:T(8,128)(2,1)S(1)}, bf16[64,256]{1,0:T(8,128)(2,1)S(1)}, u32[]{:S(2)}, u32[]{:S(2)}) collective-permute-start(bf16[64,256]{1,0:T(8,128)(2,1)S(1)} %get-tuple-element.374), channel_id=1, source_target_pairs={{0,8},{1,9},{2,10},{3,11},{4,12},{5,13},{6,14},{7,15},{8,0},{9,1},... | collective-permute-start | bytes 98312 | tf_op jit(solution)/shard_map/ppermute | solution.py:167
  6.5 10.5 %collective-permute-start.5 = (bf16[208,256]{1,0:T(8,128)(2,1)S(1)}, bf16[208,256]{1,0:T(8,128)(2,1)S(1)}, u32[]{:S(2)}, u32[]{:S(2)}) collective-permute-start(bf16[208,256]{1,0:T(8,128)(2,1)S(1)} %concatenate.184), channel_id=1, source_target_pairs={{0,8},{1,9},{2,10},{3,11},{4,12},{5,13},{6,14},{7,15},{8,0},{9,1},... | collective-permute-start | bytes 319496 | tf_op jit(solution)/shard_map/ppermute | solution.py:167
  8.7 55.7 %collective-permute-start = (bf16[2,128,1024]{2,1,0:T(8,128)(2,1)}, bf16[2,128,1024]{2,1,0:T(8,128)(2,1)S(1)}, u32[]{:S(2)}, u32[]{:S(2)}) collective-permute-start(bf16[2,128,1024]{2,1,0:T(8,128)(2,1)} %get-tuple-element.341), channel_id=1, source_target_pairs={{0,0},{1,1},{2,2},{3,3},{4,8},{5,9},{6,10},{7,11},{8,4},{9,5},{10,... | collective-permute-start | bytes 1572872 | tf_op jit(solution)/shard_map/ppermute | solution.py:167
  13.3 51.3 %collective-permute-start.1 = (bf16[2,128,1024]{2,1,0:T(8,128)(2,1)S(1)}, bf16[2,128,1024]{2,1,0:T(8,128)(2,1)S(1)}, u32[]{:S(2)}, u32[]{:S(2)}) collective-permute-start(bf16[2,128,1024]{2,1,0:T(8,128)(2,1)S(1)} %get-tuple-element.342), channel_id=1, source_target_pairs={{0,2},{1,3},{2,0},{3,1},{4,10},{5,11},{6,8},{7,9},{8,6},{9,7},{10,... | collective-permute-start | bytes 1572872 | tf_op jit(solution)/shard_map/ppermute | solution.py:167
  13.7 32.1 %collective-permute-start.13 = (bf16[64,512]{1,0:T(8,128)(2,1)S(1)}, bf16[64,512]{1,0:T(8,128)(2,1)S(1)}, u32[]{:S(2)}, u32[]{:S(2)}) collective-permute-start(bf16[64,512]{1,0:T(8,128)(2,1)S(1)} %maximum_select_fusion.15), channel_id=1, source_target_pairs={{0,2},{1,3},{2,4},{3,5},{4,6},{5,7},{6,0},{7,1},{8,10},{9,11},{10,... | collective-permute-start | bytes 196616 | tf_op jit(solution)/shard_map/ppermute | solution.py:167
  13.8 34.0 %collective-permute-start.12 = (bf16[64,512]{1,0:T(8,128)(2,1)S(1)}, bf16[64,512]{1,0:T(8,128)(2,1)S(1)}, u32[]{:S(2)}, u32[]{:S(2)}) collective-permute-start(bf16[64,512]{1,0:T(8,128)(2,1)S(1)} %maximum_select_fusion.15), channel_id=1, source_target_pairs={{0,4},{1,5},{2,6},{3,7},{4,0},{5,1},{6,2},{7,3},{8,12},{9,13},{10,... | collective-permute-start | bytes 196616 | tf_op jit(solution)/shard_map/ppermute | solution.py:167
  17.0 32.3 %collective-permute-start.11 = (bf16[64,512]{1,0:T(8,128)(2,1)S(1)}, bf16[64,512]{1,0:T(8,128)(2,1)S(1)}, u32[]{:S(2)}, u32[]{:S(2)}) collective-permute-start(bf16[64,512]{1,0:T(8,128)(2,1)S(1)} %maximum_select_fusion.15), channel_id=1, source_target_pairs={{0,6},{1,7},{2,0},{3,1},{4,2},{5,3},{6,4},{7,5},{8,14},{9,15},{10,... | collective-permute-start | bytes 196616 | tf_op jit(solution)/shard_map/ppermute | solution.py:167
  45.9 13.8 %collective-permute-start.8 = (bf16[208,512]{1,0:T(8,128)(2,1)S(1)}, bf16[208,512]{1,0:T(8,128)(2,1)S(1)}, u32[]{:S(2)}, u32[]{:S(2)}) collective-permute-start(bf16[208,512]{1,0:T(8,128)(2,1)S(1)} %maximum_select_fusion.12), channel_id=1, source_target_pairs={{0,2},{1,3},{2,4},{3,5},{4,6},{5,7},{6,0},{7,1},{8,10},{9,11},{10,... | collective-permute-start | bytes 638984 | tf_op jit(solution)/shard_map/ppermute | solution.py:167
  47.8 14.2 %collective-permute-start.7 = (bf16[208,512]{1,0:T(8,128)(2,1)S(1)}, bf16[208,512]{1,0:T(8,128)(2,1)S(1)}, u32[]{:S(2)}, u32[]{:S(2)}) collective-permute-start(bf16[208,512]{1,0:T(8,128)(2,1)S(1)} %maximum_select_fusion.12), channel_id=1, source_target_pairs={{0,4},{1,5},{2,6},{3,7},{4,0},{5,1},{6,2},{7,3},{8,12},{9,13},{10,... | collective-permute-start | bytes 638984 | tf_op jit(solution)/shard_map/ppermute | solution.py:167
  49.4 12.8 %collective-permute-start.6 = (bf16[208,512]{1,0:T(8,128)(2,1)S(1)}, bf16[208,512]{1,0:T(8,128)(2,1)}, u32[]{:S(2)}, u32[]{:S(2)}) collective-permute-start(bf16[208,512]{1,0:T(8,128)(2,1)S(1)} %maximum_select_fusion.12), channel_id=1, source_target_pairs={{0,6},{1,7},{2,0},{3,1},{4,2},{5,3},{6,4},{7,5},{8,14},{9,15},{10,... | collective-permute-start | bytes 638984 | tf_op jit(solution)/shard_map/ppermute | solution.py:167
  59.7 5.8 %collective-permute-start.21 = (bf16[256,256]{1,0:T(8,128)(2,1)}, bf16[256,256]{1,0:T(8,128)(2,1)S(1)}, u32[]{:S(2)}, u32[]{:S(2)}) collective-permute-start(bf16[256,256]{1,0:T(8,128)(2,1)} %get-tuple-element.368), channel_id=1, source_target_pairs={{0,8},{1,9},{2,10},{3,11},{4,12},{5,13},{6,14},{7,15},{8,0},{9,1},... | collective-permute-start | bytes 393224 | tf_op jit(solution)/shard_map/ppermute | solution.py:167
  62.0 50.5 %collective-permute-start.14 = (bf16[256,512]{1,0:T(8,128)(2,1)}, bf16[256,512]{1,0:T(8,128)(2,1)}, u32[]{:S(2)}, u32[]{:S(2)}) collective-permute-start(bf16[256,512]{1,0:T(8,128)(2,1)} %pad_maximum_fusion.17), channel_id=1, source_target_pairs={{0,16},{1,17},{2,18},{3,19},{4,20},{5,21},{6,22},{7,23},{8,24},{9,... | collective-permute-start | bytes 786440 | tf_op jit(solution)/shard_map/ppermute | solution.py:167
  63.2 24.0 %collective-permute-start.9 = (bf16[832,512]{1,0:T(8,128)(2,1)S(1)}, bf16[832,512]{1,0:T(8,128)(2,1)S(1)}, u32[]{:S(2)}, u32[]{:S(2)}) collective-permute-start(bf16[832,512]{1,0:T(8,128)(2,1)S(1)} %pad_maximum_fusion.7), channel_id=1, source_target_pairs={{0,16},{1,17},{2,18},{3,19},{4,20},{5,21},{6,22},{7,23},{8,24},{9,... | collective-permute-start | bytes 2555912 | tf_op jit(solution)/shard_map/ppermute | solution.py:167
  66.3 49.0 %collective-permute-start.24 = (bf16[256,512]{1,0:T(8,128)(2,1)}, bf16[256,512]{1,0:T(8,128)(2,1)}, u32[]{:S(2)}, u32[]{:S(2)}) collective-permute-start(bf16[256,512]{1,0:T(8,128)(2,1)} %maximum_select_fusion.10), channel_id=1, source_target_pairs={{0,2},{1,3},{2,4},{3,5},{4,6},{5,7},{6,0},{7,1},{8,10},{9,11},{10,... | collective-permute-start | bytes 786440 | tf_op jit(solution)/shard_map/ppermute | solution.py:167
  67.0 13.3 %collective-permute-start.3 = (bf16[256,1024]{1,0:T(8,128)(2,1)S(1)}, bf16[256,1024]{1,0:T(8,128)(2,1)S(1)}, u32[]{:S(2)}, u32[]{:S(2)}) collective-permute-start(bf16[256,1024]{1,0:T(8,128)(2,1)S(1)} %pad_maximum_fusion.9), channel_id=1, source_target_pairs={{0,1},{1,0},{2,3},{3,2},{4,5},{5,4},{6,7},{7,6},{8,9},{9,8},{10,11... | collective-permute-start | bytes 1572872 | tf_op jit(solution)/shard_map/ppermute | solution.py:167
  68.3 47.1 %collective-permute-start.23 = (bf16[256,512]{1,0:T(8,128)(2,1)}, bf16[256,512]{1,0:T(8,128)(2,1)}, u32[]{:S(2)}, u32[]{:S(2)}) collective-permute-start(bf16[256,512]{1,0:T(8,128)(2,1)} %maximum_select_fusion.10), channel_id=1, source_target_pairs={{0,4},{1,5},{2,6},{3,7},{4,0},{5,1},{6,2},{7,3},{8,12},{9,13},{10,... | collective-permute-start | bytes 786440 | tf_op jit(solution)/shard_map/ppermute | solution.py:167
  80.3 35.0 %collective-permute-start.22 = (bf16[256,512]{1,0:T(8,128)(2,1)}, bf16[256,512]{1,0:T(8,128)(2,1)}, u32[]{:S(2)}, u32[]{:S(2)}) collective-permute-start(bf16[256,512]{1,0:T(8,128)(2,1)} %maximum_select_fusion.10), channel_id=1, source_target_pairs={{0,6},{1,7},{2,0},{3,1},{4,2},{5,3},{6,4},{7,5},{8,14},{9,15},{10,... | collective-permute-start | bytes 786440 | tf_op jit(solution)/shard_map/ppermute | solution.py:167
  117.6 45.7 %collective-permute-start.25 = (bf16[1024,512]{1,0:T(8,128)(2,1)}, bf16[1024,512]{1,0:T(8,128)(2,1)}, u32[]{:S(2)}, u32[]{:S(2)}) collective-permute-start(bf16[1024,512]{1,0:T(8,128)(2,1)} %pad_maximum_fusion.3), channel_id=1, source_target_pairs={{0,16},{1,17},{2,18},{3,19},{4,20},{5,21},{6,22},{7,23},{8,24},{9,... | collective-permute-start | bytes 3145736 | tf_op jit(solution)/shard_map/ppermute | solution.py:167
  118.3 13.5 %collective-permute-start.17 = (bf16[256,1024]{1,0:T(8,128)(2,1)S(1)}, bf16[256,1024]{1,0:T(8,128)(2,1)S(1)}, u32[]{:S(2)}, u32[]{:S(2)}) collective-permute-start(bf16[256,1024]{1,0:T(8,128)(2,1)S(1)} %fusion.62), channel_id=1, source_target_pairs={{0,1},{1,0},{2,3},{3,2},{4,5},{5,4},{6,7},{7,6},{8,9},{9,8},{10,11... | collective-permute-start | bytes 1572872 | tf_op jit(solution)/shard_map/ppermute | solution.py:167
  133.5 23.8 %collective-permute-start.19 = (bf16[256,1024]{1,0:T(8,128)(2,1)}, bf16[256,1024]{1,0:T(8,128)(2,1)}, u32[]{:S(2)}, u32[]{:S(2)}) collective-permute-start(bf16[256,1024]{1,0:T(8,128)(2,1)} %fusion.70), channel_id=1, source_target_pairs={{0,1},{1,0},{2,3},{3,2},{4,5},{5,4},{6,7},{7,6},{8,9},{9,8},{10,11... | collective-permute-start | bytes 1572872 | tf_op jit(solution)/shard_map/ppermute | solution.py:167
  137.1 7.7 %collective-permute-start.29 = (bf16[256,512]{1,0:T(8,128)(2,1)S(1)}, bf16[256,512]{1,0:T(8,128)(2,1)S(1)}, u32[]{:S(2)}, u32[]{:S(2)}) collective-permute-start(bf16[256,512]{1,0:T(8,128)(2,1)S(1)} %maximum_select_fusion.11), channel_id=1, source_target_pairs={{0,2},{1,3},{2,4},{3,5},{4,6},{5,7},{6,0},{7,1},{8,10},{9,11},{10,... | collective-permute-start | bytes 786440 | tf_op jit(solution)/shard_map/ppermute | solution.py:167
  138.8 22.2 %collective-permute-start.28 = (bf16[256,512]{1,0:T(8,128)(2,1)S(1)}, bf16[256,512]{1,0:T(8,128)(2,1)S(1)}, u32[]{:S(2)}, u32[]{:S(2)}) collective-permute-start(bf16[256,512]{1,0:T(8,128)(2,1)S(1)} %maximum_select_fusion.11), channel_id=1, source_target_pairs={{0,4},{1,5},{2,6},{3,7},{4,0},{5,1},{6,2},{7,3},{8,12},{9,13},{10,... | collective-permute-start | bytes 786440 | tf_op jit(solution)/shard_map/ppermute | solution.py:167
  138.8 23.0 %collective-permute-start.27 = (bf16[256,512]{1,0:T(8,128)(2,1)S(1)}, bf16[256,512]{1,0:T(8,128)(2,1)S(1)}, u32[]{:S(2)}, u32[]{:S(2)}) collective-permute-start(bf16[256,512]{1,0:T(8,128)(2,1)S(1)} %maximum_select_fusion.11), channel_id=1, source_target_pairs={{0,6},{1,7},{2,0},{3,1},{4,2},{5,3},{6,4},{7,5},{8,14},{9,15},{10,... | collective-permute-start | bytes 786440 | tf_op jit(solution)/shard_map/ppermute | solution.py:167
  144.8 18.5 %collective-permute-start.18 = (bf16[256,1024]{1,0:T(8,128)(2,1)}, bf16[256,1024]{1,0:T(8,128)(2,1)}, u32[]{:S(2)}, u32[]{:S(2)}) collective-permute-start(bf16[256,1024]{1,0:T(8,128)(2,1)} %fusion.70), channel_id=1, source_target_pairs={{0,8},{1,9},{2,10},{3,11},{4,12},{5,13},{6,14},{7,15},{8,0},{9,1},... | collective-permute-start | bytes 1572872 | tf_op jit(solution)/shard_map/ppermute | solution.py:167
  157.3 5.9 %collective-permute-start.20 = (bf16[256,1024]{1,0:T(8,128)(2,1)}, bf16[256,1024]{1,0:T(8,128)(2,1)}, u32[]{:S(2)}, u32[]{:S(2)}) collective-permute-start(bf16[256,1024]{1,0:T(8,128)(2,1)} %collective-permute-done.19), channel_id=1, source_target_pairs={{0,8},{1,9},{2,10},{3,11},{4,12},{5,13},{6,14},{7,15},{8,0},{9,1},... | collective-permute-start | bytes 1572872 | tf_op jit(solution)/shard_map/ppermute | solution.py:167
  161.8 24.4 %collective-permute-start.30 = (bf16[1024,512]{1,0:T(8,128)(2,1)S(1)}, bf16[1024,512]{1,0:T(8,128)(2,1)}, u32[]{:S(2)}, u32[]{:S(2)}) collective-permute-start(bf16[1024,512]{1,0:T(8,128)(2,1)S(1)} %pad_maximum_fusion.4), channel_id=1, source_target_pairs={{0,16},{1,17},{2,18},{3,19},{4,20},{5,21},{6,22},{7,23},{8,24},{9,... | collective-permute-start | bytes 3145736 | tf_op jit(solution)/shard_map/ppermute | solution.py:167
  200.8 13.2 %collective-permute-start.33 = (bf16[256,1024]{1,0:T(8,128)(2,1)S(1)}, bf16[256,1024]{1,0:T(8,128)(2,1)S(1)}, u32[]{:S(2)}, u32[]{:S(2)}) collective-permute-start(bf16[256,1024]{1,0:T(8,128)(2,1)S(1)} %fusion.58), channel_id=1, source_target_pairs={{0,1},{1,0},{2,3},{3,2},{4,5},{5,4},{6,7},{7,6},{8,9},{9,8},{10,11... | collective-permute-start | bytes 1572872 | tf_op jit(solution)/shard_map/ppermute | solution.py:167
  219.6 12.5 %collective-permute-start.37 = (bf16[256,1024]{1,0:T(8,128)(2,1)}, bf16[256,1024]{1,0:T(8,128)(2,1)}, u32[]{:S(2)}, u32[]{:S(2)}) collective-permute-start(bf16[256,1024]{1,0:T(8,128)(2,1)} %convert_element_type.303), channel_id=1, source_target_pairs={{0,1},{1,0},{2,3},{3,2},{4,5},{5,4},{6,7},{7,6},{8,9},{9,8},{10,11... | collective-permute-start | bytes 1572872 | tf_op jit(solution)/shard_map/ppermute | solution.py:167
  226.0 26.9 %collective-permute-start.36 = (bf16[256,1024]{1,0:T(8,128)(2,1)}, bf16[256,1024]{1,0:T(8,128)(2,1)}, u32[]{:S(2)}, u32[]{:S(2)}) collective-permute-start(bf16[256,1024]{1,0:T(8,128)(2,1)} %convert_element_type.303), channel_id=1, source_target_pairs={{0,8},{1,9},{2,10},{3,11},{4,12},{5,13},{6,14},{7,15},{8,0},{9,1},... | collective-permute-start | bytes 1572872 | tf_op jit(solution)/shard_map/ppermute | solution.py:167
  232.2 20.7 %collective-permute-start.38 = (bf16[256,1024]{1,0:T(8,128)(2,1)}, bf16[256,1024]{1,0:T(8,128)(2,1)}, u32[]{:S(2)}, u32[]{:S(2)}) collective-permute-start(bf16[256,1024]{1,0:T(8,128)(2,1)} %collective-permute-done.37), channel_id=1, source_target_pairs={{0,8},{1,9},{2,10},{3,11},{4,12},{5,13},{6,14},{7,15},{8,0},{9,1},... | collective-permute-start | bytes 1572872 | tf_op jit(solution)/shard_map/ppermute | solution.py:167
  236.1 10.6 %collective-permute-start.34 = (bf16[128,1024]{1,0:T(8,128)(2,1)}, bf16[128,1024]{1,0:T(8,128)(2,1)}, u32[]{:S(2)}, u32[]{:S(2)}) collective-permute-start(bf16[128,1024]{1,0:T(8,128)(2,1)} %get-tuple-element.358), channel_id=1, source_target_pairs={{0,0},{1,1},{2,2},{3,3},{4,8},{5,9},{6,10},{7,11},{8,4},{9,5},{10,... | collective-permute-start | bytes 786440 | tf_op jit(solution)/shard_map/ppermute | solution.py:167
  240.3 10.5 %collective-permute-start.35 = (bf16[128,1024]{1,0:T(8,128)(2,1)}, bf16[128,1024]{1,0:T(8,128)(2,1)}, u32[]{:S(2)}, u32[]{:S(2)}) collective-permute-start(bf16[128,1024]{1,0:T(8,128)(2,1)} %get-tuple-element.359), channel_id=1, source_target_pairs={{0,2},{1,3},{2,0},{3,1},{4,10},{5,11},{6,8},{7,9},{8,6},{9,7},{10,... | collective-permute-start | bytes 786440 | tf_op jit(solution)/shard_map/ppermute | solution.py:167
  279.1 7.3 %collective-permute-start.40 = (bf16[256,1024]{1,0:T(8,128)(2,1)S(1)}, bf16[256,1024]{1,0:T(8,128)(2,1)S(1)}, u32[]{:S(2)}, u32[]{:S(2)}) collective-permute-start(bf16[256,1024]{1,0:T(8,128)(2,1)S(1)} %get-tuple-element.318), channel_id=1, source_target_pairs={{0,8},{1,9},{2,10},{3,11},{4,12},{5,13},{6,14},{7,15},{8,0},{9,1},... | collective-permute-start | bytes 1572872 | tf_op jit(solution)/shard_map/ppermute | solution.py:167
  284.4 24.6 %collective-permute-start.65 = (bf16[4,256,512]{2,1,0:T(8,128)(2,1)}, bf16[4,256,512]{2,1,0:T(8,128)(2,1)}, u32[]{:S(2)}, u32[]{:S(2)}) collective-permute-start(bf16[4,256,512]{2,1,0:T(8,128)(2,1)} %dynamic-slice_convert_fusion), channel_id=1, source_target_pairs={{0,16},{1,17},{2,18},{3,19},{4,20},{5,21},{6,22},{7,23},{8,24},{9,... | collective-permute-start | bytes 3145736 | tf_op jit(solution)/shard_map/ppermute | solution.py:167
  285.6 7.5 %collective-permute-start.39 = (bf16[256,1024]{1,0:T(8,128)(2,1)S(1)}, bf16[256,1024]{1,0:T(8,128)(2,1)S(1)}, u32[]{:S(2)}, u32[]{:S(2)}) collective-permute-start(bf16[256,1024]{1,0:T(8,128)(2,1)S(1)} %get-tuple-element.317), channel_id=1, source_target_pairs={{0,8},{1,9},{2,10},{3,11},{4,12},{5,13},{6,14},{7,15},{8,0},{9,1},... | collective-permute-start | bytes 1572872 | tf_op jit(solution)/shard_map/ppermute | solution.py:167
  286.6 13.7 %collective-permute-start.41 = (bf16[256,1024]{1,0:T(8,128)(2,1)S(1)}, bf16[256,1024]{1,0:T(8,128)(2,1)S(1)}, u32[]{:S(2)}, u32[]{:S(2)}) collective-permute-start(bf16[256,1024]{1,0:T(8,128)(2,1)S(1)} %fusion.55), channel_id=1, source_target_pairs={{0,1},{1,0},{2,3},{3,2},{4,5},{5,4},{6,7},{7,6},{8,9},{9,8},{10,11... | collective-permute-start | bytes 1572872 | tf_op jit(solution)/shard_map/ppermute | solution.py:167
  292.4 39.0 %collective-permute-start.60 = (bf16[4,256,512]{2,1,0:T(8,128)(2,1)}, bf16[4,256,512]{2,1,0:T(8,128)(2,1)}, u32[]{:S(2)}, u32[]{:S(2)}) collective-permute-start(bf16[4,256,512]{2,1,0:T(8,128)(2,1)} %dynamic-slice_convert_fusion.1), channel_id=1, source_target_pairs={{0,16},{1,17},{2,18},{3,19},{4,20},{5,21},{6,22},{7,23},{8,24},{9,... | collective-permute-start | bytes 3145736 | tf_op jit(solution)/shard_map/ppermute | solution.py:167
  305.4 89.9 %collective-permute-start.43 = (bf16[256,1024]{1,0:T(8,128)(2,1)}, bf16[256,1024]{1,0:T(8,128)(2,1)}, u32[]{:S(2)}, u32[]{:S(2)}) collective-permute-start(bf16[256,1024]{1,0:T(8,128)(2,1)} %convert_element_type.309), channel_id=1, source_target_pairs={{0,1},{1,0},{2,3},{3,2},{4,5},{5,4},{6,7},{7,6},{8,9},{9,8},{10,11... | collective-permute-start | bytes 1572872 | tf_op jit(solution)/shard_map/ppermute | solution.py:167
  305.7 100.5 %collective-permute-start.42 = (bf16[256,1024]{1,0:T(8,128)(2,1)}, bf16[256,1024]{1,0:T(8,128)(2,1)}, u32[]{:S(2)}, u32[]{:S(2)}) collective-permute-start(bf16[256,1024]{1,0:T(8,128)(2,1)} %convert_element_type.309), channel_id=1, source_target_pairs={{0,8},{1,9},{2,10},{3,11},{4,12},{5,13},{6,14},{7,15},{8,0},{9,1},... | collective-permute-start | bytes 1572872 | tf_op jit(solution)/shard_map/ppermute | solution.py:167
  306.0 14.0 %collective-permute-start.71 = (f32[6,1024]{1,0:T(8,128)S(1)}, f32[6,1024]{1,0:T(8,128)S(1)}, u32[]{:S(2)}, u32[]{:S(2)}) collective-permute-start(f32[6,1024]{1,0:T(8,128)S(1)} %add.551), channel_id=1, source_target_pairs={{0,1},{1,0},{2,3},{3,2},{4,5},{5,4},{6,7},{7,6},{8,9},{9,8},{10,11... | collective-permute-start | bytes 73736 | tf_op jit(solution)/shard_map/ppermute | solution.py:167
  320.0 13.1 %collective-permute-start.72 = (f32[6,1024]{1,0:T(8,128)S(1)}, f32[6,1024]{1,0:T(8,128)S(1)}, u32[]{:S(2)}, u32[]{:S(2)}) collective-permute-start(f32[6,1024]{1,0:T(8,128)S(1)} %add.552), channel_id=1, source_target_pairs={{0,16},{1,17},{2,18},{3,19},{4,20},{5,21},{6,22},{7,23},{8,24},{9,... | collective-permute-start | bytes 73736 | tf_op jit(solution)/shard_map/ppermute | solution.py:167
  335.9 3.9 collective-permute-start.74
  338.2 5.6 %collective-permute-start.61 = (bf16[256,512]{1,0:T(8,128)(2,1)S(1)}, bf16[256,512]{1,0:T(8,128)(2,1)S(1)}, u32[]{:S(2)}, u32[]{:S(2)}) collective-permute-start(bf16[256,512]{1,0:T(8,128)(2,1)S(1)} %get-tuple-element.336), channel_id=1, source_target_pairs={{0,2},{1,3},{2,4},{3,5},{4,6},{5,7},{6,0},{7,1},{8,10},{9,11},{10,... | collective-permute-start | bytes 786440 | tf_op jit(solution)/shard_map/ppermute | solution.py:167
  338.6 12.1 %collective-permute-start.63 = (bf16[256,512]{1,0:T(8,128)(2,1)S(1)}, bf16[256,512]{1,0:T(8,128)(2,1)S(1)}, u32[]{:S(2)}, u32[]{:S(2)}) collective-permute-start(bf16[256,512]{1,0:T(8,128)(2,1)S(1)} %get-tuple-element.337), channel_id=1, source_target_pairs={{0,6},{1,7},{2,0},{3,1},{4,2},{5,3},{6,4},{7,5},{8,14},{9,15},{10,... | collective-permute-start | bytes 786440 | tf_op jit(solution)/shard_map/ppermute | solution.py:167
  339.8 18.8 %collective-permute-start.62 = (bf16[256,512]{1,0:T(8,128)(2,1)S(1)}, bf16[256,512]{1,0:T(8,128)(2,1)S(1)}, u32[]{:S(2)}, u32[]{:S(2)}) collective-permute-start(bf16[256,512]{1,0:T(8,128)(2,1)S(1)} %get-tuple-element.338), channel_id=1, source_target_pairs={{0,4},{1,5},{2,6},{3,7},{4,0},{5,1},{6,2},{7,3},{8,12},{9,13},{10,... | collective-permute-start | bytes 786440 | tf_op jit(solution)/shard_map/ppermute | solution.py:167
  343.8 29.9 %collective-permute-start.66 = (bf16[256,512]{1,0:T(8,128)(2,1)S(1)}, bf16[256,512]{1,0:T(8,128)(2,1)S(1)}, u32[]{:S(2)}, u32[]{:S(2)}) collective-permute-start(bf16[256,512]{1,0:T(8,128)(2,1)S(1)} %get-tuple-element.333), channel_id=1, source_target_pairs={{0,2},{1,3},{2,4},{3,5},{4,6},{5,7},{6,0},{7,1},{8,10},{9,11},{10,... | collective-permute-start | bytes 786440 | tf_op jit(solution)/shard_map/ppermute | solution.py:167
  350.7 32.0 %collective-permute-start.68 = (bf16[256,512]{1,0:T(8,128)(2,1)S(1)}, bf16[256,512]{1,0:T(8,128)(2,1)S(1)}, u32[]{:S(2)}, u32[]{:S(2)}) collective-permute-start(bf16[256,512]{1,0:T(8,128)(2,1)S(1)} %get-tuple-element.334), channel_id=1, source_target_pairs={{0,6},{1,7},{2,0},{3,1},{4,2},{5,3},{6,4},{7,5},{8,14},{9,15},{10,... | collective-permute-start | bytes 786440 | tf_op jit(solution)/shard_map/ppermute | solution.py:167
  358.6 24.1 %collective-permute-start.67 = (bf16[256,512]{1,0:T(8,128)(2,1)S(1)}, bf16[256,512]{1,0:T(8,128)(2,1)S(1)}, u32[]{:S(2)}, u32[]{:S(2)}) collective-permute-start(bf16[256,512]{1,0:T(8,128)(2,1)S(1)} %get-tuple-element.335), channel_id=1, source_target_pairs={{0,4},{1,5},{2,6},{3,7},{4,0},{5,1},{6,2},{7,3},{8,12},{9,13},{10,... | collective-permute-start | bytes 786440 | tf_op jit(solution)/shard_map/ppermute | solution.py:167
  373.8 13.2 %collective-permute-start.64 = (f32[256,256]{1,0:T(8,128)S(1)}, f32[256,256]{1,0:T(8,128)S(1)}, u32[]{:S(2)}, u32[]{:S(2)}) collective-permute-start(f32[256,256]{1,0:T(8,128)S(1)} %get-tuple-element.352), channel_id=1, source_target_pairs={{0,8},{1,9},{2,10},{3,11},{4,12},{5,13},{6,14},{7,15},{8,0},{9,1},... | collective-permute-start | bytes 786440 | tf_op jit(solution)/shard_map/ppermute | solution.py:167
  383.5 6.5 %collective-permute-start.69 = (f32[256,256]{1,0:T(8,128)}, f32[256,256]{1,0:T(8,128)}, u32[]{:S(2)}, u32[]{:S(2)}) collective-permute-start(f32[256,256]{1,0:T(8,128)} %get-tuple-element.350), channel_id=1, source_target_pairs={{0,8},{1,9},{2,10},{3,11},{4,12},{5,13},{6,14},{7,15},{8,0},{9,1},... | collective-permute-start | bytes 786440 | tf_op jit(solution)/shard_map/ppermute | solution.py:167
  395.3 10.8 %collective-permute-start.44 = (bf16[256,1024]{1,0:T(8,128)(2,1)}, bf16[256,1024]{1,0:T(8,128)(2,1)}, u32[]{:S(2)}, u32[]{:S(2)}) collective-permute-start(bf16[256,1024]{1,0:T(8,128)(2,1)} %collective-permute-done.43), channel_id=1, source_target_pairs={{0,8},{1,9},{2,10},{3,11},{4,12},{5,13},{6,14},{7,15},{8,0},{9,1},... | collective-permute-start | bytes 1572872 | tf_op jit(solution)/shard_map/ppermute | solution.py:167
  446.6 7.4 %collective-permute-start.55 = (bf16[4,64,512]{2,1,0:T(8,128)(2,1)S(1)}, bf16[4,64,512]{2,1,0:T(8,128)(2,1)S(1)}, u32[]{:S(2)}, u32[]{:S(2)}) collective-permute-start(bf16[4,64,512]{2,1,0:T(8,128)(2,1)S(1)} %dynamic-slice_convert_fusion.2), channel_id=1, source_target_pairs={{0,16},{1,17},{2,18},{3,19},{4,20},{5,21},{6,22},{7,23},{8,24},{9,... | collective-permute-start | bytes 786440 | tf_op jit(solution)/shard_map/ppermute | solution.py:167
  453.3 19.8 %collective-permute-start.50 = (bf16[4,208,512]{2,1,0:T(8,128)(2,1)S(1)}, bf16[4,208,512]{2,1,0:T(8,128)(2,1)S(1)}, u32[]{:S(2)}, u32[]{:S(2)}) collective-permute-start(bf16[4,208,512]{2,1,0:T(8,128)(2,1)S(1)} %fusion.42), channel_id=1, source_target_pairs={{0,16},{1,17},{2,18},{3,19},{4,20},{5,21},{6,22},{7,23},{8,24},{9,... | collective-permute-start | bytes 2555912 | tf_op jit(solution)/shard_map/ppermute | solution.py:167
  454.1 7.4 %collective-permute-start.56 = (bf16[64,512]{1,0:T(8,128)(2,1)S(1)}, bf16[64,512]{1,0:T(8,128)(2,1)S(1)}, u32[]{:S(2)}, u32[]{:S(2)}) collective-permute-start(bf16[64,512]{1,0:T(8,128)(2,1)S(1)} %get-tuple-element.362), channel_id=1, source_target_pairs={{0,2},{1,3},{2,4},{3,5},{4,6},{5,7},{6,0},{7,1},{8,10},{9,11},{10,... | collective-permute-start | bytes 196616 | tf_op jit(solution)/shard_map/ppermute | solution.py:167
  455.3 6.2 %collective-permute-start.58 = (bf16[64,512]{1,0:T(8,128)(2,1)S(1)}, bf16[64,512]{1,0:T(8,128)(2,1)S(1)}, u32[]{:S(2)}, u32[]{:S(2)}) collective-permute-start(bf16[64,512]{1,0:T(8,128)(2,1)S(1)} %get-tuple-element.363), channel_id=1, source_target_pairs={{0,6},{1,7},{2,0},{3,1},{4,2},{5,3},{6,4},{7,5},{8,14},{9,15},{10,... | collective-permute-start | bytes 196616 | tf_op jit(solution)/shard_map/ppermute | solution.py:167
  457.6 5.0 collective-permute-start.57
  465.4 13.3 %collective-permute-start.45 = (bf16[256,1024]{1,0:T(8,128)(2,1)S(1)}, bf16[256,1024]{1,0:T(8,128)(2,1)S(1)}, u32[]{:S(2)}, u32[]{:S(2)}) collective-permute-start(bf16[256,1024]{1,0:T(8,128)(2,1)S(1)} %get-tuple-element.315), channel_id=1, source_target_pairs={{0,8},{1,9},{2,10},{3,11},{4,12},{5,13},{6,14},{7,15},{8,0},{9,1},... | collective-permute-start | bytes 1572872 | tf_op jit(solution)/shard_map/ppermute | solution.py:167
  468.3 13.4 %collective-permute-start.47 = (bf16[256,1024]{1,0:T(8,128)(2,1)S(1)}, bf16[256,1024]{1,0:T(8,128)(2,1)S(1)}, u32[]{:S(2)}, u32[]{:S(2)}) collective-permute-start(bf16[256,1024]{1,0:T(8,128)(2,1)S(1)} %fusion.52), channel_id=1, source_target_pairs={{0,1},{1,0},{2,3},{3,2},{4,5},{5,4},{6,7},{7,6},{8,9},{9,8},{10,11... | collective-permute-start | bytes 1572872 | tf_op jit(solution)/shard_map/ppermute | solution.py:167
  473.5 8.6 %collective-permute-start.51 = (bf16[208,512]{1,0:T(8,128)(2,1)S(1)}, bf16[208,512]{1,0:T(8,128)(2,1)S(1)}, u32[]{:S(2)}, u32[]{:S(2)}) collective-permute-start(bf16[208,512]{1,0:T(8,128)(2,1)S(1)} %get-tuple-element.343), channel_id=1, source_target_pairs={{0,2},{1,3},{2,4},{3,5},{4,6},{5,7},{6,0},{7,1},{8,10},{9,11},{10,... | collective-permute-start | bytes 638984 | tf_op jit(solution)/shard_map/ppermute | solution.py:167
  474.7 9.3 %collective-permute-start.53 = (bf16[208,512]{1,0:T(8,128)(2,1)S(1)}, bf16[208,512]{1,0:T(8,128)(2,1)S(1)}, u32[]{:S(2)}, u32[]{:S(2)}) collective-permute-start(bf16[208,512]{1,0:T(8,128)(2,1)S(1)} %get-tuple-element.344), channel_id=1, source_target_pairs={{0,6},{1,7},{2,0},{3,1},{4,2},{5,3},{6,4},{7,5},{8,14},{9,15},{10,... | collective-permute-start | bytes 638984 | tf_op jit(solution)/shard_map/ppermute | solution.py:167
  476.7 15.6 %collective-permute-start.52 = (bf16[208,512]{1,0:T(8,128)(2,1)S(1)}, bf16[208,512]{1,0:T(8,128)(2,1)S(1)}, u32[]{:S(2)}, u32[]{:S(2)}) collective-permute-start(bf16[208,512]{1,0:T(8,128)(2,1)S(1)} %get-tuple-element.345), channel_id=1, source_target_pairs={{0,4},{1,5},{2,6},{3,7},{4,0},{5,1},{6,2},{7,3},{8,12},{9,13},{10,... | collective-permute-start | bytes 638984 | tf_op jit(solution)/shard_map/ppermute | solution.py:167
  492.4 10.3 %collective-permute-start.54 = (f32[208,256]{1,0:T(8,128)S(1)}, f32[208,256]{1,0:T(8,128)S(1)}, u32[]{:S(2)}, u32[]{:S(2)}) collective-permute-start(f32[208,256]{1,0:T(8,128)S(1)} %constant_dynamic-slice_fusion.8), channel_id=1, source_target_pairs={{0,8},{1,9},{2,10},{3,11},{4,12},{5,13},{6,14},{7,15},{8,0},{9,1},... | collective-permute-start | bytes 638984 | tf_op jit(solution)/shard_map/ppermute | solution.py:167
  495.4 17.3 %collective-permute-start.48 = (f32[128,1024]{1,0:T(8,128)}, f32[128,1024]{1,0:T(8,128)S(1)}, u32[]{:S(2)}, u32[]{:S(2)}) collective-permute-start(f32[128,1024]{1,0:T(8,128)} %get-tuple-element.339), channel_id=1, source_target_pairs={{0,0},{1,1},{2,2},{3,3},{4,8},{5,9},{6,10},{7,11},{8,4},{9,5},{10,... | collective-permute-start | bytes 1572872 | tf_op jit(solution)/shard_map/ppermute | solution.py:167
  500.0 25.3 %collective-permute-start.49 = (f32[128,1024]{1,0:T(8,128)}, f32[128,1024]{1,0:T(8,128)}, u32[]{:S(2)}, u32[]{:S(2)}) collective-permute-start(f32[128,1024]{1,0:T(8,128)} %get-tuple-element.340), channel_id=1, source_target_pairs={{0,2},{1,3},{2,0},{3,1},{4,10},{5,11},{6,8},{7,9},{8,6},{9,7},{10,... | collective-permute-start | bytes 1572872 | tf_op jit(solution)/shard_map/ppermute | solution.py:167
  (99 other events, 1159.6 us)

commit v2 on v1

v2 whole, which is shorter than its diff:
```python
import functools

import jax
import jax.numpy as jnp
from jax import lax
from jax.experimental import pallas as pl
from jax.experimental.pallas import tpu as pltpu
from jax.sharding import PartitionSpec as P

norm_eps = 1e-05
beta_one = 0.9
beta_two = 0.999
adam_eps = 1e-08
adam_step = 4.0
matrix_rate = 0.01
output_rate = 0.1
vector_rate = 0.1
decay_rate = 0.1
inv_root_two = 0.7071067811865476
inv_root_tau = 0.3989422804014327


def layer_norm(resid, gain_row, shift_row):
    center = resid - jnp.mean(resid, axis=-1, keepdims=True)
    spread = lax.rsqrt(jnp.mean(center * center, axis=-1, keepdims=True) + norm_eps)
    normed = center * spread
    return (normed * gain_row + shift_row, normed, spread)


def norm_back(grad_out, gain_row, normed, spread):
    scaled = grad_out * gain_row
    return spread * (
        scaled
        - jnp.mean(scaled, axis=-1, keepdims=True)
        - normed * jnp.mean(scaled * normed, axis=-1, keepdims=True)
    )


def gelu_value(inner):
    return inner * 0.5 * (1.0 + jax.scipy.special.erf(inner * inv_root_two))


def gelu_slope(inner):
    return (
        0.5 * (1.0 + jax.scipy.special.erf(inner * inv_root_two))
        + inner * jnp.exp(-0.5 * inner * inner) * inv_root_tau
    )


def adamw_update(weight, moments, grad, rate, decay):
    first_moment = beta_one * moments[0] + (1.0 - beta_one) * grad
    second_moment = beta_two * moments[1] + (1.0 - beta_two) * grad * grad
    direction = (
        first_moment
        / (1.0 - beta_one**adam_step)
        / (jnp.sqrt(second_moment / (1.0 - beta_two**adam_step)) + adam_eps)
    )
    return (weight - rate * (direction + decay * weight), jnp.stack([first_moment, second_moment]))


half = jnp.bfloat16
wide = jnp.float32
VMEM_BYTES = 40 * 1024 * 1024


def times(left, right):
    return lax.dot_general(left, right, (((1,), (0,)), ((), ())), preferred_element_type=wide)


def times_t(left, right):
    return lax.dot_general(left, right, (((1,), (1,)), ((), ())), preferred_element_type=wide)


def t_times(left, right):
    return lax.dot_general(left, right, (((0,), (0,)), ((), ())), preferred_element_type=wide)


def whole_block(*shape):
    return pl.BlockSpec(shape, lambda step: (0,) * len(shape))


def sum_shapes(rows, other, width):
    shapes = [jax.ShapeDtypeStruct((rows - other, width), wide)]
    if other:
        shapes.append(jax.ShapeDtypeStruct((other, width), half))
    return shapes, [whole_block(*shape.shape) for shape in shapes]


def write_sums(total, refs):
    mine = refs[0].shape[0]
    refs[0][...] = total[:mine]
    if len(refs) > 1:
        refs[1][...] = total[mine:].astype(half)


def params():
    return pltpu.CompilerParams(
        dimension_semantics=("arbitrary",), vmem_limit_bytes=VMEM_BYTES
    )


def up_kernel(x_ref, up_ref, bias_ref, down_ref, active_ref, slope_ref, *rest):
    sums, total = rest[:-1], rest[-1]
    inner = times_t(x_ref[...], up_ref[...]) + bias_ref[...]
    chance = 0.5 * (1.0 + lax.erf(inner * inv_root_two))
    active = (inner * chance).astype(half)
    active_ref[...] = active
    slope_ref[...] = chance + inner * jnp.exp(-0.5 * inner * inner) * inv_root_tau
    part = times(active, down_ref[...])
    step = pl.program_id(0)

    @pl.when(step == 0)
    def _():
        total[...] = part

    @pl.when(step > 0)
    def _():
        total[...] += part

    @pl.when(step == pl.num_programs(0) - 1)
    def _():
        write_sums(total[...], sums)


def ffn_forward(x, w_upward, b_upward, w_downward, other):
    rows, width = x.shape
    hidden = w_upward.shape[0]
    tile = 256
    shapes, specs = sum_shapes(rows, other, width)
    return pl.pallas_call(
        up_kernel,
        grid=(hidden // tile,),
        in_specs=[
            whole_block(rows, width),
            pl.BlockSpec((tile, width), lambda step: (step, 0)),
            pl.BlockSpec((1, tile), lambda step: (0, step)),
            pl.BlockSpec((tile, width), lambda step: (step, 0)),
        ],
        out_specs=[
            pl.BlockSpec((rows, tile), lambda step: (0, step)),
            pl.BlockSpec((rows, tile), lambda step: (0, step)),
        ]
        + specs,
        out_shape=[
            jax.ShapeDtypeStruct((rows, hidden), half),
            jax.ShapeDtypeStruct((rows, hidden), wide),
        ]
        + shapes,
        scratch_shapes=[pltpu.VMEM((rows, width), wide)],
        compiler_params=params(),
        cost_estimate=pl.CostEstimate(
            flops=4 * rows * width * hidden,
            bytes_accessed=rows * hidden * 6 + hidden * width * 4,
            transcendentals=2 * rows * hidden,
        ),
        name="ffn_forward",
    )(x, w_upward, b_upward, w_downward)


def down_kernel(grad_ref, slope_ref, down_ref, up_ref, inner_ref, bias_ref, *rest):
    sums, total = rest[:-1], rest[-1]
    grad_inner = times_t(grad_ref[...], down_ref[...]) * slope_ref[...]
    bias_ref[...] = jnp.sum(grad_inner, axis=0, keepdims=True)
    grad_inner_b = grad_inner.astype(half)
    inner_ref[...] = grad_inner_b
    part = times(grad_inner_b, up_ref[...])
    step = pl.program_id(0)

    @pl.when(step == 0)
    def _():
        total[...] = part

    @pl.when(step > 0)
    def _():
        total[...] += part

    @pl.when(step == pl.num_programs(0) - 1)
    def _():
        write_sums(total[...], sums)


def ffn_backward(grad, slope, w_downward, w_upward, other):
    rows, width = grad.shape
    hidden = w_upward.shape[0]
    tile = 256
    shapes, specs = sum_shapes(rows, other, width)
    return pl.pallas_call(
        down_kernel,
        grid=(hidden // tile,),
        in_specs=[
            whole_block(rows, width),
            pl.BlockSpec((rows, tile), lambda step: (0, step)),
            pl.BlockSpec((tile, width), lambda step: (step, 0)),
            pl.BlockSpec((tile, width), lambda step: (step, 0)),
        ],
        out_specs=[
            pl.BlockSpec((rows, tile), lambda step: (0, step)),
            pl.BlockSpec((1, tile), lambda step: (0, step)),
        ]
        + specs,
        out_shape=[
            jax.ShapeDtypeStruct((rows, hidden), half),
            jax.ShapeDtypeStruct((1, hidden), wide),
        ]
        + shapes,
        scratch_shapes=[pltpu.VMEM((rows, width), wide)],
        compiler_params=params(),
        cost_estimate=pl.CostEstimate(
            flops=4 * rows * width * hidden,
            bytes_accessed=rows * hidden * 6 + hidden * width * 4,
            transcendentals=0,
        ),
        name="ffn_backward",
    )(grad, slope, w_downward, w_upward)


def attention_kernel(first, chunk, head_width, qkv_ref, out_ref, attn_ref, log_ref, *rest):
    sums, mixed = rest[:-1], rest[-1]
    head = pl.program_id(0)
    scale = head_width ** (-0.5)
    keys = jnp.transpose(qkv_ref[head_width : 2 * head_width, :])
    values = qkv_ref[2 * head_width : 3 * head_width, :]
    count = attn_ref.shape[1]
    for start in range(0, count, chunk):
        here = slice(first + start, first + start + chunk)
        scores = times(keys, qkv_ref[0:head_width, here]) * scale
        top = jnp.max(scores, axis=0, keepdims=True)
        powers = jnp.exp(scores - top)
        norm = jnp.sum(powers, axis=0, keepdims=True)
        weights = (powers * (1.0 / norm)).astype(half)
        log_ref[0, :, start : start + chunk] = top + jnp.log(norm)
        block = times(values, weights).astype(half)
        attn_ref[:, start : start + chunk] = block
        mixed[pl.ds(pl.multiple_of(head * head_width, head_width), head_width), pl.ds(start, chunk)] = block

    @pl.when(head == pl.num_programs(0) - 1)
    def _():
        write_sums(t_times(mixed[...], out_ref[...]), sums)


def attention_forward(qkv, w_output, first, count, other, head_width):
    length = qkv.shape[1]
    heads = qkv.shape[0] // (3 * head_width)
    width = w_output.shape[1]
    chunk = 256 if count % 256 == 0 else 128
    shapes, specs = sum_shapes(count, other, width)
    return pl.pallas_call(
        functools.partial(attention_kernel, first, chunk, head_width),
        grid=(heads,),
        in_specs=[
            pl.BlockSpec((3 * head_width, length), lambda head: (head, 0)),
            whole_block(heads * head_width, width),
        ],
        out_specs=[
            pl.BlockSpec((head_width, count), lambda head: (head, 0)),
            pl.BlockSpec((1, 1, count), lambda head: (head, 0, 0)),
        ]
        + specs,
        out_shape=[
            jax.ShapeDtypeStruct((heads * head_width, count), half),
            jax.ShapeDtypeStruct((heads, 1, count), wide),
        ]
        + shapes,
        scratch_shapes=[pltpu.VMEM((heads * head_width, count), half)],
        compiler_params=params(),
        cost_estimate=pl.CostEstimate(
            flops=16 * heads * count * length * head_width,
            bytes_accessed=qkv.size * 2 + count * width * 6,
            transcendentals=heads * count * length,
        ),
        name="attention_forward",
    )(qkv, w_output)


def attention_back_kernel(chunk, head_width, qkv_ref, log_ref, grad_ref, out_ref, bias_ref):
    scale = head_width ** (-0.5)
    key_rows = qkv_ref[head_width : 2 * head_width, :]
    keys = jnp.transpose(key_rows)
    values = jnp.transpose(qkv_ref[2 * head_width : 3 * head_width, :])
    length = keys.shape[0]
    grad_keys = jnp.zeros((length, head_width), wide)
    grad_values = jnp.zeros((length, head_width), wide)
    query_sum = jnp.zeros((head_width, 1), wide)
    for start in range(0, length, chunk):
        here = slice(start, start + chunk)
        queries = qkv_ref[0:head_width, here]
        grads = grad_ref[:, here]
        scores = times(keys, queries) * scale
        chances = jnp.exp(scores - log_ref[0, :, here])
        grad_scores = times(values, grads)
        mean = jnp.sum(chances * grad_scores, axis=0, keepdims=True)
        logits = (chances * (grad_scores - mean)).astype(half)
        grad_values = grad_values + times(chances.astype(half), jnp.transpose(grads))
        grad_keys = grad_keys + times(logits, jnp.transpose(queries))
        grad_query = times(key_rows, logits) * scale
        out_ref[0:head_width, here] = grad_query.astype(half)
        query_sum = query_sum + jnp.sum(grad_query, axis=1, keepdims=True)
    grad_keys = jnp.transpose(grad_keys) * scale
    grad_values = jnp.transpose(grad_values)
    out_ref[head_width : 2 * head_width, :] = grad_keys.astype(half)
    out_ref[2 * head_width : 3 * head_width, :] = grad_values.astype(half)
    sums = jnp.concatenate(
        [
            query_sum,
            jnp.sum(grad_keys, axis=1, keepdims=True),
            jnp.sum(grad_values, axis=1, keepdims=True),
        ],
        axis=0,
    )
    bias_ref[...] = jnp.broadcast_to(sums, bias_ref.shape)


def attention_backward(qkv, logsum, grad, head_width):
    length = qkv.shape[1]
    heads = qkv.shape[0] // (3 * head_width)
    chunk = 256
    return pl.pallas_call(
        functools.partial(attention_back_kernel, chunk, head_width),
        grid=(heads,),
        in_specs=[
            pl.BlockSpec((3 * head_width, length), lambda head: (head, 0)),
            pl.BlockSpec((1, 1, length), lambda head: (head, 0, 0)),
            pl.BlockSpec((head_width, length), lambda head: (head, 0)),
        ],
        out_specs=[
            pl.BlockSpec((3 * head_width, length), lambda head: (head, 0)),
            pl.BlockSpec((3 * head_width, 128), lambda head: (head, 0)),
        ],
        out_shape=[
            jax.ShapeDtypeStruct(qkv.shape, half),
            jax.ShapeDtypeStruct((qkv.shape[0], 128), wide),
        ],
        compiler_params=params(),
        cost_estimate=pl.CostEstimate(
            flops=40 * heads * length * length * head_width,
            bytes_accessed=qkv.size * 5,
            transcendentals=heads * length * length,
        ),
        name="attention_backward",
    )(qkv, logsum, grad)


def gate(value, *before):
    return lax.optimization_barrier((value,) + before)[0]


AXES = ("fsdp", "tensor")


class Layout:
    def __init__(self, local_heads, local_seqs):
        self.fsdp = lax.axis_size("fsdp")
        self.tensor = lax.axis_size("tensor")
        self.seqs = local_seqs
        self.core = 2 if local_heads % 2 == 0 and self.fsdp % 2 == 0 else 1
        self.outer = self.fsdp // self.core
        self.high = self.core * local_seqs
        self.low = self.tensor // self.high
        self.fsdp_index = lax.axis_index("fsdp")
        self.outer_index = self.fsdp_index // self.core
        self.core_index = self.fsdp_index % self.core
        self.high_index = lax.axis_index("tensor") // self.low

    def send(self, value, target):
        pairs = []
        for outer in range(self.outer):
            for core in range(self.core):
                for high in range(self.high):
                    for low in range(self.low):
                        o, c, h, l = target(outer, core, high, low)
                        source_id = (outer * self.core + core) * self.tensor + high * self.low + low
                        target_id = (o * self.core + c) * self.tensor + h * self.low + l
                        pairs.append((source_id, target_id))
        return lax.ppermute(value, AXES, pairs)

    def swap_core(self, value):
        return self.send(value, lambda o, c, h, l: (o, 1 - c, h, l))

    def to_low(self, value, step):
        return self.send(value, lambda o, c, h, l: (o, c, h, (l + step) % self.low))

    def to_high(self, value, step):
        return self.send(value, lambda o, c, h, l: (o, c, (h + step) % self.high, l))

    def to_outer(self, value, step):
        return self.send(value, lambda o, c, h, l: ((o + step) % self.outer, c, h, l))

    def to_sequence(self, blocks):
        within = self.high_index % self.seqs
        return [
            self.send(
                lax.dynamic_index_in_dim(blocks, (within + k) % self.seqs, 0, keepdims=False),
                lambda o, c, h, l, k=k: (
                    o,
                    h // self.seqs,
                    c * self.seqs + (h % self.seqs + k) % self.seqs,
                    l,
                ),
            )
            for k in range(self.seqs)
        ]

    def from_sequence(self, pieces):
        within = self.high_index % self.seqs
        back = []
        for k in range(self.seqs):
            back.append(
                self.send(
                    pieces[k],
                    lambda o, c, h, l, k=k: (
                        o,
                        h // self.seqs,
                        c * self.seqs + (h % self.seqs - k) % self.seqs,
                        l,
                    ),
                )
            )
        if self.seqs == 2:
            return jnp.where(within == 0, jnp.stack(back), jnp.stack(back[::-1]))
        stacked = jnp.stack(back)
        order = (jnp.arange(self.seqs) - within) % self.seqs
        return jnp.take(stacked, order, axis=0)

    def share(self, own):
        far = [self.to_low(own, -step) for step in range(1, self.low)]
        near = [own]
        if self.core == 2:
            near.append(self.swap_core(own))
            far += [self.swap_core(piece) for piece in far]
        return jnp.concatenate(near, axis=0), jnp.concatenate(far, axis=0)

    def start_reduce(self, parts):
        total = parts[0]
        if self.core == 2:
            total = total + self.swap_core(parts[1]).astype(wide)
        total = total.astype(half)
        count = total.shape[0] // (self.low - 1)
        return [
            self.to_low(total[(step - 1) * count : step * count], step)
            for step in range(1, self.low)
        ]

    def finish_reduce(self, parts, received):
        total = parts[0]
        if self.core == 2:
            total = total + self.swap_core(parts[1]).astype(wide)
        for piece in received:
            total = total + piece.astype(wide)
        return total

    def ordered(self, index, parts, axis):
        count = len(parts)
        if count == 1:
            return parts[0]
        if count == 2:
            return jnp.where(
                index == 0,
                jnp.concatenate(parts, axis=axis),
                jnp.concatenate(parts[::-1], axis=axis),
            )
        width = parts[0].shape[axis]
        shape = list(parts[0].shape)
        shape[axis] = width * count
        result = jnp.zeros(shape, parts[0].dtype)
        for step, part in enumerate(parts):
            result = lax.dynamic_update_slice_in_dim(
                result, part, ((index + step) % count) * width, axis
            )
        return result

    def core_rows(self, rows, core):
        count = rows.shape[0] // self.core
        return lax.dynamic_slice_in_dim(rows, core * count, count, 0)

    def pair_weights(self, matrices, extra=None):
        def pack(core):
            rows = [self.core_rows(matrix, core) for matrix in matrices]
            if extra is not None:
                rows.append(extra)
            return jnp.concatenate(rows, axis=0)

        if self.core == 1:
            return pack(0)
        other = self.swap_core(pack(1 - self.core_index))
        return self.ordered(self.core_index, [pack(self.core_index), other], 1)

    def high_weights(self, rows):
        return [rows] + [self.to_high(rows, -step) for step in range(1, self.high)]

    def outer_weights(self, column):
        return [
            [rows] + [self.to_outer(rows, -step) for step in range(1, self.outer)]
            for rows in column
        ]

    def rows_of(self, gathered, first, count):
        return jnp.concatenate(
            [
                self.ordered(self.outer_index, [part[first : first + count] for part in parts], 1)
                for parts in gathered
            ],
            axis=0,
        )

    def scatter_outer(self, grads):
        width = grads[0].shape[1] // self.outer

        def columns(grad, place):
            return lax.dynamic_slice_in_dim(grad, (place % self.outer) * width, width, 1)

        received = [
            [
                self.to_outer(columns(grad, self.outer_index + step).astype(half), step)
                for step in range(1, self.outer)
            ]
            for grad in grads
        ]
        sums = []
        for grad, parts in zip(grads, received):
            total = columns(grad, self.outer_index).astype(wide)
            for part in parts:
                total = total + part.astype(wide)
            sums.append(total)
        return sums

    def scatter_high(self, sums):
        received = [
            self.to_high(sums[step].astype(half), step) for step in range(1, self.high)
        ]
        total = sums[0]
        for part in received:
            total = total + part.astype(wide)
        return total

    def scatter_core(self, column):
        if self.core == 1:
            return [column]
        width = column.shape[1] // self.core
        mine = lax.dynamic_slice_in_dim(column, self.core_index * width, width, 1)
        other = self.swap_core(
            lax.dynamic_slice_in_dim(column, (1 - self.core_index) * width, width, 1)
        )
        first = self.core_index == 0
        return [jnp.where(first, mine, other), jnp.where(first, other, mine)]

    def total(self, value):
        if self.core == 2:
            value = value + self.swap_core(value)
        bit = 1
        while bit < self.low:
            value = value + self.send(value, lambda o, c, h, l: (o, c, h, l ^ bit))
            bit *= 2
        bit = 1
        while bit < self.outer:
            value = value + self.send(value, lambda o, c, h, l: (o ^ bit, c, h, l))
            bit *= 2
        bit = 1
        while bit < self.high:
            value = value + self.send(value, lambda o, c, h, l: (o, c, h ^ bit, l))
            bit *= 2
        return value


SMALL_ROWS = 16


def pad_columns(rows, width):
    return jnp.pad(rows, [(0, 0)] * (rows.ndim - 1) + [(0, width - rows.shape[-1])])


def per_device(
    layer_input,
    cotangent,
    attn_weight,
    attn_bias,
    out_weight,
    up_weight,
    up_bias,
    down_weight,
    norm_gains,
    norm_shifts,
    attn_weight_moments,
    attn_bias_moments,
    out_weight_moments,
    up_weight_moments,
    up_bias_moments,
    down_weight_moments,
    norm_gains_moments,
    norm_shifts_moments,
):
    local_heads = attn_bias.shape[0]
    local_seqs, block_tokens, model_width = layer_input.shape
    lay = Layout(local_heads, local_seqs)
    fsdp, core, high = lay.fsdp, lay.core, lay.high
    bias_width = attn_bias.shape[1]
    head_width = bias_width * fsdp // 3
    part_heads = local_heads // core
    shard_width = model_width // fsdp
    hidden_part = up_bias.shape[0]
    own_tokens = local_seqs * block_tokens
    near_tokens = core * own_tokens
    far_tokens = near_tokens * (lay.low - 1)
    near_other = near_tokens - near_tokens // core
    far_other = far_tokens - far_tokens // core
    weights = (
        attn_weight,
        attn_bias,
        out_weight,
        up_weight,
        up_bias,
        down_weight,
        norm_gains,
        norm_shifts,
    )

    tokens = jnp.concatenate(lay.to_sequence(layer_input), axis=0)
    small = jnp.concatenate(
        [
            norm_gains.astype(half),
            norm_shifts.astype(half),
            pad_columns(attn_bias.astype(half).reshape(1, -1), shard_width),
            pad_columns(up_bias.astype(half).reshape(1, -1), shard_width),
            jnp.zeros((SMALL_ROWS - 8, shard_width), half),
        ],
        axis=0,
    )
    attn_rows = part_heads * 3 * head_width
    out_rows = part_heads * head_width
    hidden_rows = up_weight.shape[1] // core
    column = lay.high_weights(
        lay.pair_weights([attn_weight.astype(half).T, out_weight.astype(half)], small)
    )
    gathered = lay.outer_weights(column)
    w_attn = lay.rows_of(gathered, 0, attn_rows)
    w_output = lay.rows_of(gathered, attn_rows, out_rows)
    small = lay.rows_of(gathered, attn_rows + out_rows, SMALL_ROWS)
    small = small.reshape(high, SMALL_ROWS, model_width)
    gain_rows = small[0, 0:2].astype(wide)
    shift_rows = small[0, 2:6].astype(wide)
    b_attn = small[:, 6].reshape(high, fsdp, shard_width)[:, :, : local_heads * bias_width]
    b_attn = b_attn.reshape(high, fsdp, core, part_heads, bias_width)
    b_attn = lax.dynamic_index_in_dim(b_attn, lay.core_index, 2, keepdims=False)
    b_attn = jnp.transpose(b_attn, (0, 2, 1, 3)).reshape(-1, 1).astype(wide)
    b_upward = small[:, 7].reshape(high, fsdp, shard_width)[:, :, :hidden_part]
    b_upward = b_upward.reshape(high, core, (fsdp // core) * hidden_part)
    b_upward = lax.dynamic_index_in_dim(b_upward, lay.core_index, 1, keepdims=False)
    b_upward = b_upward.reshape(1, -1).astype(wide)

    near, far = lay.share(tokens)
    tokens_full = jnp.concatenate([near, far], axis=0)
    second = lay.pair_weights([up_weight.astype(half).T, down_weight.astype(half)])
    second = lay.high_weights(gate(second, tokens, *column))
    upward = lay.to_sequence(gate(cotangent, *second))
    upward = jnp.concatenate(upward, axis=0).astype(wide)
    gathered = lay.outer_weights(second)
    w_upward = lay.rows_of(gathered, 0, hidden_rows)
    w_downward = lay.rows_of(gathered, hidden_rows, hidden_rows)

    qkv = (times_t(w_attn, tokens_full) + b_attn).astype(half)
    attn_far, log_far, *parts_far = attention_forward(
        qkv, w_output, near_tokens, far_tokens, far_other, head_width
    )
    received = lay.start_reduce(parts_far)
    attn_near, log_near, *parts_near = attention_forward(
        qkv, w_output, 0, near_tokens, near_other, head_width
    )
    logsum = jnp.concatenate([log_near, log_far], axis=2)
    attn_out = lay.finish_reduce(parts_near, received)
    resid_one = attn_out + shift_rows[0] + tokens.astype(wide)
    hidden_one, normed_one, spread_one = layer_norm(resid_one, gain_rows[0], shift_rows[1])
    hidden_near, hidden_far = lay.share(hidden_one.astype(half))
    active_far, slope_far, *parts_far = ffn_forward(
        hidden_far, w_upward, b_upward, w_downward, far_other
    )
    received = lay.start_reduce(parts_far)
    active_near, slope_near, *parts_near = ffn_forward(
        hidden_near, w_upward, b_upward, w_downward, near_other
    )
    ffn_out = lay.finish_reduce(parts_near, received)
    resid_two = ffn_out + shift_rows[2] + hidden_one
    result, normed_two, spread_two = layer_norm(resid_two, gain_rows[1], shift_rows[3])

    grad_two = norm_back(upward, gain_rows[1], normed_two, spread_two)
    grad_near, grad_far = lay.share(grad_two.astype(half))
    output = result.astype(half).reshape(local_seqs, block_tokens, model_width)
    outputs = lay.from_sequence(output)
    inner_far, up_far, *parts_far = ffn_backward(
        grad_far, slope_far, w_downward, w_upward, far_other
    )
    received = lay.start_reduce(parts_far)
    inner_near, up_near, *parts_near = ffn_backward(
        grad_near, slope_near, w_downward, w_upward, near_other
    )
    grad_down = t_times(active_near, grad_near) + t_times(active_far, grad_far)
    grad_upward = t_times(inner_near, hidden_near) + t_times(inner_far, hidden_far)
    grad_hidden = grad_two + lay.finish_reduce(parts_near, received)
    grad_one = norm_back(grad_hidden, gain_rows[0], normed_one, spread_one)
    second_grads = [
        jnp.concatenate(
            [
                grad_upward[place * hidden_rows : (place + 1) * hidden_rows],
                grad_down[place * hidden_rows : (place + 1) * hidden_rows],
            ],
            axis=0,
        )
        for place in range(high)
    ]
    second_sums = lay.scatter_outer(second_grads)
    one_near, one_far = lay.share(grad_one.astype(half))
    one_full = jnp.concatenate([one_near, one_far], axis=0)
    grad_attn = times_t(w_output, one_full).astype(half)
    grad_qkv, bias_sums = attention_backward(qkv, logsum, grad_attn, head_width)
    grad_far_qkv = grad_qkv[:, near_tokens:]
    far_mine = t_times(grad_far_qkv[:, : far_tokens - far_other], w_attn)
    parts_far = [far_mine]
    parts_near = [t_times(grad_qkv[:, : near_tokens - near_other], w_attn)]
    if core == 2:
        parts_far.append(t_times(grad_far_qkv[:, far_tokens - far_other :], w_attn).astype(half))
        parts_near.append(
            t_times(grad_qkv[:, near_tokens - near_other : near_tokens], w_attn).astype(half)
        )
    received = lay.start_reduce(parts_far)
    input_grad = grad_one + lay.finish_reduce(parts_near, received)
    input_grads = lay.from_sequence(
        input_grad.astype(half).reshape(local_seqs, block_tokens, model_width)
    ).astype(wide)
    grad_attn_w = times(grad_qkv, tokens_full)
    grad_output = times(attn_near, one_near) + times(attn_far, one_far)

    norm_sums = lay.total(
        jnp.stack(
            [
                jnp.sum(grad_hidden * normed_one, axis=0),
                jnp.sum(upward * normed_two, axis=0),
                jnp.sum(grad_one, axis=0),
                jnp.sum(grad_hidden, axis=0),
                jnp.sum(grad_two, axis=0),
                jnp.sum(upward, axis=0),
            ]
        )
    )
    norm_sums = lax.dynamic_slice_in_dim(norm_sums, lay.fsdp_index * shard_width, shard_width, 1)
    core_here = jnp.arange(core) == lay.core_index
    bias_sums = bias_sums[:, 0].reshape(high, part_heads, fsdp, bias_width)
    bias_sums = jnp.transpose(bias_sums, (0, 2, 1, 3))[:, :, None]
    bias_sums = jnp.where(core_here[:, None, None], bias_sums, 0.0)
    bias_sums = pad_columns(bias_sums.reshape(high, fsdp, -1), shard_width)
    up_sums = (up_near + up_far).reshape(high, 1, (fsdp // core) * hidden_part)
    up_sums = jnp.where(core_here[:, None], up_sums, 0.0)
    up_sums = pad_columns(up_sums.reshape(high, fsdp, hidden_part), shard_width)
    small_sums = jnp.pad(
        jnp.stack([bias_sums.reshape(high, -1), up_sums.reshape(high, -1)], axis=1),
        ((0, 0), (0, SMALL_ROWS - 2), (0, 0)),
    )
    second_sums = [gate(part, grad_qkv) for part in second_sums]
    second_shards = lay.scatter_core(lay.scatter_high(second_sums))
    up_shard = jnp.concatenate([part[:hidden_rows] for part in second_shards], axis=0).T
    down_shard = jnp.concatenate([part[hidden_rows:] for part in second_shards], axis=0)
    first_grads = [
        jnp.concatenate(
            [
                grad_attn_w[place * attn_rows : (place + 1) * attn_rows],
                grad_output[place * out_rows : (place + 1) * out_rows],
                small_sums[place],
            ],
            axis=0,
        )
        for place in range(high)
    ]
    first_shards = lay.scatter_core(lay.scatter_high(lay.scatter_outer(first_grads)))
    attn_shard = jnp.concatenate([part[:attn_rows] for part in first_shards], axis=0).T
    out_shard = jnp.concatenate(
        [part[attn_rows : attn_rows + out_rows] for part in first_shards], axis=0
    )
    small_shard = sum(part[attn_rows + out_rows :] for part in first_shards)
    grads = (
        attn_shard,
        small_shard[0, : local_heads * bias_width].reshape(local_heads, bias_width),
        out_shard,
        up_shard,
        small_shard[1, :hidden_part],
        down_shard,
        norm_sums[0:2],
        norm_sums[2:6],
    )
    moments = (
        attn_weight_moments,
        attn_bias_moments,
        out_weight_moments,
        up_weight_moments,
        up_bias_moments,
        down_weight_moments,
        norm_gains_moments,
        norm_shifts_moments,
    )
    rates = (
        matrix_rate,
        vector_rate,
        output_rate,
        matrix_rate,
        vector_rate,
        matrix_rate,
        vector_rate,
        vector_rate,
    )
    decays = (decay_rate, 0.0, decay_rate, decay_rate, 0.0, decay_rate, 0.0, 0.0)
    updated = [
        adamw_update(weights[place], moments[place], grads[place], rates[place], decays[place])
        for place in range(8)
    ]
    new_weights = tuple((pair[0] for pair in updated))
    new_moments = tuple((pair[1] for pair in updated))
    return (outputs, input_grads) + grads + new_weights + new_moments


def solution(mesh):
    return jax.shard_map(
        per_device,
        mesh=mesh,
        in_specs=(
            P("fsdp", "tensor", None),
            P("fsdp", "tensor", None),
            P("fsdp", "tensor"),
            P("tensor", "fsdp"),
            P("tensor", "fsdp"),
            P("fsdp", "tensor"),
            P(("tensor", "fsdp")),
            P("tensor", "fsdp"),
            P(None, "fsdp"),
            P(None, "fsdp"),
            P(None, "fsdp", "tensor"),
            P(None, "tensor", "fsdp"),
            P(None, "tensor", "fsdp"),
            P(None, "fsdp", "tensor"),
            P(None, ("tensor", "fsdp")),
            P(None, "tensor", "fsdp"),
            P(None, None, "fsdp"),
            P(None, None, "fsdp"),
        ),
        out_specs=(
            P("fsdp", "tensor", None),
            P("fsdp", "tensor", None),
            P("fsdp", "tensor"),
            P("tensor", "fsdp"),
            P("tensor", "fsdp"),
            P("fsdp", "tensor"),
            P(("tensor", "fsdp")),
            P("tensor", "fsdp"),
            P(None, "fsdp"),
            P(None, "fsdp"),
            P("fsdp", "tensor"),
            P("tensor", "fsdp"),
            P("tensor", "fsdp"),
            P("fsdp", "tensor"),
            P(("tensor", "fsdp")),
            P("tensor", "fsdp"),
            P(None, "fsdp"),
            P(None, "fsdp"),
            P(None, "fsdp", "tensor"),
            P(None, "tensor", "fsdp"),
            P(None, "tensor", "fsdp"),
            P(None, "fsdp", "tensor"),
            P(None, ("tensor", "fsdp")),
            P(None, "tensor", "fsdp"),
            P(None, None, "fsdp"),
            P(None, None, "fsdp"),
        ),
        check_vma=False,
    )
```

time: 538 us -> 473 us (0.88)
  matrix products: 95.9 us -> 20 us
  Pallas kernels: 0 us -> 57.9 us
  starting transfers between devices: 106 us -> 69.9 us
  waiting for transfers between devices: 207 us -> 197 us
  local copies, waits for them, and re-layouts: 51.8 us -> 59.1 us
    pallas_call x0 -> x7, Pallas kernels: none -> 57.9 us  [the longest x2 15.3 us: attention_forward(): pl.pallas_call(functools.partial(attention_kernel, first, chunk, head_wid...]
    dot_general x18 -> x3, matrix products: 56.9 us -> 2.66 us  [times(): lax.dot_general(left, right, (((1,), (0,)), ((), ())), preferred_element_...]
    ppermute x75 -> x69, starting transfers between devices: 106 us -> 69.9 us  [send(): return lax.ppermute(value, AXES, pairs)]
    dot_general x4 -> x2, matrix products: 24.6 us -> 4.16 us  [times_t(): lax.dot_general(left, right, (((1,), (1,)), ((), ())), preferred_element_...]
    unnamed x169 -> x212, local copies, waits for them, and re-layouts: 19.3 us -> 34.5 us
    ppermute x75 -> x69, waiting for transfers between devices: 207 us -> 197 us  [send(): return lax.ppermute(value, AXES, pairs)]
    add x6 -> x8, other arithmetic: 0.72 us -> 10.4 us  [the longest x4 8.51 us: scatter_outer(): total = total + part.astype(wide)]
    slice x7 -> x39, local copies, waits for them, and re-layouts: 1.6 us -> 10.9 us  [the longest x32 4.34 us: rows_of(): part[first:first + count]]
  transfers between devices with their start and end apart: 75 -> 69, of which waited for: 36 -> 31; matrix products, arithmetic and copies ran while one was open for 23% -> 25% of each run, Pallas kernels for 0% -> 9%
where the time goes in v2:
time: 473 us; the launch traced here: 466 us
  waiting for transfers between devices  197 us (42%)
  starting transfers between devices  69.9 us (15%)
  other arithmetic  59.4 us (13%)
  local copies, waits for them, and re-layouts  59.1 us (12%)
  Pallas kernels  57.9 us (12%)
  matrix products  20 us (4%)
    ppermute x69, waiting for transfers between devices, send(): return lax.ppermute(value, AXES, pairs)  197 us
    ppermute x69, starting transfers between devices, send(): return lax.ppermute(value, AXES, pairs)  69.9 us
    unnamed x212, local copies, waits for them, and re-layouts  34.5 us
    pallas_call x2, Pallas kernels, attention_forward(): pl.pallas_call(functools.partial(attention_kernel, first, chunk, head_wid...  15.3 us
    pallas_call x1, Pallas kernels, attention_backward(): pl.pallas_call(functools.partial(attention_back_kernel, chunk, head_width...  15.1 us
    pallas_call x2, Pallas kernels, ffn_forward(): pl.pallas_call(up_kernel, grid=(hidden // tile,), in_specs=[whole_block(r...  14.1 us
    pallas_call x2, Pallas kernels, ffn_backward(): pl.pallas_call(down_kernel, grid=(hidden // tile,), in_specs=[whole_block...  13.3 us
    dot_general x8, matrix products, t_times(): lax.dot_general(left, right, (((0,), (0,)), ((), ())), preferred_element_...  13.2 us
  transfers between devices with their start and end apart: 69, of which 31 were waited for; matrix products, arithmetic and copies ran while one was open for 25% of the time, Pallas kernels for 9%

profile of v2, /device:TPU:13, one launch (start us, length us, event | category | flops | bytes accessed | tf_op | source)
XLA Modules:
  0.0 466.4 jit_solution(17854319577064662159)
XLA Ops:
  2.0 4.8 %collective-permute-start.8 = (bf16[128,1024]{1,0:T(8,128)(2,1)S(1)}, bf16[128,1024]{1,0:T(8,128)(2,1)S(1)}, u32[]{:S(2)}, u32[]{:S(2)}) collective-permute-start(bf16[128,1024]{1,0:T(8,128)(2,1)S(1)} %get-tuple-element.233), channel_id=1, source_target_pairs={{0,0},{1,1},{2,2},{3,3},{4,8},{5,9},{6,10},{7,11},{8,4},{9,5},{10,... | collective-permute-start | bytes 786440 | tf_op jit(solution)/shard_map/ppermute | solution.py:374
  12.8 16.4 %collective-permute-done.8 = bf16[128,1024]{1,0:T(8,128)(2,1)S(1)} collective-permute-done((bf16[128,1024]{1,0:T(8,128)(2,1)S(1)}, bf16[128,1024]{1,0:T(8,128)(2,1)S(1)}, u32[]{:S(2)}, u32[]{:S(2)}) %collective-permute-start.8) | collective-permute-done | bytes 262176 | tf_op jit(solution)/shard_map/ppermute | solution.py:374
  29.9 4.9 %collective-permute-done.9 = bf16[128,1024]{1,0:T(8,128)(2,1)S(1)} collective-permute-done((bf16[128,1024]{1,0:T(8,128)(2,1)S(1)}, bf16[128,1024]{1,0:T(8,128)(2,1)S(1)}, u32[]{:S(2)}, u32[]{:S(2)}) %collective-permute-start.9) | collective-permute-done | bytes 262176 | tf_op jit(solution)/shard_map/ppermute | solution.py:374
  37.1 2.3 collective-permute-done.4
  39.4 3.0 collective-permute-done.6
  46.1 4.9 %collective-permute-done.3 = bf16[272,512]{1,0:T(8,128)(2,1)S(1)} collective-permute-done((bf16[272,512]{1,0:T(8,128)(2,1)S(1)}, bf16[272,512]{1,0:T(8,128)(2,1)S(1)}, u32[]{:S(2)}, u32[]{:S(2)}) %collective-permute-start.3) | collective-permute-done | bytes 278560 | tf_op jit(solution)/shard_map/ppermute | solution.py:374
  51.0 6.1 %collective-permute-done.5 = bf16[272,512]{1,0:T(8,128)(2,1)S(1)} collective-permute-done((bf16[272,512]{1,0:T(8,128)(2,1)S(1)}, bf16[272,512]{1,0:T(8,128)(2,1)S(1)}, u32[]{:S(2)}, u32[]{:S(2)}) %collective-permute-start.5) | collective-permute-done | bytes 278560 | tf_op jit(solution)/shard_map/ppermute | solution.py:374
  57.1 5.4 %collective-permute-done.7 = bf16[272,512]{1,0:T(8,128)(2,1)S(1)} collective-permute-done((bf16[272,512]{1,0:T(8,128)(2,1)S(1)}, bf16[272,512]{1,0:T(8,128)(2,1)S(1)}, u32[]{:S(2)}, u32[]{:S(2)}) %collective-permute-start.7) | collective-permute-done | bytes 278560 | tf_op jit(solution)/shard_map/ppermute | solution.py:374
  68.3 19.9 %collective-permute-done.19 = bf16[512,512]{1,0:T(8,128)(2,1)} collective-permute-done((bf16[512,512]{1,0:T(8,128)(2,1)S(1)}, bf16[512,512]{1,0:T(8,128)(2,1)}, u32[]{:S(2)}, u32[]{:S(2)}) %collective-permute-start.19) | collective-permute-done | bytes 524320 | tf_op jit(solution)/shard_map/ppermute | solution.py:374
  92.7 3.4 add_convert_fusion.qkv_ref
  96.1 7.8 %attention_forward.3 = (bf16[256,512]{1,0:T(8,128)(2,1)S(1)}, f32[4,1,512]{2,1,0:T(1,128)S(1)}, f32[256,1024]{1,0:T(8,128)S(1)}, bf16[256,1024]{1,0:T(8,128)(2,1)S(1)}) custom-call(bf16[768,1024]{1,0:T(8,128)(2,1)S(1)} %add_convert_fusion.qkv_ref, bf16[256,1024]{1,0:T(8,128)(2,1)S(1)} %pad_maximum_fusion.12.out_ref), custom_call_target="tpu_custom_call" | custom-call | flops 2147483648 | bytes 4718592 | tf_op jit(solution)/shard_map/attention_forward/pallas_call | solution.py:247
  106.5 7.5 %attention_forward.2 = (bf16[256,512]{1,0:T(8,128)(2,1)S(1)}, f32[4,1,512]{2,1,0:T(1,128)S(1)}, f32[256,1024]{1,0:T(8,128)S(1)}, bf16[256,1024]{1,0:T(8,128)(2,1)S(1)}) custom-call(bf16[768,1024]{1,0:T(8,128)(2,1)S(1)} %add_convert_fusion.qkv_ref, bf16[256,1024]{1,0:T(8,128)(2,1)S(1)} %pad_maximum_fusion.12.out_ref), custom_call_target="tpu_custom_call" | custom-call | flops 2147483648 | bytes 4718592 | tf_op jit(solution)/shard_map/attention_forward/pallas_call | solution.py:247
  116.4 12.2 %collective-permute-done.15 = bf16[256,1024]{1,0:T(8,128)(2,1)S(1)} collective-permute-done((bf16[256,1024]{1,0:T(8,128)(2,1)S(1)}, bf16[256,1024]{1,0:T(8,128)(2,1)S(1)}, u32[]{:S(2)}, u32[]{:S(2)}) %collective-permute-start.15) | collective-permute-done | bytes 524320 | tf_op jit(solution)/shard_map/ppermute | solution.py:374
  132.2 10.9 %collective-permute-done.26 = bf16[256,1024]{1,0:T(8,128)(2,1)S(1)} collective-permute-done((bf16[256,1024]{1,0:T(8,128)(2,1)S(1)}, bf16[256,1024]{1,0:T(8,128)(2,1)S(1)}, u32[]{:S(2)}, u32[]{:S(2)}) %collective-permute-start.26) | collective-permute-done | bytes 524320 | tf_op jit(solution)/shard_map/ppermute | solution.py:374
  146.3 6.7 %ffn_forward.3 = (bf16[512,1024]{1,0:T(8,128)(2,1)S(1)}, f32[512,1024]{1,0:T(8,128)S(1)}, f32[256,1024]{1,0:T(8,128)S(1)}, bf16[256,1024]{1,0:T(8,128)(2,1)S(1)}) custom-call(bf16[512,1024]{1,0:T(8,128)(2,1)S(1)} %constant_dynamic-update-slice_fusion.7.x_ref, bf16[1024,1024]{1,0:T(8,128)(2,1)S(1)} %pad_maximum_fusion.up_ref, f32[1,1024]{1,0:T(1,128)S(1)} %convert.2.bias_ref, ...), custom_call_target="tpu_custom_call" | custom-call | flops 2147483648 | bytes 7340032 | tf_op jit(solution)/shard_map/ffn_forward/pallas_call | solution.py:130
  155.5 7.5 %ffn_forward.2 = (bf16[512,1024]{1,0:T(8,128)(2,1)S(1)}, f32[512,1024]{1,0:T(8,128)S(1)}, f32[256,1024]{1,0:T(8,128)S(1)}, bf16[256,1024]{1,0:T(8,128)(2,1)}) custom-call(bf16[512,1024]{1,0:T(8,128)(2,1)S(1)} %pad_maximum_fusion.7.x_ref, bf16[1024,1024]{1,0:T(8,128)(2,1)S(1)} %pad_maximum_fusion.up_ref, f32[1,1024]{1,0:T(1,128)S(1)} %convert.2.bias_ref, ...), custom_call_target="tpu_custom_call" | custom-call | flops 2147483648 | bytes 7340032 | tf_op jit(solution)/shard_map/ffn_forward/pallas_call | solution.py:130
  166.0 2.2 fusion.107
  168.2 2.0 copy.82
  170.3 2.1 copy.83
  173.4 4.4 collective-permute-start.32
  177.8 10.6 %collective-permute-start.33 = (bf16[128,1024]{1,0:T(8,128)(2,1)S(1)}, bf16[128,1024]{1,0:T(8,128)(2,1)S(1)}, u32[]{:S(2)}, u32[]{:S(2)}) collective-permute-start(bf16[128,1024]{1,0:T(8,128)(2,1)S(1)} %get-tuple-element.213), channel_id=1, source_target_pairs={{0,2},{1,3},{2,0},{3,1},{4,10},{5,11},{6,8},{7,9},{8,6},{9,7},{10,... | collective-permute-start | bytes 786440 | tf_op jit(solution)/shard_map/ppermute | solution.py:374
  188.4 2.3 fusion.102
  191.0 6.5 %collective-permute-done.33 = bf16[128,1024]{1,0:T(8,128)(2,1)S(1)} collective-permute-done((bf16[128,1024]{1,0:T(8,128)(2,1)S(1)}, bf16[128,1024]{1,0:T(8,128)(2,1)S(1)}, u32[]{:S(2)}, u32[]{:S(2)}) %collective-permute-start.33) | collective-permute-done | bytes 262176 | tf_op jit(solution)/shard_map/ppermute | solution.py:374
  200.3 2.9 collective-permute-start.30
  205.2 1.9 copy.80
  207.2 1.9 copy.81
  210.9 6.3 %collective-permute-done.31 = bf16[128,1024]{1,0:T(8,128)(2,1)} collective-permute-done((bf16[128,1024]{1,0:T(8,128)(2,1)}, bf16[128,1024]{1,0:T(8,128)(2,1)}, u32[]{:S(2)}, u32[]{:S(2)}) %collective-permute-start.31) | collective-permute-done | bytes 262176 | tf_op jit(solution)/shard_map/ppermute | solution.py:374
  217.2 2.1 maximum_select_fusion.9
  223.8 7.0 %ffn_backward.2 = (bf16[512,1024]{1,0:T(8,128)(2,1)S(1)}, f32[1,1024]{1,0:T(1,128)S(1)}, f32[256,1024]{1,0:T(8,128)S(1)}, bf16[256,1024]{1,0:T(8,128)(2,1)}) custom-call(bf16[512,1024]{1,0:T(8,128)(2,1)S(1)} %pad_maximum_fusion.8.grad_ref, f32[512,1024]{1,0:T(8,128)S(1)} %copy-done.12, bf16[1024,1024]{1,0:T(8,128)(2,1)S(1)} %copy-done.1, ...), custom_call_target="tpu_custom_call" | custom-call | flops 2147483648 | bytes 7340032 | tf_op jit(solution)/shard_map/ffn_backward/pallas_call | solution.py:187
  231.3 2.6 fusion.97
  235.5 6.4 %ffn_backward.3 = (bf16[512,1024]{1,0:T(8,128)(2,1)S(1)}, f32[1,1024]{1,0:T(1,128)S(1)}, f32[256,1024]{1,0:T(8,128)S(1)}, bf16[256,1024]{1,0:T(8,128)(2,1)S(1)}) custom-call(bf16[512,1024]{1,0:T(8,128)(2,1)S(1)} %constant_dynamic-update-slice_fusion.9.grad_ref, f32[512,1024]{1,0:T(8,128)S(1)} %copy-done.10, bf16[1024,1024]{1,0:T(8,128)(2,1)S(1)} %copy-done.1, ...), custom_call_target="tpu_custom_call" | custom-call | flops 2147483648 | bytes 7340032 | tf_op jit(solution)/shard_map/ffn_backward/pallas_call | solution.py:187
  254.5 2.1 fusion.19
  257.8 4.4 collective-permute-done.39
  262.2 1.9 multiply_reduce_fusion
  269.0 6.3 %collective-permute-done.56 = bf16[512,512]{1,0:T(8,128)(2,1)} collective-permute-done((bf16[512,512]{1,0:T(8,128)(2,1)}, bf16[512,512]{1,0:T(8,128)(2,1)}, u32[]{:S(2)}, u32[]{:S(2)}) %collective-permute-start.56) | collective-permute-done | bytes 524320 | tf_op jit(solution)/shard_map/ppermute | solution.py:374
  275.3 2.3 fusion.33
  278.0 2.2 fusion.29
  280.1 18.3 %collective-permute-done.66 = f32[6,1024]{1,0:T(8,128)S(1)} collective-permute-done((f32[6,1024]{1,0:T(8,128)S(1)}, f32[6,1024]{1,0:T(8,128)S(1)}, u32[]{:S(2)}, u32[]{:S(2)}) %collective-permute-start.66) | collective-permute-done | bytes 24608 | tf_op jit(solution)/shard_map/ppermute | solution.py:374
  298.5 2.0 fusion.25
  302.7 2.0 fusion.21
  305.1 1.9 collective-permute-start.40
  307.6 9.0 %collective-permute-done.41 = bf16[256,1024]{1,0:T(8,128)(2,1)S(1)} collective-permute-done((bf16[256,1024]{1,0:T(8,128)(2,1)S(1)}, bf16[256,1024]{1,0:T(8,128)(2,1)S(1)}, u32[]{:S(2)}, u32[]{:S(2)}) %collective-permute-start.41) | collective-permute-done | bytes 524320 | tf_op jit(solution)/shard_map/ppermute | solution.py:374
  316.6 2.6 collective-permute-start.42
  322.9 15.1 %attention_backward.1 = (bf16[768,1024]{1,0:T(8,128)(2,1)S(1)}, f32[768,128]{1,0:T(8,128)S(1)}) custom-call(bf16[768,1024]{1,0:T(8,128)(2,1)S(1)} %copy-done.14, f32[4,1,1024]{2,1,0:T(1,128)S(1)} %pad_maximum_fusion.21.log_ref, bf16[256,1024]{1,0:T(8,128)(2,1)S(1)} %fusion.11.grad_ref), custom_call_target="tpu_custom_call" | custom-call | flops 10737418240 | bytes 3932160 | tf_op jit(solution)/shard_map/attention_backward/pallas_call | solution.py:317
  343.3 2.2 collective-permute-start.60
  353.8 5.9 %collective-permute-done.49 = bf16[272,512]{1,0:T(8,128)(2,1)S(1)} collective-permute-done((bf16[272,512]{1,0:T(8,128)(2,1)S(1)}, bf16[272,512]{1,0:T(8,128)(2,1)S(1)}, u32[]{:S(2)}, u32[]{:S(2)}) %collective-permute-start.49) | collective-permute-done | bytes 278560 | tf_op jit(solution)/shard_map/ppermute | solution.py:374
  360.0 5.7 %collective-permute-done.51 = bf16[272,512]{1,0:T(8,128)(2,1)S(1)} collective-permute-done((bf16[272,512]{1,0:T(8,128)(2,1)S(1)}, bf16[272,512]{1,0:T(8,128)(2,1)S(1)}, u32[]{:S(2)}, u32[]{:S(2)}) %collective-permute-start.51) | collective-permute-done | bytes 278560 | tf_op jit(solution)/shard_map/ppermute | solution.py:374
  366.0 5.5 %collective-permute-done.53 = bf16[272,512]{1,0:T(8,128)(2,1)S(1)} collective-permute-done((bf16[272,512]{1,0:T(8,128)(2,1)S(1)}, bf16[272,512]{1,0:T(8,128)(2,1)S(1)}, u32[]{:S(2)}, u32[]{:S(2)}) %collective-permute-start.53) | collective-permute-done | bytes 278560 | tf_op jit(solution)/shard_map/ppermute | solution.py:374
  371.5 2.5 collective-permute-start.44
  375.9 18.7 %collective-permute-done.60 = bf16[512,512]{1,0:T(8,128)(2,1)} collective-permute-done((bf16[512,512]{1,0:T(8,128)(2,1)}, bf16[512,512]{1,0:T(8,128)(2,1)}, u32[]{:S(2)}, u32[]{:S(2)}) %collective-permute-start.60) | collective-permute-done | bytes 524320 | tf_op jit(solution)/shard_map/ppermute | solution.py:374
  394.7 3.1 collective-permute-start.52
  402.7 3.8 collective-permute-done.50
  407.6 4.8 %collective-permute-done.52 = bf16[272,512]{1,0:T(8,128)(2,1)S(1)} collective-permute-done((bf16[272,512]{1,0:T(8,128)(2,1)S(1)}, bf16[272,512]{1,0:T(8,128)(2,1)S(1)}, u32[]{:S(2)}, u32[]{:S(2)}) %collective-permute-start.52) | collective-permute-done | bytes 278560 | tf_op jit(solution)/shard_map/ppermute | solution.py:374
  412.5 3.0 collective-permute-done.54
  421.9 2.3 fusion.73
  425.1 2.3 copy.76
  427.5 1.9 copy.74
  441.2 2.5 copy.77
  443.7 2.0 copy.75
  446.6 2.0 copy.73
  448.6 2.5 add_convert_fusion.1
  451.1 2.3 collective-permute-start.46
  456.1 3.7 collective-permute-done.46
  459.8 5.3 %collective-permute-done.47 = bf16[128,1024]{1,0:T(8,128)(2,1)S(1)} collective-permute-done((bf16[128,1024]{1,0:T(8,128)(2,1)S(1)}, bf16[128,1024]{1,0:T(8,128)(2,1)S(1)}, u32[]{:S(2)}, u32[]{:S(2)}) %collective-permute-start.47) | collective-permute-done | bytes 262176 | tf_op jit(solution)/shard_map/ppermute | solution.py:374
  (520 shorter events, 126.7 us)
Async XLA Ops:
  2.0 27.2 %collective-permute-start.8 = (bf16[128,1024]{1,0:T(8,128)(2,1)S(1)}, bf16[128,1024]{1,0:T(8,128)(2,1)S(1)}, u32[]{:S(2)}, u32[]{:S(2)}) collective-permute-start(bf16[128,1024]{1,0:T(8,128)(2,1)S(1)} %get-tuple-element.233), channel_id=1, source_target_pairs={{0,0},{1,1},{2,2},{3,3},{4,8},{5,9},{6,10},{7,11},{8,4},{9,5},{10,... | collective-permute-start | bytes 786440 | tf_op jit(solution)/shard_map/ppermute | solution.py:374
  6.8 28.0 %collective-permute-start.9 = (bf16[128,1024]{1,0:T(8,128)(2,1)S(1)}, bf16[128,1024]{1,0:T(8,128)(2,1)S(1)}, u32[]{:S(2)}, u32[]{:S(2)}) collective-permute-start(bf16[128,1024]{1,0:T(8,128)(2,1)S(1)} %get-tuple-element.232), channel_id=1, source_target_pairs={{0,2},{1,3},{2,0},{3,1},{4,10},{5,11},{6,8},{7,9},{8,6},{9,7},{10,... | collective-permute-start | bytes 786440 | tf_op jit(solution)/shard_map/ppermute | solution.py:374
  9.3 26.4 %collective-permute-start.17 = (bf16[512,256]{1,0:T(8,128)(2,1)S(1)}, bf16[512,256]{1,0:T(8,128)(2,1)S(1)}, u32[]{:S(2)}, u32[]{:S(2)}) collective-permute-start(bf16[512,256]{1,0:T(8,128)(2,1)S(1)} %pad_maximum_fusion.16), channel_id=1, source_target_pairs={{0,8},{1,9},{2,10},{3,11},{4,12},{5,13},{6,14},{7,15},{8,0},{9,1},... | collective-permute-start | bytes 786440 | tf_op jit(solution)/shard_map/ppermute | solution.py:374
  10.0 25.8 %collective-permute-start.2 = (bf16[272,512]{1,0:T(8,128)(2,1)S(1)}, bf16[272,512]{1,0:T(8,128)(2,1)S(1)}, u32[]{:S(2)}, u32[]{:S(2)}) collective-permute-start(bf16[272,512]{1,0:T(8,128)(2,1)S(1)} %maximum_select_fusion.15), channel_id=1, source_target_pairs={{0,6},{1,7},{2,0},{3,1},{4,2},{5,3},{6,4},{7,5},{8,14},{9,15},{10,... | collective-permute-start | bytes 835592 | tf_op jit(solution)/shard_map/ppermute | solution.py:374
  11.2 28.2 %collective-permute-start.4 = (bf16[272,512]{1,0:T(8,128)(2,1)S(1)}, bf16[272,512]{1,0:T(8,128)(2,1)S(1)}, u32[]{:S(2)}, u32[]{:S(2)}) collective-permute-start(bf16[272,512]{1,0:T(8,128)(2,1)S(1)} %maximum_select_fusion.15), channel_id=1, source_target_pairs={{0,4},{1,5},{2,6},{3,7},{4,0},{5,1},{6,2},{7,3},{8,12},{9,13},{10,... | collective-permute-start | bytes 835592 | tf_op jit(solution)/shard_map/ppermute | solution.py:374
  29.2 13.2 %collective-permute-start.6 = (bf16[272,512]{1,0:T(8,128)(2,1)S(1)}, bf16[272,512]{1,0:T(8,128)(2,1)S(1)}, u32[]{:S(2)}, u32[]{:S(2)}) collective-permute-start(bf16[272,512]{1,0:T(8,128)(2,1)S(1)} %maximum_select_fusion.15), channel_id=1, source_target_pairs={{0,2},{1,3},{2,4},{3,5},{4,6},{5,7},{6,0},{7,1},{8,10},{9,11},{10,... | collective-permute-start | bytes 835592 | tf_op jit(solution)/shard_map/ppermute | solution.py:374
  34.8 9.9 %collective-permute-start.1 = (bf16[272,512]{1,0:T(8,128)(2,1)S(1)}, bf16[272,512]{1,0:T(8,128)(2,1)S(1)}, u32[]{:S(2)}, u32[]{:S(2)}) collective-permute-start(bf16[272,512]{1,0:T(8,128)(2,1)S(1)} %maximum_select_fusion.15), channel_id=1, source_target_pairs={{0,16},{1,17},{2,18},{3,19},{4,20},{5,21},{6,22},{7,23},{8,24},{9,... | collective-permute-start | bytes 835592 | tf_op jit(solution)/shard_map/ppermute | solution.py:374
  35.7 30.6 %collective-permute-start.10 = (bf16[256,1024]{1,0:T(8,128)(2,1)S(1)}, bf16[256,1024]{1,0:T(8,128)(2,1)S(1)}, u32[]{:S(2)}, u32[]{:S(2)}) collective-permute-start(bf16[256,1024]{1,0:T(8,128)(2,1)S(1)} %get-tuple-element.249), channel_id=1, source_target_pairs={{0,8},{1,9},{2,10},{3,11},{4,12},{5,13},{6,14},{7,15},{8,0},{9,1},... | collective-permute-start | bytes 1572872 | tf_op jit(solution)/shard_map/ppermute | solution.py:374
  35.9 30.1 %collective-permute-start.11 = (bf16[256,1024]{1,0:T(8,128)(2,1)S(1)}, bf16[256,1024]{1,0:T(8,128)(2,1)S(1)}, u32[]{:S(2)}, u32[]{:S(2)}) collective-permute-start(bf16[256,1024]{1,0:T(8,128)(2,1)S(1)} %get-tuple-element.249), channel_id=1, source_target_pairs={{0,1},{1,0},{2,3},{3,2},{4,5},{5,4},{6,7},{7,6},{8,9},{9,8},{10,11... | collective-permute-start | bytes 1572872 | tf_op jit(solution)/shard_map/ppermute | solution.py:374
  42.4 8.6 %collective-permute-start.3 = (bf16[272,512]{1,0:T(8,128)(2,1)S(1)}, bf16[272,512]{1,0:T(8,128)(2,1)S(1)}, u32[]{:S(2)}, u32[]{:S(2)}) collective-permute-start(bf16[272,512]{1,0:T(8,128)(2,1)S(1)} %collective-permute-done.2), channel_id=1, source_target_pairs={{0,16},{1,17},{2,18},{3,19},{4,20},{5,21},{6,22},{7,23},{8,24},{9,... | collective-permute-start | bytes 835592 | tf_op jit(solution)/shard_map/ppermute | solution.py:374
  42.6 14.5 %collective-permute-start.5 = (bf16[272,512]{1,0:T(8,128)(2,1)S(1)}, bf16[272,512]{1,0:T(8,128)(2,1)S(1)}, u32[]{:S(2)}, u32[]{:S(2)}) collective-permute-start(bf16[272,512]{1,0:T(8,128)(2,1)S(1)} %collective-permute-done.4), channel_id=1, source_target_pairs={{0,16},{1,17},{2,18},{3,19},{4,20},{5,21},{6,22},{7,23},{8,24},{9,... | collective-permute-start | bytes 835592 | tf_op jit(solution)/shard_map/ppermute | solution.py:374
  44.7 17.8 %collective-permute-start.7 = (bf16[272,512]{1,0:T(8,128)(2,1)S(1)}, bf16[272,512]{1,0:T(8,128)(2,1)S(1)}, u32[]{:S(2)}, u32[]{:S(2)}) collective-permute-start(bf16[272,512]{1,0:T(8,128)(2,1)S(1)} %collective-permute-done.6), channel_id=1, source_target_pairs={{0,16},{1,17},{2,18},{3,19},{4,20},{5,21},{6,22},{7,23},{8,24},{9,... | collective-permute-start | bytes 835592 | tf_op jit(solution)/shard_map/ppermute | solution.py:374
  51.0 37.2 %collective-permute-start.19 = (bf16[512,512]{1,0:T(8,128)(2,1)S(1)}, bf16[512,512]{1,0:T(8,128)(2,1)}, u32[]{:S(2)}, u32[]{:S(2)}) collective-permute-start(bf16[512,512]{1,0:T(8,128)(2,1)S(1)} %maximum_select_fusion), channel_id=1, source_target_pairs={{0,6},{1,7},{2,0},{3,1},{4,2},{5,3},{6,4},{7,5},{8,14},{9,15},{10,... | collective-permute-start | bytes 1572872 | tf_op jit(solution)/shard_map/ppermute | solution.py:374
  57.1 31.4 %collective-permute-start.21 = (bf16[512,512]{1,0:T(8,128)(2,1)S(1)}, bf16[512,512]{1,0:T(8,128)(2,1)}, u32[]{:S(2)}, u32[]{:S(2)}) collective-permute-start(bf16[512,512]{1,0:T(8,128)(2,1)S(1)} %maximum_select_fusion), channel_id=1, source_target_pairs={{0,4},{1,5},{2,6},{3,7},{4,0},{5,1},{6,2},{7,3},{8,12},{9,13},{10,... | collective-permute-start | bytes 1572872 | tf_op jit(solution)/shard_map/ppermute | solution.py:374
  62.5 42.6 %collective-permute-start.23 = (bf16[512,512]{1,0:T(8,128)(2,1)S(1)}, bf16[512,512]{1,0:T(8,128)(2,1)}, u32[]{:S(2)}, u32[]{:S(2)}) collective-permute-start(bf16[512,512]{1,0:T(8,128)(2,1)S(1)} %maximum_select_fusion), channel_id=1, source_target_pairs={{0,2},{1,3},{2,4},{3,5},{4,6},{5,7},{6,0},{7,1},{8,10},{9,11},{10,... | collective-permute-start | bytes 1572872 | tf_op jit(solution)/shard_map/ppermute | solution.py:374
  66.0 24.8 %collective-permute-start.12 = (bf16[256,1024]{1,0:T(8,128)(2,1)S(1)}, bf16[256,1024]{1,0:T(8,128)(2,1)}, u32[]{:S(2)}, u32[]{:S(2)}) collective-permute-start(bf16[256,1024]{1,0:T(8,128)(2,1)S(1)} %collective-permute-done.11), channel_id=1, source_target_pairs={{0,8},{1,9},{2,10},{3,11},{4,12},{5,13},{6,14},{7,15},{8,0},{9,1},... | collective-permute-start | bytes 1572872 | tf_op jit(solution)/shard_map/ppermute | solution.py:374
  66.3 48.7 %collective-permute-start.18 = (bf16[512,512]{1,0:T(8,128)(2,1)S(1)}, bf16[512,512]{1,0:T(8,128)(2,1)S(1)}, u32[]{:S(2)}, u32[]{:S(2)}) collective-permute-start(bf16[512,512]{1,0:T(8,128)(2,1)S(1)} %maximum_select_fusion), channel_id=1, source_target_pairs={{0,16},{1,17},{2,18},{3,19},{4,20},{5,21},{6,22},{7,23},{8,24},{9,... | collective-permute-start | bytes 1572872 | tf_op jit(solution)/shard_map/ppermute | solution.py:374
  88.2 27.2 %collective-permute-start.20 = (bf16[512,512]{1,0:T(8,128)(2,1)}, bf16[512,512]{1,0:T(8,128)(2,1)S(1)}, u32[]{:S(2)}, u32[]{:S(2)}) collective-permute-start(bf16[512,512]{1,0:T(8,128)(2,1)} %collective-permute-done.19), channel_id=1, source_target_pairs={{0,16},{1,17},{2,18},{3,19},{4,20},{5,21},{6,22},{7,23},{8,24},{9,... | collective-permute-start | bytes 1572872 | tf_op jit(solution)/shard_map/ppermute | solution.py:374
  88.4 27.0 %collective-permute-start.22 = (bf16[512,512]{1,0:T(8,128)(2,1)}, bf16[512,512]{1,0:T(8,128)(2,1)S(1)}, u32[]{:S(2)}, u32[]{:S(2)}) collective-permute-start(bf16[512,512]{1,0:T(8,128)(2,1)} %collective-permute-done.21), channel_id=1, source_target_pairs={{0,16},{1,17},{2,18},{3,19},{4,20},{5,21},{6,22},{7,23},{8,24},{9,... | collective-permute-start | bytes 1572872 | tf_op jit(solution)/shard_map/ppermute | solution.py:374
  104.0 10.1 %collective-permute-start.14 = (bf16[256,1024]{1,0:T(8,128)(2,1)S(1)}, bf16[256,1024]{1,0:T(8,128)(2,1)S(1)}, u32[]{:S(2)}, u32[]{:S(2)}) collective-permute-start(bf16[256,1024]{1,0:T(8,128)(2,1)S(1)} %get-tuple-element.61), channel_id=1, source_target_pairs={{0,8},{1,9},{2,10},{3,11},{4,12},{5,13},{6,14},{7,15},{8,0},{9,1},... | collective-permute-start | bytes 1572872 | tf_op jit(solution)/shard_map/ppermute | solution.py:374
  105.1 25.8 %collective-permute-start.24 = (bf16[512,512]{1,0:T(8,128)(2,1)}, bf16[512,512]{1,0:T(8,128)(2,1)S(1)}, u32[]{:S(2)}, u32[]{:S(2)}) collective-permute-start(bf16[512,512]{1,0:T(8,128)(2,1)} %collective-permute-done.23), channel_id=1, source_target_pairs={{0,16},{1,17},{2,18},{3,19},{4,20},{5,21},{6,22},{7,23},{8,24},{9,... | collective-permute-start | bytes 1572872 | tf_op jit(solution)/shard_map/ppermute | solution.py:374
  115.0 13.6 %collective-permute-start.15 = (bf16[256,1024]{1,0:T(8,128)(2,1)S(1)}, bf16[256,1024]{1,0:T(8,128)(2,1)S(1)}, u32[]{:S(2)}, u32[]{:S(2)}) collective-permute-start(bf16[256,1024]{1,0:T(8,128)(2,1)S(1)} %add_convert_fusion.6), channel_id=1, source_target_pairs={{0,1},{1,0},{2,3},{3,2},{4,5},{5,4},{6,7},{7,6},{8,9},{9,8},{10,11... | collective-permute-start | bytes 1572872 | tf_op jit(solution)/shard_map/ppermute | solution.py:374
  130.3 12.7 %collective-permute-start.26 = (bf16[256,1024]{1,0:T(8,128)(2,1)S(1)}, bf16[256,1024]{1,0:T(8,128)(2,1)S(1)}, u32[]{:S(2)}, u32[]{:S(2)}) collective-permute-start(bf16[256,1024]{1,0:T(8,128)(2,1)S(1)} %fusion.41), channel_id=1, source_target_pairs={{0,1},{1,0},{2,3},{3,2},{4,5},{5,4},{6,7},{7,6},{8,9},{9,8},{10,11... | collective-permute-start | bytes 1572872 | tf_op jit(solution)/shard_map/ppermute | solution.py:374
  143.0 3.2 collective-permute-start.27
  145.4 9.3 %collective-permute-start.16 = (bf16[256,1024]{1,0:T(8,128)(2,1)S(1)}, bf16[256,1024]{1,0:T(8,128)(2,1)S(1)}, u32[]{:S(2)}, u32[]{:S(2)}) collective-permute-start(bf16[256,1024]{1,0:T(8,128)(2,1)S(1)} %fusion.41), channel_id=1, source_target_pairs={{0,8},{1,9},{2,10},{3,11},{4,12},{5,13},{6,14},{7,15},{8,0},{9,1},... | collective-permute-start | bytes 1572872 | tf_op jit(solution)/shard_map/ppermute | solution.py:374
  154.3 9.8 %collective-permute-start.28 = (bf16[256,1024]{1,0:T(8,128)(2,1)S(1)}, bf16[256,1024]{1,0:T(8,128)(2,1)S(1)}, u32[]{:S(2)}, u32[]{:S(2)}) collective-permute-start(bf16[256,1024]{1,0:T(8,128)(2,1)S(1)} %get-tuple-element.66), channel_id=1, source_target_pairs={{0,8},{1,9},{2,10},{3,11},{4,12},{5,13},{6,14},{7,15},{8,0},{9,1},... | collective-permute-start | bytes 1572872 | tf_op jit(solution)/shard_map/ppermute | solution.py:374
  164.0 24.4 %collective-permute-start.25 = (bf16[256,1024]{1,0:T(8,128)(2,1)}, bf16[256,1024]{1,0:T(8,128)(2,1)}, u32[]{:S(2)}, u32[]{:S(2)}) collective-permute-start(bf16[256,1024]{1,0:T(8,128)(2,1)} %get-tuple-element.64), channel_id=1, source_target_pairs={{0,8},{1,9},{2,10},{3,11},{4,12},{5,13},{6,14},{7,15},{8,0},{9,1},... | collective-permute-start | bytes 1572872 | tf_op jit(solution)/shard_map/ppermute | solution.py:374
  165.4 23.0 %collective-permute-start.29 = (bf16[256,1024]{1,0:T(8,128)(2,1)}, bf16[256,1024]{1,0:T(8,128)(2,1)}, u32[]{:S(2)}, u32[]{:S(2)}) collective-permute-start(bf16[256,1024]{1,0:T(8,128)(2,1)} %add_convert_fusion.5), channel_id=1, source_target_pairs={{0,1},{1,0},{2,3},{3,2},{4,5},{5,4},{6,7},{7,6},{8,9},{9,8},{10,11... | collective-permute-start | bytes 1572872 | tf_op jit(solution)/shard_map/ppermute | solution.py:374
  173.4 17.6 %collective-permute-start.32 = (bf16[128,1024]{1,0:T(8,128)(2,1)S(1)}, bf16[128,1024]{1,0:T(8,128)(2,1)S(1)}, u32[]{:S(2)}, u32[]{:S(2)}) collective-permute-start(bf16[128,1024]{1,0:T(8,128)(2,1)S(1)} %get-tuple-element.212), channel_id=1, source_target_pairs={{0,0},{1,1},{2,2},{3,3},{4,8},{5,9},{6,10},{7,11},{8,4},{9,5},{10,... | collective-permute-start | bytes 786440 | tf_op jit(solution)/shard_map/ppermute | solution.py:374
  177.8 19.7 %collective-permute-start.33 = (bf16[128,1024]{1,0:T(8,128)(2,1)S(1)}, bf16[128,1024]{1,0:T(8,128)(2,1)S(1)}, u32[]{:S(2)}, u32[]{:S(2)}) collective-permute-start(bf16[128,1024]{1,0:T(8,128)(2,1)S(1)} %get-tuple-element.213), channel_id=1, source_target_pairs={{0,2},{1,3},{2,0},{3,1},{4,10},{5,11},{6,8},{7,9},{8,6},{9,7},{10,... | collective-permute-start | bytes 786440 | tf_op jit(solution)/shard_map/ppermute | solution.py:374
  199.4 19.8 %collective-permute-start.34 = (bf16[256,1024]{1,0:T(8,128)(2,1)}, bf16[256,1024]{1,0:T(8,128)(2,1)}, u32[]{:S(2)}, u32[]{:S(2)}) collective-permute-start(bf16[256,1024]{1,0:T(8,128)(2,1)} %convert_element_type.253), channel_id=1, source_target_pairs={{0,8},{1,9},{2,10},{3,11},{4,12},{5,13},{6,14},{7,15},{8,0},{9,1},... | collective-permute-start | bytes 1572872 | tf_op jit(solution)/shard_map/ppermute | solution.py:374
  200.3 10.6 %collective-permute-start.30 = (bf16[128,1024]{1,0:T(8,128)(2,1)}, bf16[128,1024]{1,0:T(8,128)(2,1)}, u32[]{:S(2)}, u32[]{:S(2)}) collective-permute-start(bf16[128,1024]{1,0:T(8,128)(2,1)} %get-tuple-element.214), channel_id=1, source_target_pairs={{0,0},{1,1},{2,2},{3,3},{4,8},{5,9},{6,10},{7,11},{8,4},{9,5},{10,... | collective-permute-start | bytes 786440 | tf_op jit(solution)/shard_map/ppermute | solution.py:374
  203.1 14.1 %collective-permute-start.31 = (bf16[128,1024]{1,0:T(8,128)(2,1)}, bf16[128,1024]{1,0:T(8,128)(2,1)}, u32[]{:S(2)}, u32[]{:S(2)}) collective-permute-start(bf16[128,1024]{1,0:T(8,128)(2,1)} %get-tuple-element.215), channel_id=1, source_target_pairs={{0,2},{1,3},{2,0},{3,1},{4,10},{5,11},{6,8},{7,9},{8,6},{9,7},{10,... | collective-permute-start | bytes 786440 | tf_op jit(solution)/shard_map/ppermute | solution.py:374
  209.1 21.6 %collective-permute-start.36 = (bf16[256,1024]{1,0:T(8,128)(2,1)}, bf16[256,1024]{1,0:T(8,128)(2,1)S(1)}, u32[]{:S(2)}, u32[]{:S(2)}) collective-permute-start(bf16[256,1024]{1,0:T(8,128)(2,1)} %convert_element_type.253), channel_id=1, source_target_pairs={{0,1},{1,0},{2,3},{3,2},{4,5},{5,4},{6,7},{7,6},{8,9},{9,8},{10,11... | collective-permute-start | bytes 1572872 | tf_op jit(solution)/shard_map/ppermute | solution.py:374
  230.7 25.9 %collective-permute-start.35 = (bf16[256,1024]{1,0:T(8,128)(2,1)}, bf16[256,1024]{1,0:T(8,128)(2,1)}, u32[]{:S(2)}, u32[]{:S(2)}) collective-permute-start(bf16[256,1024]{1,0:T(8,128)(2,1)} %get-tuple-element.70), channel_id=1, source_target_pairs={{0,8},{1,9},{2,10},{3,11},{4,12},{5,13},{6,14},{7,15},{8,0},{9,1},... | collective-permute-start | bytes 1572872 | tf_op jit(solution)/shard_map/ppermute | solution.py:374
  230.7 4.5 collective-permute-start.37
  241.9 5.8 %collective-permute-start.38 = (bf16[256,1024]{1,0:T(8,128)(2,1)S(1)}, bf16[256,1024]{1,0:T(8,128)(2,1)S(1)}, u32[]{:S(2)}, u32[]{:S(2)}) collective-permute-start(bf16[256,1024]{1,0:T(8,128)(2,1)S(1)} %get-tuple-element.73), channel_id=1, source_target_pairs={{0,8},{1,9},{2,10},{3,11},{4,12},{5,13},{6,14},{7,15},{8,0},{9,1},... | collective-permute-start | bytes 1572872 | tf_op jit(solution)/shard_map/ppermute | solution.py:374
  248.8 13.4 %collective-permute-start.39 = (bf16[256,1024]{1,0:T(8,128)(2,1)}, bf16[256,1024]{1,0:T(8,128)(2,1)}, u32[]{:S(2)}, u32[]{:S(2)}) collective-permute-start(bf16[256,1024]{1,0:T(8,128)(2,1)} %add_convert_fusion.3), channel_id=1, source_target_pairs={{0,1},{1,0},{2,3},{3,2},{4,5},{5,4},{6,7},{7,6},{8,9},{9,8},{10,11... | collective-permute-start | bytes 1572872 | tf_op jit(solution)/shard_map/ppermute | solution.py:374
  251.0 27.0 %collective-permute-start.57 = (bf16[512,512]{1,0:T(8,128)(2,1)}, bf16[512,512]{1,0:T(8,128)(2,1)}, u32[]{:S(2)}, u32[]{:S(2)}) collective-permute-start(bf16[512,512]{1,0:T(8,128)(2,1)} %fusion.27), channel_id=1, source_target_pairs={{0,16},{1,17},{2,18},{3,19},{4,20},{5,21},{6,22},{7,23},{8,24},{9,... | collective-permute-start | bytes 1572872 | tf_op jit(solution)/shard_map/ppermute | solution.py:374
  252.1 23.2 %collective-permute-start.56 = (bf16[512,512]{1,0:T(8,128)(2,1)}, bf16[512,512]{1,0:T(8,128)(2,1)}, u32[]{:S(2)}, u32[]{:S(2)}) collective-permute-start(bf16[512,512]{1,0:T(8,128)(2,1)} %fusion.31), channel_id=1, source_target_pairs={{0,16},{1,17},{2,18},{3,19},{4,20},{5,21},{6,22},{7,23},{8,24},{9,... | collective-permute-start | bytes 1572872 | tf_op jit(solution)/shard_map/ppermute | solution.py:374
  254.2 44.2 %collective-permute-start.59 = (bf16[512,512]{1,0:T(8,128)(2,1)}, bf16[512,512]{1,0:T(8,128)(2,1)}, u32[]{:S(2)}, u32[]{:S(2)}) collective-permute-start(bf16[512,512]{1,0:T(8,128)(2,1)} %fusion.23), channel_id=1, source_target_pairs={{0,16},{1,17},{2,18},{3,19},{4,20},{5,21},{6,22},{7,23},{8,24},{9,... | collective-permute-start | bytes 1572872 | tf_op jit(solution)/shard_map/ppermute | solution.py:374
  256.6 46.1 %collective-permute-start.61 = (bf16[512,512]{1,0:T(8,128)(2,1)}, bf16[512,512]{1,0:T(8,128)(2,1)}, u32[]{:S(2)}, u32[]{:S(2)}) collective-permute-start(bf16[512,512]{1,0:T(8,128)(2,1)} %fusion.19), channel_id=1, source_target_pairs={{0,16},{1,17},{2,18},{3,19},{4,20},{5,21},{6,22},{7,23},{8,24},{9,... | collective-permute-start | bytes 1572872 | tf_op jit(solution)/shard_map/ppermute | solution.py:374
  267.7 9.9 %collective-permute-start.65 = (f32[6,1024]{1,0:T(8,128)S(1)}, f32[6,1024]{1,0:T(8,128)S(1)}, u32[]{:S(2)}, u32[]{:S(2)}) collective-permute-start(f32[6,1024]{1,0:T(8,128)S(1)} %add.524), channel_id=1, source_target_pairs={{0,1},{1,0},{2,3},{3,2},{4,5},{5,4},{6,7},{7,6},{8,9},{9,8},{10,11... | collective-permute-start | bytes 73736 | tf_op jit(solution)/shard_map/ppermute | solution.py:374
  277.6 20.8 %collective-permute-start.66 = (f32[6,1024]{1,0:T(8,128)S(1)}, f32[6,1024]{1,0:T(8,128)S(1)}, u32[]{:S(2)}, u32[]{:S(2)}) collective-permute-start(f32[6,1024]{1,0:T(8,128)S(1)} %add.525), channel_id=1, source_target_pairs={{0,16},{1,17},{2,18},{3,19},{4,20},{5,21},{6,22},{7,23},{8,24},{9,... | collective-permute-start | bytes 73736 | tf_op jit(solution)/shard_map/ppermute | solution.py:374
  301.3 5.7 %collective-permute-start.68 = (f32[6,1024]{1,0:T(8,128)S(1)}, f32[6,1024]{1,0:T(8,128)S(1)}, u32[]{:S(2)}, u32[]{:S(2)}) collective-permute-start(f32[6,1024]{1,0:T(8,128)S(1)} %add.527), channel_id=1, source_target_pairs={{0,4},{1,5},{2,6},{3,7},{4,0},{5,1},{6,2},{7,3},{8,12},{9,13},{10,... | collective-permute-start | bytes 73736 | tf_op jit(solution)/shard_map/ppermute | solution.py:374
  304.8 11.8 %collective-permute-start.41 = (bf16[256,1024]{1,0:T(8,128)(2,1)S(1)}, bf16[256,1024]{1,0:T(8,128)(2,1)S(1)}, u32[]{:S(2)}, u32[]{:S(2)}) collective-permute-start(bf16[256,1024]{1,0:T(8,128)(2,1)S(1)} %convert_element_type.258), channel_id=1, source_target_pairs={{0,1},{1,0},{2,3},{3,2},{4,5},{5,4},{6,7},{7,6},{8,9},{9,8},{10,11... | collective-permute-start | bytes 1572872 | tf_op jit(solution)/shard_map/ppermute | solution.py:374
  305.1 15.9 %collective-permute-start.40 = (bf16[256,1024]{1,0:T(8,128)(2,1)S(1)}, bf16[256,1024]{1,0:T(8,128)(2,1)S(1)}, u32[]{:S(2)}, u32[]{:S(2)}) collective-permute-start(bf16[256,1024]{1,0:T(8,128)(2,1)S(1)} %convert_element_type.258), channel_id=1, source_target_pairs={{0,8},{1,9},{2,10},{3,11},{4,12},{5,13},{6,14},{7,15},{8,0},{9,1},... | collective-permute-start | bytes 1572872 | tf_op jit(solution)/shard_map/ppermute | solution.py:374
  316.6 4.8 %collective-permute-start.42 = (bf16[256,1024]{1,0:T(8,128)(2,1)S(1)}, bf16[256,1024]{1,0:T(8,128)(2,1)S(1)}, u32[]{:S(2)}, u32[]{:S(2)}) collective-permute-start(bf16[256,1024]{1,0:T(8,128)(2,1)S(1)} %collective-permute-done.41), channel_id=1, source_target_pairs={{0,8},{1,9},{2,10},{3,11},{4,12},{5,13},{6,14},{7,15},{8,0},{9,1},... | collective-permute-start | bytes 1572872 | tf_op jit(solution)/shard_map/ppermute | solution.py:374
  342.7 31.4 %collective-permute-start.58 = (bf16[512,512]{1,0:T(8,128)(2,1)}, bf16[512,512]{1,0:T(8,128)(2,1)}, u32[]{:S(2)}, u32[]{:S(2)}) collective-permute-start(bf16[512,512]{1,0:T(8,128)(2,1)} %fusion.29), channel_id=1, source_target_pairs={{0,2},{1,3},{2,4},{3,5},{4,6},{5,7},{6,0},{7,1},{8,10},{9,11},{10,... | collective-permute-start | bytes 1572872 | tf_op jit(solution)/shard_map/ppermute | solution.py:374
  343.3 51.4 %collective-permute-start.60 = (bf16[512,512]{1,0:T(8,128)(2,1)}, bf16[512,512]{1,0:T(8,128)(2,1)}, u32[]{:S(2)}, u32[]{:S(2)}) collective-permute-start(bf16[512,512]{1,0:T(8,128)(2,1)} %fusion.25), channel_id=1, source_target_pairs={{0,4},{1,5},{2,6},{3,7},{4,0},{5,1},{6,2},{7,3},{8,12},{9,13},{10,... | collective-permute-start | bytes 1572872 | tf_op jit(solution)/shard_map/ppermute | solution.py:374
  345.5 52.2 %collective-permute-start.62 = (bf16[512,512]{1,0:T(8,128)(2,1)}, bf16[512,512]{1,0:T(8,128)(2,1)}, u32[]{:S(2)}, u32[]{:S(2)}) collective-permute-start(bf16[512,512]{1,0:T(8,128)(2,1)} %fusion.21), channel_id=1, source_target_pairs={{0,6},{1,7},{2,0},{3,1},{4,2},{5,3},{6,4},{7,5},{8,14},{9,15},{10,... | collective-permute-start | bytes 1572872 | tf_op jit(solution)/shard_map/ppermute | solution.py:374
  351.9 7.8 %collective-permute-start.49 = (bf16[272,512]{1,0:T(8,128)(2,1)S(1)}, bf16[272,512]{1,0:T(8,128)(2,1)S(1)}, u32[]{:S(2)}, u32[]{:S(2)}) collective-permute-start(bf16[272,512]{1,0:T(8,128)(2,1)S(1)} %dynamic-slice_convert_fusion.2), channel_id=1, source_target_pairs={{0,16},{1,17},{2,18},{3,19},{4,20},{5,21},{6,22},{7,23},{8,24},{9,... | collective-permute-start | bytes 835592 | tf_op jit(solution)/shard_map/ppermute | solution.py:374
  352.4 13.3 %collective-permute-start.51 = (bf16[272,512]{1,0:T(8,128)(2,1)S(1)}, bf16[272,512]{1,0:T(8,128)(2,1)S(1)}, u32[]{:S(2)}, u32[]{:S(2)}) collective-permute-start(bf16[272,512]{1,0:T(8,128)(2,1)S(1)} %dynamic-slice_convert_fusion.1), channel_id=1, source_target_pairs={{0,16},{1,17},{2,18},{3,19},{4,20},{5,21},{6,22},{7,23},{8,24},{9,... | collective-permute-start | bytes 835592 | tf_op jit(solution)/shard_map/ppermute | solution.py:374
  359.7 11.8 %collective-permute-start.53 = (bf16[272,512]{1,0:T(8,128)(2,1)S(1)}, bf16[272,512]{1,0:T(8,128)(2,1)S(1)}, u32[]{:S(2)}, u32[]{:S(2)}) collective-permute-start(bf16[272,512]{1,0:T(8,128)(2,1)S(1)} %dynamic-slice_convert_fusion), channel_id=1, source_target_pairs={{0,16},{1,17},{2,18},{3,19},{4,20},{5,21},{6,22},{7,23},{8,24},{9,... | collective-permute-start | bytes 835592 | tf_op jit(solution)/shard_map/ppermute | solution.py:374
  365.7 35.6 %collective-permute-start.48 = (bf16[272,512]{1,0:T(8,128)(2,1)S(1)}, bf16[272,512]{1,0:T(8,128)(2,1)S(1)}, u32[]{:S(2)}, u32[]{:S(2)}) collective-permute-start(bf16[272,512]{1,0:T(8,128)(2,1)S(1)} %dynamic-slice_convert_fusion.3), channel_id=1, source_target_pairs={{0,16},{1,17},{2,18},{3,19},{4,20},{5,21},{6,22},{7,23},{8,24},{9,... | collective-permute-start | bytes 835592 | tf_op jit(solution)/shard_map/ppermute | solution.py:374
  371.5 44.8 %collective-permute-start.44 = (bf16[256,1024]{1,0:T(8,128)(2,1)S(1)}, bf16[256,1024]{1,0:T(8,128)(2,1)S(1)}, u32[]{:S(2)}, u32[]{:S(2)}) collective-permute-start(bf16[256,1024]{1,0:T(8,128)(2,1)S(1)} %copy-done.96), channel_id=1, source_target_pairs={{0,8},{1,9},{2,10},{3,11},{4,12},{5,13},{6,14},{7,15},{8,0},{9,1},... | collective-permute-start | bytes 1572872 | tf_op jit(solution)/shard_map/ppermute | solution.py:374
  374.1 32.4 %collective-permute-start.50 = (bf16[272,512]{1,0:T(8,128)(2,1)S(1)}, bf16[272,512]{1,0:T(8,128)(2,1)S(1)}, u32[]{:S(2)}, u32[]{:S(2)}) collective-permute-start(bf16[272,512]{1,0:T(8,128)(2,1)S(1)} %add_convert_fusion.9), channel_id=1, source_target_pairs={{0,2},{1,3},{2,4},{3,5},{4,6},{5,7},{6,0},{7,1},{8,10},{9,11},{10,... | collective-permute-start | bytes 835592 | tf_op jit(solution)/shard_map/ppermute | solution.py:374
  394.7 17.8 %collective-permute-start.52 = (bf16[272,512]{1,0:T(8,128)(2,1)S(1)}, bf16[272,512]{1,0:T(8,128)(2,1)S(1)}, u32[]{:S(2)}, u32[]{:S(2)}) collective-permute-start(bf16[272,512]{1,0:T(8,128)(2,1)S(1)} %add_convert_fusion.8), channel_id=1, source_target_pairs={{0,4},{1,5},{2,6},{3,7},{4,0},{5,1},{6,2},{7,3},{8,12},{9,13},{10,... | collective-permute-start | bytes 835592 | tf_op jit(solution)/shard_map/ppermute | solution.py:374
  397.8 17.7 %collective-permute-start.54 = (bf16[272,512]{1,0:T(8,128)(2,1)S(1)}, bf16[272,512]{1,0:T(8,128)(2,1)S(1)}, u32[]{:S(2)}, u32[]{:S(2)}) collective-permute-start(bf16[272,512]{1,0:T(8,128)(2,1)S(1)} %add_convert_fusion.7), channel_id=1, source_target_pairs={{0,6},{1,7},{2,0},{3,1},{4,2},{5,3},{6,4},{7,5},{8,14},{9,15},{10,... | collective-permute-start | bytes 835592 | tf_op jit(solution)/shard_map/ppermute | solution.py:374
  401.3 47.3 %collective-permute-start.43 = (bf16[256,1024]{1,0:T(8,128)(2,1)}, bf16[256,1024]{1,0:T(8,128)(2,1)}, u32[]{:S(2)}, u32[]{:S(2)}) collective-permute-start(bf16[256,1024]{1,0:T(8,128)(2,1)} %convolution_convert_fusion.1), channel_id=1, source_target_pairs={{0,8},{1,9},{2,10},{3,11},{4,12},{5,13},{6,14},{7,15},{8,0},{9,1},... | collective-permute-start | bytes 1572872 | tf_op jit(solution)/shard_map/ppermute | solution.py:374
  406.5 29.5 %collective-permute-start.63 = (f32[512,256]{1,0:T(8,128)}, f32[512,256]{1,0:T(8,128)}, u32[]{:S(2)}, u32[]{:S(2)}) collective-permute-start(f32[512,256]{1,0:T(8,128)} %constant_dynamic-slice_fusion.1), channel_id=1, source_target_pairs={{0,8},{1,9},{2,10},{3,11},{4,12},{5,13},{6,14},{7,15},{8,0},{9,1},... | collective-permute-start | bytes 1572872 | tf_op jit(solution)/shard_map/ppermute | solution.py:374
  417.8 30.8 %collective-permute-start.45 = (bf16[256,1024]{1,0:T(8,128)(2,1)}, bf16[256,1024]{1,0:T(8,128)(2,1)}, u32[]{:S(2)}, u32[]{:S(2)}) collective-permute-start(bf16[256,1024]{1,0:T(8,128)(2,1)} %add_convert_fusion.2), channel_id=1, source_target_pairs={{0,1},{1,0},{2,3},{3,2},{4,5},{5,4},{6,7},{7,6},{8,9},{9,8},{10,11... | collective-permute-start | bytes 1572872 | tf_op jit(solution)/shard_map/ppermute | solution.py:374
  451.1 8.7 %collective-permute-start.46 = (bf16[128,1024]{1,0:T(8,128)(2,1)S(1)}, bf16[128,1024]{1,0:T(8,128)(2,1)S(1)}, u32[]{:S(2)}, u32[]{:S(2)}) collective-permute-start(bf16[128,1024]{1,0:T(8,128)(2,1)S(1)} %get-tuple-element.210), channel_id=1, source_target_pairs={{0,0},{1,1},{2,2},{3,3},{4,8},{5,9},{6,10},{7,11},{8,4},{9,5},{10,... | collective-permute-start | bytes 786440 | tf_op jit(solution)/shard_map/ppermute | solution.py:374
  453.5 11.6 %collective-permute-start.47 = (bf16[128,1024]{1,0:T(8,128)(2,1)S(1)}, bf16[128,1024]{1,0:T(8,128)(2,1)S(1)}, u32[]{:S(2)}, u32[]{:S(2)}) collective-permute-start(bf16[128,1024]{1,0:T(8,128)(2,1)S(1)} %get-tuple-element.211), channel_id=1, source_target_pairs={{0,2},{1,3},{2,0},{3,1},{4,10},{5,11},{6,8},{7,9},{8,6},{9,7},{10,... | collective-permute-start | bytes 786440 | tf_op jit(solution)/shard_map/ppermute | solution.py:374
  (102 other events, 907.8 us)
